TPU v7x, 256 devices: a whole 4x4x8 slice. The times are simulated.
256 devices in a mesh: blk: 32 (over z, y_hi, core), rep: 8 (over x, y_lo).
Axes of the slice: x: 4, y: 4 (y_hi: 2, y_lo: 2; y = y_hi * 2 + y_lo), z: 8, core: 2. Of those that a mesh axis runs over, the one named last changes fastest.
Arguments:
- features: bfloat16 [65536, 256], P(('blk', 'rep')), may hold values from -6 to 6
- aggregated: bfloat16 [65536, 256], P(('blk', 'rep')), may hold values from -6 to 6
- out_grad: bfloat16 [65536, 256], P(('blk', 'rep')), may hold values from -6 to 6
- w_self: bfloat16 [256, 256], replicated, may hold values from -0.375 to 0.375
- w_neigh: bfloat16 [256, 256], replicated, may hold values from -0.375 to 0.375
- tiles: bfloat16 [32, 32, 8, 128, 128], P('blk'), may hold values from -0.046875 to 0.046875
- tile_rows: int32 [32, 32, 8], P('blk'), may hold values from 0 to 15
- tile_cols: int32 [32, 32, 8], P('blk'), may hold values from 0 to 15
- tile_counts: int32 [32, 32], P('blk'), may hold values from 0 to 8, as said below
Outputs:
- feature_grad: float32 [65536, 256], P(('blk', 'rep'))
- self_grad: float32 [256, 256], replicated
- neigh_grad: float32 [256, 256], replicated
Inputs may be any that keep to these rules, and one draw needn't show every extreme that they name: `tile_counts`: at most 8; some pair of blocks uses all 8 slots; tiles, rows and columns of slots beyond the count carry no meaning.
All inputs are finite; a program needn't handle non-finite values.
Results may differ from a plain program's by a relative error of at most 0.00082.
Values may be sent and summed in bfloat16 or wider, within the bound.
No kernel may reach another device: no remote copies, remote signals or barrier semaphores. Data moves between devices by JAX's collectives and lax.ppermute only.
A program may use at most 64 MiB of HBM per device.

v0:
```python
import jax
import jax.numpy as jnp
from jax import lax
from jax.sharding import PartitionSpec as P


def from_everyone(x, axis):
    copies = jnp.broadcast_to(x, (lax.axis_size(axis), *x.shape))
    return lax.all_to_all(copies, axis, split_axis=0, concat_axis=0, tiled=True)


def in_order(parts, dim):
    dims = list(parts.shape[1:])
    dims[dim] *= parts.shape[0]
    return jnp.moveaxis(parts, 0, dim).reshape(dims)


def gather_directly(x, axis, dim):
    parts = from_everyone(x, axis)
    return in_order(parts, dim)


def split_up(x, dim, length):
    dims = x.shape
    parts = x.reshape(*dims[:dim], length, dims[dim] // length, *dims[dim + 1 :])
    return jnp.moveaxis(parts, dim, 0)


def sent_and_summed(x, axis, dim):
    parts = split_up(x, dim, lax.axis_size(axis))
    arrived = lax.all_to_all(parts, axis, split_axis=0, concat_axis=0, tiled=True)
    return arrived.sum(axis=0)


def over_copies(x, axis):
    return from_everyone(x, axis).sum(axis=0)


def on_device(
    features, aggregated, out_grad, w_self, w_neigh, tiles, tile_rows, tile_cols, tile_counts
):
    block_total = lax.axis_size("blk")
    copies = lax.axis_size("rep")
    replica = lax.axis_index("rep")
    width = out_grad.shape[1]
    side = tiles.shape[-1]
    slots_total = tiles.shape[2]
    share = jnp.dot(out_grad, w_neigh.T, preferred_element_type=jnp.float32).astype(jnp.bfloat16)
    whole = gather_directly(share, "rep", 0)
    block_rows = whole.shape[0]
    tiles_side = block_rows // side
    pieces_whole = whole.reshape(tiles_side, side, width)
    per_copy = (slots_total + copies - 1) // copies
    slot_ids = replica + copies * jnp.arange(per_copy, dtype=jnp.int32)
    valid = slot_ids < slots_total
    safe = jnp.minimum(slot_ids, slots_total - 1)
    wanted = jnp.take(tile_cols[0], safe, axis=1)
    found = pieces_whole[lax.all_to_all(wanted, "blk", split_axis=0, concat_axis=0, tiled=True)]
    fetched = lax.all_to_all(found, "blk", split_axis=0, concat_axis=0, tiled=True)
    chosen_tiles = jnp.take(tiles[0], safe, axis=1)
    products = jnp.einsum(
        "ikpq,ikqf->ikpf", chosen_tiles, fetched, preferred_element_type=jnp.float32
    )
    live = valid[None, :] & (slot_ids[None, :] < tile_counts[0][:, None])
    products = jnp.where(live[:, :, None, None], products, jnp.zeros_like(products))
    target_rows = jnp.take(tile_rows[0], safe, axis=1).reshape(-1)
    accumulated = jnp.zeros((tiles_side, side, width), jnp.float32)
    accumulated = accumulated.at[target_rows].add(products.reshape(-1, side, width))
    flat = accumulated.reshape(block_rows, width)
    self_part = jnp.dot(out_grad, w_self.T, preferred_element_type=jnp.float32)
    contract = (((0,), (0,)), ((), ()))
    terms_self = lax.dot_general(features, out_grad, contract, preferred_element_type=jnp.float32)
    terms_neigh = lax.dot_general(
        aggregated, out_grad, contract, preferred_element_type=jnp.float32
    )
    scale = (out_grad.shape[0] * block_total * copies) ** (-0.5)
    stacked = jnp.concatenate([terms_self, terms_neigh], axis=0)
    spread_share, stacked_share = (
        sent_and_summed(flat, "rep", 0),
        sent_and_summed(stacked, "rep", 0),
    )
    summed = over_copies(stacked_share, "blk")
    complete = gather_directly(summed, "rep", 0)
    self_sum = complete[:width]
    neigh_sum = complete[width:]
    return (spread_share + self_part, self_sum * scale, neigh_sum * scale)


def solution(mesh):
    placed = (
        P(("blk", "rep"), None),
        P(("blk", "rep"), None),
        P(("blk", "rep"), None),
        P(),
        P(),
        P("blk", None, None, None, None),
        P("blk", None, None),
        P("blk", None, None),
        P("blk", None),
    )
    return jax.shard_map(
        on_device,
        mesh=mesh,
        in_specs=placed,
        out_specs=(P(("blk", "rep"), None), P(), P()),
        check_vma=False,
    )
```

profile of v0, /device:TPU:8, one launch (start us, length us, event | category | flops | bytes accessed | tf_op | source)
XLA Modules:
  0.0 226.6 jit_solution(15578091327331218589)
XLA Ops:
  0.6 0.0 copy-start
  0.6 0.0 copy-start.1
  0.7 0.7 fusion.8
  1.4 0.7 copy.18
  2.1 10.6 %all-to-all-start.1 = ((s32[32,1,1]{2,1,0:T(1,128)}), s32[32,1,1]{2,1,0:T(1,128)S(1)}, u32[]{:S(2)}, u32[]{:S(2)}) async-start(s32[32,1,1]{2,1,0:T(1,128)} %copy.18), calls=%async_computation.1 | async-start | bytes 32768 | tf_op jit(solution)/shard_map/all_to_all | solution.py:58
  12.7 0.0 copy-done
  12.7 1.1 fusion.11
  13.8 1.1 fusion.12
  15.0 0.8 pad_maximum_fusion
  15.8 6.6 %all-to-all-done.1 = s32[32,1,1]{2,1,0:T(1,128)S(1)} async-done(((s32[32,1,1]{2,1,0:T(1,128)}), s32[32,1,1]{2,1,0:T(1,128)S(1)}, u32[]{:S(2)}, u32[]{:S(2)}) %all-to-all-start.1) | async-done | bytes 160 | tf_op jit(solution)/shard_map/all_to_all | solution.py:58
  22.3 5.8 %all-to-all-start.4 = ((f32[8,64,256]{2,1,0:T(8,128)}), f32[8,64,256]{2,1,0:T(8,128)S(1)}, u32[]{:S(2)}, u32[]{:S(2)}) async-start(f32[8,64,256]{2,1,0:T(8,128)} %bitcast.17), calls=%async_computation.4 | async-start | bytes 1048576 | tf_op jit(solution)/shard_map/all_to_all | solution.py:31
  28.1 0.0 copy-done.1
  28.1 0.2 convolution_convert_fusion
  28.3 8.8 %all-to-all-done.4 = f32[8,64,256]{2,1,0:T(8,128)S(1)} async-done(((f32[8,64,256]{2,1,0:T(8,128)}), f32[8,64,256]{2,1,0:T(8,128)S(1)}, u32[]{:S(2)}, u32[]{:S(2)}) %all-to-all-start.4) | async-done | bytes 524320 | tf_op jit(solution)/shard_map/all_to_all | solution.py:31
  37.1 1.0 broadcast_in_dim.53
  38.1 4.0 %all-to-all-start = ((bf16[8,256,256]{2,1,0:T(8,128)(2,1)}), bf16[8,256,256]{2,1,0:T(8,128)(2,1)S(1)}, u32[]{:S(2)}, u32[]{:S(2)}) async-start(bf16[8,256,256]{2,1,0:T(8,128)(2,1)} %broadcast_in_dim.53), calls=%async_computation | async-start | bytes 2097152 | tf_op jit(solution)/shard_map/all_to_all | solution.py:9
  42.2 14.0 %all-to-all-done = bf16[8,256,256]{2,1,0:T(8,128)(2,1)S(1)} async-done(((bf16[8,256,256]{2,1,0:T(8,128)(2,1)}), bf16[8,256,256]{2,1,0:T(8,128)(2,1)S(1)}, u32[]{:S(2)}, u32[]{:S(2)}) %all-to-all-start) | async-done | bytes 1048608 | tf_op jit(solution)/shard_map/all_to_all | solution.py:9
  56.2 1.5 broadcast_in_dim.55
  57.7 4.0 %all-to-all-start.5 = ((f32[32,64,256]{2,1,0:T(8,128)}), f32[32,64,256]{2,1,0:T(8,128)S(1)}, u32[]{:S(2)}, u32[]{:S(2)}) async-start(f32[32,64,256]{2,1,0:T(8,128)} %broadcast_in_dim.55), calls=%async_computation.5 | async-start | bytes 4194304 | tf_op jit(solution)/shard_map/all_to_all | solution.py:9
  61.7 0.7 fusion.6
  62.4 2.0 gather_fusion
  64.4 49.0 %all-to-all-done.5 = f32[32,64,256]{2,1,0:T(8,128)S(1)} async-done(((f32[32,64,256]{2,1,0:T(8,128)}), f32[32,64,256]{2,1,0:T(8,128)S(1)}, u32[]{:S(2)}, u32[]{:S(2)}) %all-to-all-start.5) | async-done | bytes 2097184 | tf_op jit(solution)/shard_map/all_to_all | solution.py:9
  113.4 0.0 copy-start.3
  113.4 5.0 %all-to-all-start.2 = ((bf16[32,1,128,256]{3,2,1,0:T(8,128)(2,1)}), bf16[32,1,128,256]{3,2,1,0:T(8,128)(2,1)}, u32[]{:S(2)}, u32[]{:S(2)}) async-start(bf16[32,1,128,256]{3,2,1,0:T(8,128)(2,1)} %bitcast.41), calls=%async_computation.2 | async-start | bytes 4194304 | tf_op jit(solution)/shard_map/all_to_all | solution.py:59
  118.4 0.0 copy-done.3
  118.4 0.1 reduce_sum.29
  118.6 50.2 %all-to-all-done.2 = bf16[32,1,128,256]{3,2,1,0:T(8,128)(2,1)} async-done(((bf16[32,1,128,256]{3,2,1,0:T(8,128)(2,1)}), bf16[32,1,128,256]{3,2,1,0:T(8,128)(2,1)}, u32[]{:S(2)}, u32[]{:S(2)}) %all-to-all-start.2) | async-done | bytes 2097184 | tf_op jit(solution)/shard_map/all_to_all | solution.py:59
  168.7 0.9 broadcast_in_dim.56
  169.6 4.9 %all-to-all-start.6 = ((f32[8,64,256]{2,1,0:T(8,128)}), f32[8,64,256]{2,1,0:T(8,128)S(1)}, u32[]{:S(2)}, u32[]{:S(2)}) async-start(f32[8,64,256]{2,1,0:T(8,128)} %broadcast_in_dim.56), calls=%async_computation.6 | async-start | bytes 1048576 | tf_op jit(solution)/shard_map/all_to_all | solution.py:9
  174.4 0.7 fusion.9
  175.1 4.6 %convolution_select_fusion = f32[32,128,256]{2,1,0:T(8,128)} fusion(bf16[32,1,128,256]{3,2,1,0:T(8,128)(2,1)} %all-to-all-done.2, pred[32]{0:T(512)(128)(4,1)S(1)} %and_bitcast_fusion, bf16[1,32,8,128,128]{4,3,2,1,0:T(8,128)(2,1)} %param.16, s32[]{:T(128)} %bitcast.3, pred[]{:T(512)} %bitcast.1), kind=kOutput, calls=%fused_computation.2 | convolution fusion | flops 270008320 | bytes 7341088 | tf_op jit(solution)/shard_map/ikpq,ikqf->ikpf/dot_general | solution.py:61
  179.7 1.5 broadcast_in_dim.48
  181.2 9.7 %scatter_fusion = f32[16,128,256]{2,1,0:T(8,128)} fusion(f32[16,128,256]{2,1,0:T(8,128)} %broadcast_in_dim.48, s32[32]{0:T(128)S(1)} %fusion.9, f32[32,128,256]{2,1,0:T(8,128)} %convolution_select_fusion), kind=kCustom, calls=%fused_computation.1 | custom fusion | flops 1048576 | bytes 12583040 | tf_op jit(solution)/shard_map/scatter-add | solution.py:68
  190.9 0.0 all-to-all-done.6
  190.9 5.9 %all-to-all-start.3 = ((f32[8,256,256]{2,1,0:T(8,128)}), f32[8,256,256]{2,1,0:T(8,128)S(1)}, u32[]{:S(2)}, u32[]{:S(2)}) async-start(f32[8,256,256]{2,1,0:T(8,128)} %bitcast.16), calls=%async_computation.3 | async-start | bytes 4194304 | tf_op jit(solution)/shard_map/all_to_all | solution.py:31
  196.8 0.0 copy-start.2
  196.8 0.8 slice_multiply_fusion
  197.6 27.9 %all-to-all-done.3 = f32[8,256,256]{2,1,0:T(8,128)S(1)} async-done(((f32[8,256,256]{2,1,0:T(8,128)}), f32[8,256,256]{2,1,0:T(8,128)S(1)}, u32[]{:S(2)}, u32[]{:S(2)}) %all-to-all-start.3) | async-done | bytes 2097184 | tf_op jit(solution)/shard_map/all_to_all | solution.py:31
  225.5 0.1 reduce_sum.27
  225.7 0.0 copy-done.2
  225.7 0.9 convolution_add_fusion
  (3 shorter events, 0.1 us)
Async XLA Ops:
  0.6 12.1 %copy-start = (bf16[256,256]{1,0:T(8,128)(2,1)S(1)}, bf16[256,256]{1,0:T(8,128)(2,1)}, u32[]{:S(2)}) copy-start(bf16[256,256]{1,0:T(8,128)(2,1)} %param.13) | copy-start | bytes 393220
  0.6 27.5 %copy-start.1 = (bf16[256,256]{1,0:T(8,128)(2,1)S(1)}, bf16[256,256]{1,0:T(8,128)(2,1)}, u32[]{:S(2)}) copy-start(bf16[256,256]{1,0:T(8,128)(2,1)} %param.15) | copy-start | bytes 393220
  2.1 20.3 %all-to-all-start.1 = ((s32[32,1,1]{2,1,0:T(1,128)}), s32[32,1,1]{2,1,0:T(1,128)S(1)}, u32[]{:S(2)}, u32[]{:S(2)}) async-start(s32[32,1,1]{2,1,0:T(1,128)} %copy.18), calls=%async_computation.1 | async-start | bytes 32768 | tf_op jit(solution)/shard_map/all_to_all | solution.py:58
  22.3 14.7 %all-to-all-start.4 = ((f32[8,64,256]{2,1,0:T(8,128)}), f32[8,64,256]{2,1,0:T(8,128)S(1)}, u32[]{:S(2)}, u32[]{:S(2)}) async-start(f32[8,64,256]{2,1,0:T(8,128)} %bitcast.17), calls=%async_computation.4 | async-start | bytes 1048576 | tf_op jit(solution)/shard_map/all_to_all | solution.py:31
  38.1 18.1 %all-to-all-start = ((bf16[8,256,256]{2,1,0:T(8,128)(2,1)}), bf16[8,256,256]{2,1,0:T(8,128)(2,1)S(1)}, u32[]{:S(2)}, u32[]{:S(2)}) async-start(bf16[8,256,256]{2,1,0:T(8,128)(2,1)} %broadcast_in_dim.53), calls=%async_computation | async-start | bytes 2097152 | tf_op jit(solution)/shard_map/all_to_all | solution.py:9
  57.7 55.7 %all-to-all-start.5 = ((f32[32,64,256]{2,1,0:T(8,128)}), f32[32,64,256]{2,1,0:T(8,128)S(1)}, u32[]{:S(2)}, u32[]{:S(2)}) async-start(f32[32,64,256]{2,1,0:T(8,128)} %broadcast_in_dim.55), calls=%async_computation.5 | async-start | bytes 4194304 | tf_op jit(solution)/shard_map/all_to_all | solution.py:9
  113.4 5.0 %copy-start.3 = (s32[1,32]{1,0:T(1,128)S(1)}, s32[1,32]{1,0:T(1,128)}, u32[]{:S(2)}) copy-start(s32[1,32]{1,0:T(1,128)} %param.19) | copy-start | bytes 388
  113.4 55.3 %all-to-all-start.2 = ((bf16[32,1,128,256]{3,2,1,0:T(8,128)(2,1)}), bf16[32,1,128,256]{3,2,1,0:T(8,128)(2,1)}, u32[]{:S(2)}, u32[]{:S(2)}) async-start(bf16[32,1,128,256]{3,2,1,0:T(8,128)(2,1)} %bitcast.41), calls=%async_computation.2 | async-start | bytes 4194304 | tf_op jit(solution)/shard_map/all_to_all | solution.py:59
  169.6 21.3 %all-to-all-start.6 = ((f32[8,64,256]{2,1,0:T(8,128)}), f32[8,64,256]{2,1,0:T(8,128)S(1)}, u32[]{:S(2)}, u32[]{:S(2)}) async-start(f32[8,64,256]{2,1,0:T(8,128)} %broadcast_in_dim.56), calls=%async_computation.6 | async-start | bytes 1048576 | tf_op jit(solution)/shard_map/all_to_all | solution.py:9
  190.9 34.6 %all-to-all-start.3 = ((f32[8,256,256]{2,1,0:T(8,128)}), f32[8,256,256]{2,1,0:T(8,128)S(1)}, u32[]{:S(2)}, u32[]{:S(2)}) async-start(f32[8,256,256]{2,1,0:T(8,128)} %bitcast.16), calls=%async_computation.3 | async-start | bytes 4194304 | tf_op jit(solution)/shard_map/all_to_all | solution.py:31
  196.8 28.9 %copy-start.2 = (bf16[256,256]{1,0:T(8,128)(2,1)S(1)}, bf16[256,256]{1,0:T(8,128)(2,1)}, u32[]{:S(2)}) copy-start(bf16[256,256]{1,0:T(8,128)(2,1)} %param.14) | copy-start | bytes 393220
where the time goes:
time: 229 us; the launch traced here: 227 us
  waiting for transfers between devices  156 us (68%)
  starting transfers between devices  40.1 us (18%)
  other arithmetic  13.7 us (6%)
  matrix products  7.95 us (3%)
  local copies, waits for them, and re-layouts  7.7 us (3%)
    all_to_all x3, waiting for transfers between devices, from_everyone(): return lax.all_to_all(copies, axis, split_axis=0, concat_axis=0, tiled=True)  63 us
    all_to_all x1, waiting for transfers between devices, on_device(): lax.all_to_all(found, 'blk', split_axis=0, concat_axis=0, tiled=True)  50.2 us
    all_to_all x2, waiting for transfers between devices, sent_and_summed(): lax.all_to_all(parts, axis, split_axis=0, concat_axis=0, tiled=True)  36.7 us
    all_to_all x3, starting transfers between devices, from_everyone(): return lax.all_to_all(copies, axis, split_axis=0, concat_axis=0, tiled=True)  12.9 us
    all_to_all x2, starting transfers between devices, sent_and_summed(): lax.all_to_all(parts, axis, split_axis=0, concat_axis=0, tiled=True)  11.6 us
    all_to_all x1, starting transfers between devices, on_device(): lax.all_to_all(wanted, 'blk', split_axis=0, concat_axis=0, tiled=True)  10.6 us
    scatter-add x1, other arithmetic, on_device(): accumulated.at[target_rows].add(products.reshape(-1, side, width))  9.65 us
    all_to_all x1, waiting for transfers between devices, on_device(): lax.all_to_all(wanted, 'blk', split_axis=0, concat_axis=0, tiled=True)  6.55 us
  transfers between devices with their start and end apart: 7, of which 6 were waited for; matrix products, arithmetic and copies ran while one was open for 10% of the time, Pallas kernels for 0%

commit v1 on v0

v1 whole, which is shorter than its diff:
```python
import functools

import jax
import jax.numpy as jnp
from jax import lax
from jax.experimental import pallas as pl
from jax.experimental.pallas import tpu as pltpu
from jax.sharding import PartitionSpec as P

PLANE = 4
BOTH = ("blk", "rep")


def plane_exchange(x, groups):
    return lax.all_to_all(x, BOTH, 0, 0, axis_index_groups=groups, tiled=True)


def spread_kernel(
    pieces_total, slots, ids, rows, cols, tiles, *rest
):
    pieces = rest[:pieces_total]
    out = rest[pieces_total]
    held, tile_buf, acc, piece_sems, tile_sems = rest[pieces_total + 1 :]
    tiles_side = out.shape[0]
    blocks_total = ids.shape[0]
    begun = []
    at = 0
    for index, piece in enumerate(pieces):
        length = piece.shape[0]
        begun.append(
            pltpu.make_async_copy(piece, held.at[pl.ds(at, length)], piece_sems.at[index])
        )
        at += length

    def tile_copy(n):
        return pltpu.make_async_copy(tiles.at[ids[n]], tile_buf.at[n], tile_sems.at[n])

    for copy in begun:
        copy.start()

    @pl.loop(0, blocks_total)
    def _(n):
        tile_copy(n).start()

    acc[...] = jnp.zeros_like(acc)
    for copy in begun:
        copy.wait()

    @pl.loop(0, blocks_total)
    def _(n):
        tile_copy(n).wait()
        base = ids[n] * slots
        products = [
            lax.dot_general(
                held[n, cols[base + k]],
                tile_buf[n, k],
                (((1,), (1,)), ((), ())),
                preferred_element_type=jnp.float32,
            )
            for k in range(slots)
        ]
        for k in range(slots):
            row = rows[base + k]
            acc[row] = acc[row] + products[k]

    out[...] = acc[:tiles_side]


def spread_over(pieces, ids, rows, cols, tiles, tiles_side):
    blocks_total, slots, side, _ = tiles.shape
    features = pieces[0].shape[-2]
    held = (blocks_total, *pieces[0].shape[1:])
    smem = pl.BlockSpec(memory_space=pltpu.SMEM)
    anywhere = pl.BlockSpec(memory_space=pl.ANY)
    return pl.pallas_call(
        functools.partial(spread_kernel, len(pieces), slots),
        out_shape=jax.ShapeDtypeStruct((tiles_side, features, side), jnp.float32),
        in_specs=[smem, smem, smem, anywhere, *([anywhere] * len(pieces))],
        out_specs=pl.BlockSpec(memory_space=pltpu.VMEM),
        scratch_shapes=[
            pltpu.VMEM(held, jnp.bfloat16),
            pltpu.VMEM(tiles.shape, jnp.bfloat16),
            pltpu.VMEM((tiles_side + 1, features, side), jnp.float32),
            pltpu.SemaphoreType.DMA((len(pieces),)),
            pltpu.SemaphoreType.DMA((blocks_total,)),
        ],
        compiler_params=pltpu.CompilerParams(vmem_limit_bytes=40 * 2**20),
        cost_estimate=pl.CostEstimate(
            flops=2 * blocks_total * slots * side * side * features,
            bytes_accessed=tiles.size * 2 + blocks_total * tiles_side * features * side * 2,
            transcendentals=0,
        ),
        name="spread",
    )(ids, rows, cols, tiles, *pieces)


def on_device(
    features, aggregated, out_grad, w_self, w_neigh, tiles, tile_rows, tile_cols, tile_counts
):
    block_total = lax.axis_size("blk")
    copies = lax.axis_size("rep")
    planes = block_total // PLANE
    block = lax.axis_index("blk")
    core = lax.rem(block, 2)
    plane = block // PLANE
    share_rows, width = out_grad.shape
    side = tiles.shape[-1]
    slots = tiles.shape[2]
    per_share = share_rows // side
    tiles_side = per_share * copies
    slice_width = width // copies
    member = PLANE * copies
    groups = [[p * member + m for m in range(member)] for p in range(planes)]

    share = lax.dot_general(
        w_neigh, out_grad, (((1,), (1,)), ((), ())), preferred_element_type=jnp.float32
    ).astype(jnp.bfloat16)
    share = share.reshape(copies, slice_width, per_share, side).swapaxes(1, 2)
    sent = jnp.broadcast_to(share, (PLANE, *share.shape)).reshape(member, *share.shape[1:])
    arrived = plane_exchange(sent, groups)
    own = arrived.reshape(PLANE, tiles_side, slice_width, side)

    contract = (((0,), (0,)), ((), ()))
    terms_self = lax.dot_general(features, out_grad, contract, preferred_element_type=jnp.float32)
    terms_neigh = lax.dot_general(
        aggregated, out_grad, contract, preferred_element_type=jnp.float32
    )
    stacked = jnp.concatenate([terms_self, terms_neigh], axis=0)
    part = plane_exchange(stacked.reshape(member, -1, width), groups).sum(axis=0)
    hop = 1
    while hop < planes:
        pairs = [(b, b ^ (PLANE * hop)) for b in range(block_total)]
        part = part + lax.ppermute(part, "blk", pairs)
        hop *= 2
    scale = (share_rows * block_total * copies) ** (-0.5)
    part = part * scale
    whole = plane_exchange(jnp.broadcast_to(part, (member, *part.shape)), groups)
    whole = whole.reshape(2 * width, width)

    onward = [
        (b, (b + PLANE) % block_total if b % 2 == 0 else (b - PLANE) % block_total)
        for b in range(block_total)
    ]
    partner = [(b, b ^ 1) for b in range(block_total)]
    back = 1 - 2 * core
    lanes = jnp.arange(PLANE, dtype=jnp.int32)
    moving = [own[m : m + 1] for m in range(PLANE)]
    got, got_ids = [], []
    for step in range(1, planes // 2):
        moving = [lax.ppermute(m, "blk", onward) for m in moving]
        got += moving
        got_ids.append(lax.rem(plane - back * step + planes, planes) * PLANE + lanes)
    half = PLANE // 2
    last = [
        lax.ppermute(jnp.where(core == 0, moving[m], moving[m + half]), "blk", onward)
        for m in range(half)
    ]
    got += last
    far = lax.rem(plane + planes // 2, planes) * PLANE
    got_ids.append(far + core * half + lanes[:half])
    swapped = [lax.ppermute(g, "blk", partner) for g in got]
    swapped_ids = [
        lax.rem(plane + back * step + planes, planes) * PLANE + lanes
        for step in range(1, planes // 2)
    ]
    swapped_ids.append(far + (1 - core) * half + lanes[:half])
    ids = jnp.concatenate([plane * PLANE + lanes, *got_ids, *swapped_ids])

    live = jnp.arange(slots, dtype=jnp.int32)[None, :] < tile_counts[0][:, None]
    rows = jnp.where(live, tile_rows[0], tiles_side).reshape(-1)
    cols = jnp.where(live, tile_cols[0], 0).reshape(-1)
    spread = spread_over([own, *got, *swapped], ids, rows, cols, tiles[0], tiles_side)

    parts = spread.reshape(copies, per_share, slice_width, side)
    parts = lax.all_to_all(parts, "rep", 0, 0, tiled=True)
    spread_share = parts.transpose(1, 3, 0, 2).reshape(share_rows, width)
    self_part = lax.dot_general(
        out_grad, w_self, (((1,), (1,)), ((), ())), preferred_element_type=jnp.float32
    )
    return (spread_share + self_part, whole[:width], whole[width:])


def solution(mesh):
    placed = (
        P(("blk", "rep"), None),
        P(("blk", "rep"), None),
        P(("blk", "rep"), None),
        P(),
        P(),
        P("blk", None, None, None, None),
        P("blk", None, None),
        P("blk", None, None),
        P("blk", None),
    )
    return jax.shard_map(
        on_device,
        mesh=mesh,
        in_specs=placed,
        out_specs=(P(("blk", "rep"), None), P(), P()),
        check_vma=False,
    )
```

time: 229 us -> 119 us (0.52)
  waiting for transfers between devices: 156 us -> 20.5 us
  starting transfers between devices: 40.1 us -> 56.2 us
  Pallas kernels: 0 us -> 15.4 us
  other arithmetic: 13.7 us -> 6.61 us
  local copies, waits for them, and re-layouts: 7.7 us -> 13.5 us
  matrix products: 7.95 us -> 5.2 us
    all_to_all x7 -> x4, waiting for transfers between devices: 156 us -> 16.4 us  [the longest x3 11.8 us: plane_exchange(): return lax.all_to_all(x, BOTH, 0, 0, axis_index_groups=groups, tiled=True)]
    ppermute x0 -> x31, starting transfers between devices: none -> 31.3 us  [the longest x12 16 us: on_device(): moving = [lax.ppermute(m, 'blk', onward) for m in moving]]
    pallas_call x0 -> x1, Pallas kernels: none -> 15.4 us  [spread_over(): pl.pallas_call(functools.partial(spread_kernel, len(pieces), slots), out_...]
    all_to_all x7 -> x4, starting transfers between devices: 40.1 us -> 25 us  [the longest x3 19.2 us: plane_exchange(): return lax.all_to_all(x, BOTH, 0, 0, axis_index_groups=groups, tiled=True)]
    scatter-add x1 -> x0, other arithmetic: 9.65 us -> none  [on_device(): accumulated.at[target_rows].add(products.reshape(-1, side, width))]
    unnamed x8 -> x7, local copies, waits for them, and re-layouts: 0.02 us -> 5.82 us
    ppermute x0 -> x31, waiting for transfers between devices: none -> 4.07 us  [the longest x12 3.21 us: on_device(): moving = [lax.ppermute(m, 'blk', onward) for m in moving]]
    broadcast_in_dim x4 -> x2, local copies, waits for them, and re-layouts: 4.98 us -> 1.8 us  [the longest x1 0.91 us: on_device(): jnp.broadcast_to(share, (PLANE, *share.shape))]
  transfers between devices with their start and end apart: 7 -> 35, of which waited for: 6 -> 8; matrix products, arithmetic and copies ran while one was open for 10% -> 14% of each run, Pallas kernels for 0% -> 13%
where the time goes in v1:
time: 119 us; the launch traced here: 118 us
  starting transfers between devices  56.2 us (47%)
  waiting for transfers between devices  20.5 us (17%)
  Pallas kernels  15.4 us (13%)
  local copies, waits for them, and re-layouts  13.5 us (11%)
  other arithmetic  6.61 us (6%)
  matrix products  5.2 us (4%)
    all_to_all x3, starting transfers between devices, plane_exchange(): return lax.all_to_all(x, BOTH, 0, 0, axis_index_groups=groups, tiled=True)  19.2 us
    ppermute x12, starting transfers between devices, on_device(): moving = [lax.ppermute(m, 'blk', onward) for m in moving]  16 us
    pallas_call x1, Pallas kernels, spread_over(): pl.pallas_call(functools.partial(spread_kernel, len(pieces), slots), out_...  15.4 us
    all_to_all x3, waiting for transfers between devices, plane_exchange(): return lax.all_to_all(x, BOTH, 0, 0, axis_index_groups=groups, tiled=True)  11.8 us
    ppermute x3, starting transfers between devices, on_device(): part = part + lax.ppermute(part, 'blk', pairs)  9.53 us
    unnamed x7, local copies, waits for them, and re-layouts  5.82 us
    all_to_all x1, starting transfers between devices, on_device(): parts = lax.all_to_all(parts, 'rep', 0, 0, tiled=True)  5.73 us
    all_to_all x1, waiting for transfers between devices, on_device(): parts = lax.all_to_all(parts, 'rep', 0, 0, tiled=True)  4.62 us
  transfers between devices with their start and end apart: 35, of which 8 were waited for; matrix products, arithmetic and copies ran while one was open for 14% of the time, Pallas kernels for 13%

profile of v1, /device:TPU:8, one launch (start us, length us, event | category | flops | bytes accessed | tf_op | source)
XLA Modules:
  0.0 118.3 jit_solution(5310606894563353719)
XLA Ops:
  0.6 0.9 copy-done
  1.5 1.1 convolution_convert_fusion
  2.7 0.9 broadcast_in_dim.16
  3.6 7.5 %all-to-all-start = ((bf16[32,2,32,128]{3,2,1,0:T(8,128)(2,1)}), bf16[32,2,32,128]{3,2,1,0:T(8,128)(2,1)S(1)}, u32[]{:S(2)}, u32[]{:S(2)}) async-start(bf16[32,2,32,128]{3,2,1,0:T(8,128)(2,1)} %bitcast.3), calls=%async_computation | async-start | bytes 1048576 | tf_op jit(solution)/shard_map/all_to_all | solution.py:15
  11.2 1.1 fusion.2
  12.3 1.1 fusion.3
  13.4 0.9 pad_maximum_fusion
  14.3 7.0 %all-to-all-done = bf16[32,2,32,128]{3,2,1,0:T(8,128)(2,1)S(1)} async-done(((bf16[32,2,32,128]{3,2,1,0:T(8,128)(2,1)}), bf16[32,2,32,128]{3,2,1,0:T(8,128)(2,1)S(1)}, u32[]{:S(2)}, u32[]{:S(2)}) %all-to-all-start) | async-done | bytes 524320 | tf_op jit(solution)/shard_map/all_to_all | solution.py:15
  21.3 5.8 %all-to-all-start.2 = ((f32[32,16,256]{2,1,0:T(8,128)}), f32[32,16,256]{2,1,0:T(8,128)S(1)}, u32[]{:S(2)}, u32[]{:S(2)}) async-start(f32[32,16,256]{2,1,0:T(8,128)} %bitcast.11), calls=%async_computation.2 | async-start | bytes 1048576 | tf_op jit(solution)/shard_map/all_to_all | solution.py:15
  27.1 1.3 %iota_compare_fusion = pred[32,8]{1,0:T(8,128)(4,1)} fusion(s32[32]{0:T(128)} %bitcast.41), kind=kLoop, calls=%fused_computation.7 | loop fusion | flops 256 | bytes 384 | tf_op jit(solution)/shard_map/lt | solution.py:169
  28.5 2.0 %collective-permute-start.3 = (bf16[1,16,32,128]{3,2,1,0:T(8,128)(2,1)S(1)}, bf16[1,16,32,128]{3,2,1,0:T(8,128)(2,1)S(1)}, u32[]{:S(2)}, u32[]{:S(2)}) collective-permute-start(bf16[1,16,32,128]{3,2,1,0:T(8,128)(2,1)S(1)} %bitcast.40), channel_id=1, source_target_pairs={{0,32},{8,232},{16,48},{24,248},{32,64},{40,8},{48,80},{56,24},{64... | collective-permute-start | bytes 393224 | tf_op jit(solution)/shard_map/ppermute | solution.py:150
  30.5 1.9 %collective-permute-start.1 = (bf16[1,16,32,128]{3,2,1,0:T(8,128)(2,1)S(1)}, bf16[1,16,32,128]{3,2,1,0:T(8,128)(2,1)S(1)}, u32[]{:S(2)}, u32[]{:S(2)}) collective-permute-start(bf16[1,16,32,128]{3,2,1,0:T(8,128)(2,1)S(1)} %bitcast.39), channel_id=1, source_target_pairs={{0,32},{8,232},{16,48},{24,248},{32,64},{40,8},{48,80},{56,24},{64... | collective-permute-start | bytes 393224 | tf_op jit(solution)/shard_map/ppermute | solution.py:150
  32.4 4.8 %all-to-all-done.2 = f32[32,16,256]{2,1,0:T(8,128)S(1)} async-done(((f32[32,16,256]{2,1,0:T(8,128)}), f32[32,16,256]{2,1,0:T(8,128)S(1)}, u32[]{:S(2)}, u32[]{:S(2)}) %all-to-all-start.2) | async-done | bytes 524320 | tf_op jit(solution)/shard_map/all_to_all | solution.py:15
  37.2 2.0 %collective-permute-start.28 = (f32[16,256]{1,0:T(8,128)S(1)}, f32[16,256]{1,0:T(8,128)S(1)}, u32[]{:S(2)}, u32[]{:S(2)}) collective-permute-start(f32[16,256]{1,0:T(8,128)S(1)} %reduce_sum.9), channel_id=1, source_target_pairs={{0,32},{8,40},{16,48},{24,56},{32,0},{40,8},{48,16},{56,24},{64,96... | collective-permute-start | bytes 49160 | tf_op jit(solution)/shard_map/ppermute | solution.py:133
  39.3 0.6 slice_add_fusion
  39.9 3.7 %collective-permute-start = (bf16[1,16,32,128]{3,2,1,0:T(8,128)(2,1)S(1)}, bf16[1,16,32,128]{3,2,1,0:T(8,128)(2,1)S(1)}, u32[]{:S(2)}, u32[]{:S(2)}) collective-permute-start(bf16[1,16,32,128]{3,2,1,0:T(8,128)(2,1)S(1)} %bitcast.37), channel_id=1, source_target_pairs={{0,32},{8,232},{16,48},{24,248},{32,64},{40,8},{48,80},{56,24},{64... | collective-permute-start | bytes 393224 | tf_op jit(solution)/shard_map/ppermute | solution.py:150
  43.7 3.7 %collective-permute-start.29 = (f32[16,256]{1,0:T(8,128)S(1)}, f32[16,256]{1,0:T(8,128)S(1)}, u32[]{:S(2)}, u32[]{:S(2)}) collective-permute-start(f32[16,256]{1,0:T(8,128)S(1)} %add.134), channel_id=1, source_target_pairs={{0,64},{8,72},{16,80},{24,88},{32,96},{40,104},{48,112},{56,120},{... | collective-permute-start | bytes 49160 | tf_op jit(solution)/shard_map/ppermute | solution.py:133
  47.3 1.0 collective-permute-start.7
  49.3 3.9 %collective-permute-start.30 = (f32[16,256]{1,0:T(8,128)S(1)}, f32[16,256]{1,0:T(8,128)S(1)}, u32[]{:S(2)}, u32[]{:S(2)}) collective-permute-start(f32[16,256]{1,0:T(8,128)S(1)} %add.135), channel_id=1, source_target_pairs={{0,128},{8,136},{16,144},{24,152},{32,160},{40,168},{48,176},{56,1... | collective-permute-start | bytes 49160 | tf_op jit(solution)/shard_map/ppermute | solution.py:133
  53.1 0.6 iota_add_fusion.2
  53.7 1.0 collective-permute-start.6
  54.8 1.5 %collective-permute-start.4 = (bf16[1,16,32,128]{3,2,1,0:T(8,128)(2,1)S(1)}, bf16[1,16,32,128]{3,2,1,0:T(8,128)(2,1)S(1)}, u32[]{:S(2)}, u32[]{:S(2)}) collective-permute-start(bf16[1,16,32,128]{3,2,1,0:T(8,128)(2,1)S(1)} %collective-permute-done.rest_1_), channel_id=1, source_target_pairs={{0,32},{8,232},{16,48},{24,248},{32,64},{40,8},{48,80},{56,24},{64... | collective-permute-start | bytes 393224 | tf_op jit(solution)/shard_map/ppermute | solution.py:150
  56.2 1.0 collective-permute-start.11
  57.5 0.9 broadcast_in_dim.17
  58.4 6.0 %all-to-all-start.3 = ((f32[32,16,256]{2,1,0:T(8,128)}), f32[32,16,256]{2,1,0:T(8,128)}, u32[]{:S(2)}, u32[]{:S(2)}) async-start(f32[32,16,256]{2,1,0:T(8,128)} %broadcast_in_dim.17), calls=%async_computation.3 | async-start | bytes 1048576 | tf_op jit(solution)/shard_map/all_to_all | solution.py:15
  65.3 1.0 collective-permute-start.10
  66.3 2.4 %collective-permute-start.8 = (bf16[1,16,32,128]{3,2,1,0:T(8,128)(2,1)S(1)}, bf16[1,16,32,128]{3,2,1,0:T(8,128)(2,1)S(1)}, u32[]{:S(2)}, u32[]{:S(2)}) collective-permute-start(bf16[1,16,32,128]{3,2,1,0:T(8,128)(2,1)S(1)} %collective-permute-done.4.rest_5_), channel_id=1, source_target_pairs={{0,32},{8,232},{16,48},{24,248},{32,64},{40,8},{48,80},{56,24},{64... | collective-permute-start | bytes 393224 | tf_op jit(solution)/shard_map/ppermute | solution.py:150
  68.7 0.7 broadcast_select_fusion
  69.7 1.8 %collective-permute-done.10.rest_11_ = bf16[1,16,32,128]{3,2,1,0:T(8,128)(2,1)S(1)} collective-permute-done((bf16[1,16,32,128]{3,2,1,0:T(8,128)(2,1)S(1)}, bf16[1,16,32,128]{3,2,1,0:T(8,128)(2,1)S(1)}, u32[]{:S(2)}, u32[]{:S(2)}) %collective-permute-start.10) | collective-permute-done | bytes 131104 | tf_op jit(solution)/shard_map/ppermute | solution.py:150
  71.5 1.4 %collective-permute-done.8.rest_9_ = bf16[1,16,32,128]{3,2,1,0:T(8,128)(2,1)S(1)} collective-permute-done((bf16[1,16,32,128]{3,2,1,0:T(8,128)(2,1)S(1)}, bf16[1,16,32,128]{3,2,1,0:T(8,128)(2,1)S(1)}, u32[]{:S(2)}, u32[]{:S(2)}) %collective-permute-start.8) | collective-permute-done | bytes 131104 | tf_op jit(solution)/shard_map/ppermute | solution.py:150
  72.9 0.7 broadcast_select_fusion.1
  74.1 0.8 collective-permute-start.13
  75.0 1.4 %collective-permute-start.12 = (bf16[1,16,32,128]{3,2,1,0:T(8,128)(2,1)}, bf16[1,16,32,128]{3,2,1,0:T(8,128)(2,1)S(1)}, u32[]{:S(2)}, u32[]{:S(2)}) collective-permute-start(bf16[1,16,32,128]{3,2,1,0:T(8,128)(2,1)} %broadcast_select_fusion.1), channel_id=1, source_target_pairs={{0,32},{8,232},{16,48},{24,248},{32,64},{40,8},{48,80},{56,24},{64... | collective-permute-start | bytes 393224 | tf_op jit(solution)/shard_map/ppermute | solution.py:155
  76.9 0.6 iota_add_fusion.6
  77.4 0.8 copy.15
  78.2 0.7 squeeze.10
  78.9 0.8 copy.14
  79.6 0.7 squeeze.9
  80.3 0.8 lt.24
  81.1 0.8 concatenate.6.ids
  83.1 0.7 broadcast_select_fusion.2
  84.3 3.4 %copy-done.1 = bf16[1,32,8,128,128]{4,3,2,1,0:T(8,128)(2,1)S(1)} copy-done((bf16[1,32,8,128,128]{4,3,2,1,0:T(8,128)(2,1)S(1)}, bf16[1,32,8,128,128]{4,3,2,1,0:T(8,128)(2,1)}, u32[]{:S(2)}) %copy-start.1) | copy-done | bytes 8388632
  87.7 15.4 %spread.1 = f32[16,32,128]{2,1,0:T(8,128)S(1)} custom-call(s32[32]{0:T(128)S(1)} %concatenate.6.ids, s32[256]{0:T(256)S(1)} %get-tuple-element.10.rows, s32[256]{0:T(256)S(1)} %get-tuple-element.9.cols, bf16[32,8,128,128]{3,2,1,0:T(8,128)(2,1)S(1)} %bitcast.29, bf16[4,16,32,128]{3,2,1,0:T(8,128)(2,1)S(1)} %bitcast.30, ...), custom_call_target="tpu_custom_call" | custom-call | flops 268435456 | bytes 12582912 | tf_op jit(solution)/shard_map/spread/pallas_call | solution.py:75
  103.2 0.9 copy.17
  104.1 5.7 %all-to-all-start.1 = ((f32[8,2,32,128]{3,1,2,0:T(2,128)}), f32[8,2,32,128]{3,1,2,0:T(2,128)S(1)}, u32[]{:S(2)}, u32[]{:S(2)}) async-start(f32[8,2,32,128]{3,1,2,0:T(2,128)} %copy.17), calls=%async_computation.1 | async-start | bytes 524288 | tf_op jit(solution)/shard_map/all_to_all | solution.py:175
  109.8 1.9 %fusion = (f32[16,16,256]{2,1,0:T(8,128)}, f32[16,16,256]{2,1,0:T(8,128)}) fusion(f32[32,16,256]{2,1,0:T(8,128)} %all-to-all-done.3), kind=kLoop, calls=%fused_computation.19 | loop fusion | bytes 1048576 | tf_op jit(solution)/shard_map/slice | solution.py:180
  111.7 4.6 %all-to-all-done.1 = f32[8,2,32,128]{3,1,2,0:T(2,128)S(1)} async-done(((f32[8,2,32,128]{3,1,2,0:T(2,128)}), f32[8,2,32,128]{3,1,2,0:T(2,128)S(1)}, u32[]{:S(2)}, u32[]{:S(2)}) %all-to-all-start.1) | async-done | bytes 262176 | tf_op jit(solution)/shard_map/all_to_all | solution.py:175
  116.4 1.8 %convolution_add_fusion = f32[256,256]{1,0:T(8,128)} fusion(f32[256,256]{1,0:T(8,128)S(1)} %copy.18, bf16[256,256]{1,0:T(8,128)(2,1)S(1)} %copy-done, bf16[256,256]{1,0:T(8,128)(2,1)} %param.12), kind=kOutput, calls=%fused_computation | convolution fusion | flops 33619968 | bytes 786432 | tf_op jit(solution)/shard_map/dot_general | solution.py:177
  (61 shorter events, 5.7 us)
Async XLA Ops:
  0.6 0.9 copy-start
  3.6 17.7 %all-to-all-start = ((bf16[32,2,32,128]{3,2,1,0:T(8,128)(2,1)}), bf16[32,2,32,128]{3,2,1,0:T(8,128)(2,1)S(1)}, u32[]{:S(2)}, u32[]{:S(2)}) async-start(bf16[32,2,32,128]{3,2,1,0:T(8,128)(2,1)} %bitcast.3), calls=%async_computation | async-start | bytes 1048576 | tf_op jit(solution)/shard_map/all_to_all | solution.py:15
  21.3 15.9 %all-to-all-start.2 = ((f32[32,16,256]{2,1,0:T(8,128)}), f32[32,16,256]{2,1,0:T(8,128)S(1)}, u32[]{:S(2)}, u32[]{:S(2)}) async-start(f32[32,16,256]{2,1,0:T(8,128)} %bitcast.11), calls=%async_computation.2 | async-start | bytes 1048576 | tf_op jit(solution)/shard_map/all_to_all | solution.py:15
  28.5 18.9 %collective-permute-start.3 = (bf16[1,16,32,128]{3,2,1,0:T(8,128)(2,1)S(1)}, bf16[1,16,32,128]{3,2,1,0:T(8,128)(2,1)S(1)}, u32[]{:S(2)}, u32[]{:S(2)}) collective-permute-start(bf16[1,16,32,128]{3,2,1,0:T(8,128)(2,1)S(1)} %bitcast.40), channel_id=1, source_target_pairs={{0,32},{8,232},{16,48},{24,248},{32,64},{40,8},{48,80},{56,24},{64... | collective-permute-start | bytes 393224 | tf_op jit(solution)/shard_map/ppermute | solution.py:150
  30.5 17.9 %collective-permute-start.1 = (bf16[1,16,32,128]{3,2,1,0:T(8,128)(2,1)S(1)}, bf16[1,16,32,128]{3,2,1,0:T(8,128)(2,1)S(1)}, u32[]{:S(2)}, u32[]{:S(2)}) collective-permute-start(bf16[1,16,32,128]{3,2,1,0:T(8,128)(2,1)S(1)} %bitcast.39), channel_id=1, source_target_pairs={{0,32},{8,232},{16,48},{24,248},{32,64},{40,8},{48,80},{56,24},{64... | collective-permute-start | bytes 393224 | tf_op jit(solution)/shard_map/ppermute | solution.py:150
  37.2 6.4 %collective-permute-start.28 = (f32[16,256]{1,0:T(8,128)S(1)}, f32[16,256]{1,0:T(8,128)S(1)}, u32[]{:S(2)}, u32[]{:S(2)}) collective-permute-start(f32[16,256]{1,0:T(8,128)S(1)} %reduce_sum.9), channel_id=1, source_target_pairs={{0,32},{8,40},{16,48},{24,56},{32,0},{40,8},{48,16},{56,24},{64,96... | collective-permute-start | bytes 49160 | tf_op jit(solution)/shard_map/ppermute | solution.py:133
  39.8 13.9 %collective-permute-start.2 = (bf16[1,16,32,128]{3,2,1,0:T(8,128)(2,1)S(1)}, bf16[1,16,32,128]{3,2,1,0:T(8,128)(2,1)S(1)}, u32[]{:S(2)}, u32[]{:S(2)}) collective-permute-start(bf16[1,16,32,128]{3,2,1,0:T(8,128)(2,1)S(1)} %bitcast.38), channel_id=1, source_target_pairs={{0,32},{8,232},{16,48},{24,248},{32,64},{40,8},{48,80},{56,24},{64... | collective-permute-start | bytes 393224 | tf_op jit(solution)/shard_map/ppermute | solution.py:150
  39.9 14.8 %collective-permute-start = (bf16[1,16,32,128]{3,2,1,0:T(8,128)(2,1)S(1)}, bf16[1,16,32,128]{3,2,1,0:T(8,128)(2,1)S(1)}, u32[]{:S(2)}, u32[]{:S(2)}) collective-permute-start(bf16[1,16,32,128]{3,2,1,0:T(8,128)(2,1)S(1)} %bitcast.37), channel_id=1, source_target_pairs={{0,32},{8,232},{16,48},{24,248},{32,64},{40,8},{48,80},{56,24},{64... | collective-permute-start | bytes 393224 | tf_op jit(solution)/shard_map/ppermute | solution.py:150
  43.7 5.6 %collective-permute-start.29 = (f32[16,256]{1,0:T(8,128)S(1)}, f32[16,256]{1,0:T(8,128)S(1)}, u32[]{:S(2)}, u32[]{:S(2)}) collective-permute-start(f32[16,256]{1,0:T(8,128)S(1)} %add.134), channel_id=1, source_target_pairs={{0,64},{8,72},{16,80},{24,88},{32,96},{40,104},{48,112},{56,120},{... | collective-permute-start | bytes 49160 | tf_op jit(solution)/shard_map/ppermute | solution.py:133
  47.3 8.9 %collective-permute-start.7 = (bf16[1,16,32,128]{3,2,1,0:T(8,128)(2,1)S(1)}, bf16[1,16,32,128]{3,2,1,0:T(8,128)(2,1)S(1)}, u32[]{:S(2)}, u32[]{:S(2)}) collective-permute-start(bf16[1,16,32,128]{3,2,1,0:T(8,128)(2,1)S(1)} %collective-permute-done.3.rest_4_), channel_id=1, source_target_pairs={{0,32},{8,232},{16,48},{24,248},{32,64},{40,8},{48,80},{56,24},{64... | collective-permute-start | bytes 393224 | tf_op jit(solution)/shard_map/ppermute | solution.py:150
  48.4 8.9 %collective-permute-start.5 = (bf16[1,16,32,128]{3,2,1,0:T(8,128)(2,1)S(1)}, bf16[1,16,32,128]{3,2,1,0:T(8,128)(2,1)S(1)}, u32[]{:S(2)}, u32[]{:S(2)}) collective-permute-start(bf16[1,16,32,128]{3,2,1,0:T(8,128)(2,1)S(1)} %collective-permute-done.1.rest_2_), channel_id=1, source_target_pairs={{0,32},{8,232},{16,48},{24,248},{32,64},{40,8},{48,80},{56,24},{64... | collective-permute-start | bytes 393224 | tf_op jit(solution)/shard_map/ppermute | solution.py:150
  49.3 8.2 %collective-permute-start.30 = (f32[16,256]{1,0:T(8,128)S(1)}, f32[16,256]{1,0:T(8,128)S(1)}, u32[]{:S(2)}, u32[]{:S(2)}) collective-permute-start(f32[16,256]{1,0:T(8,128)S(1)} %add.135), channel_id=1, source_target_pairs={{0,128},{8,136},{16,144},{24,152},{32,160},{40,168},{48,176},{56,1... | collective-permute-start | bytes 49160 | tf_op jit(solution)/shard_map/ppermute | solution.py:133
  53.7 10.9 %collective-permute-start.6 = (bf16[1,16,32,128]{3,2,1,0:T(8,128)(2,1)S(1)}, bf16[1,16,32,128]{3,2,1,0:T(8,128)(2,1)S(1)}, u32[]{:S(2)}, u32[]{:S(2)}) collective-permute-start(bf16[1,16,32,128]{3,2,1,0:T(8,128)(2,1)S(1)} %collective-permute-done.2.rest_3_), channel_id=1, source_target_pairs={{0,32},{8,232},{16,48},{24,248},{32,64},{40,8},{48,80},{56,24},{64... | collective-permute-start | bytes 393224 | tf_op jit(solution)/shard_map/ppermute | solution.py:150
  54.8 10.2 %collective-permute-start.4 = (bf16[1,16,32,128]{3,2,1,0:T(8,128)(2,1)S(1)}, bf16[1,16,32,128]{3,2,1,0:T(8,128)(2,1)S(1)}, u32[]{:S(2)}, u32[]{:S(2)}) collective-permute-start(bf16[1,16,32,128]{3,2,1,0:T(8,128)(2,1)S(1)} %collective-permute-done.rest_1_), channel_id=1, source_target_pairs={{0,32},{8,232},{16,48},{24,248},{32,64},{40,8},{48,80},{56,24},{64... | collective-permute-start | bytes 393224 | tf_op jit(solution)/shard_map/ppermute | solution.py:150
  56.2 9.0 %collective-permute-start.11 = (bf16[1,16,32,128]{3,2,1,0:T(8,128)(2,1)S(1)}, bf16[1,16,32,128]{3,2,1,0:T(8,128)(2,1)S(1)}, u32[]{:S(2)}, u32[]{:S(2)}) collective-permute-start(bf16[1,16,32,128]{3,2,1,0:T(8,128)(2,1)S(1)} %collective-permute-done.7.rest_8_), channel_id=1, source_target_pairs={{0,32},{8,232},{16,48},{24,248},{32,64},{40,8},{48,80},{56,24},{64... | collective-permute-start | bytes 393224 | tf_op jit(solution)/shard_map/ppermute | solution.py:150
  57.3 9.0 %collective-permute-start.9 = (bf16[1,16,32,128]{3,2,1,0:T(8,128)(2,1)S(1)}, bf16[1,16,32,128]{3,2,1,0:T(8,128)(2,1)S(1)}, u32[]{:S(2)}, u32[]{:S(2)}) collective-permute-start(bf16[1,16,32,128]{3,2,1,0:T(8,128)(2,1)S(1)} %collective-permute-done.5.rest_6_), channel_id=1, source_target_pairs={{0,32},{8,232},{16,48},{24,248},{32,64},{40,8},{48,80},{56,24},{64... | collective-permute-start | bytes 393224 | tf_op jit(solution)/shard_map/ppermute | solution.py:150
  58.4 45.7 %all-to-all-start.3 = ((f32[32,16,256]{2,1,0:T(8,128)}), f32[32,16,256]{2,1,0:T(8,128)}, u32[]{:S(2)}, u32[]{:S(2)}) async-start(f32[32,16,256]{2,1,0:T(8,128)} %broadcast_in_dim.17), calls=%async_computation.3 | async-start | bytes 1048576 | tf_op jit(solution)/shard_map/all_to_all | solution.py:15
  64.4 5.0 %collective-permute-start.14 = (bf16[1,16,32,128]{3,2,1,0:T(8,128)(2,1)S(1)}, bf16[1,16,32,128]{3,2,1,0:T(8,128)(2,1)S(1)}, u32[]{:S(2)}, u32[]{:S(2)}) collective-permute-start(bf16[1,16,32,128]{3,2,1,0:T(8,128)(2,1)S(1)} %collective-permute-done.rest_1_), channel_id=1, source_target_pairs={{0,8},{8,0},{16,24},{24,16},{32,40},{40,32},{48,56},{56,48},{64,72... | collective-permute-start | bytes 393224 | tf_op jit(solution)/shard_map/ppermute | solution.py:161
  64.6 8.9 %collective-permute-start.15 = (bf16[1,16,32,128]{3,2,1,0:T(8,128)(2,1)S(1)}, bf16[1,16,32,128]{3,2,1,0:T(8,128)(2,1)S(1)}, u32[]{:S(2)}, u32[]{:S(2)}) collective-permute-start(bf16[1,16,32,128]{3,2,1,0:T(8,128)(2,1)S(1)} %collective-permute-done.1.rest_2_), channel_id=1, source_target_pairs={{0,8},{8,0},{16,24},{24,16},{32,40},{40,32},{48,56},{56,48},{64,72... | collective-permute-start | bytes 393224 | tf_op jit(solution)/shard_map/ppermute | solution.py:161
  65.0 9.1 %collective-permute-start.16 = (bf16[1,16,32,128]{3,2,1,0:T(8,128)(2,1)S(1)}, bf16[1,16,32,128]{3,2,1,0:T(8,128)(2,1)S(1)}, u32[]{:S(2)}, u32[]{:S(2)}) collective-permute-start(bf16[1,16,32,128]{3,2,1,0:T(8,128)(2,1)S(1)} %collective-permute-done.2.rest_3_), channel_id=1, source_target_pairs={{0,8},{8,0},{16,24},{24,16},{32,40},{40,32},{48,56},{56,48},{64,72... | collective-permute-start | bytes 393224 | tf_op jit(solution)/shard_map/ppermute | solution.py:161
  65.3 6.2 %collective-permute-start.10 = (bf16[1,16,32,128]{3,2,1,0:T(8,128)(2,1)S(1)}, bf16[1,16,32,128]{3,2,1,0:T(8,128)(2,1)S(1)}, u32[]{:S(2)}, u32[]{:S(2)}) collective-permute-start(bf16[1,16,32,128]{3,2,1,0:T(8,128)(2,1)S(1)} %collective-permute-done.6.rest_7_), channel_id=1, source_target_pairs={{0,32},{8,232},{16,48},{24,248},{32,64},{40,8},{48,80},{56,24},{64... | collective-permute-start | bytes 393224 | tf_op jit(solution)/shard_map/ppermute | solution.py:150
  66.3 6.6 %collective-permute-start.8 = (bf16[1,16,32,128]{3,2,1,0:T(8,128)(2,1)S(1)}, bf16[1,16,32,128]{3,2,1,0:T(8,128)(2,1)S(1)}, u32[]{:S(2)}, u32[]{:S(2)}) collective-permute-start(bf16[1,16,32,128]{3,2,1,0:T(8,128)(2,1)S(1)} %collective-permute-done.4.rest_5_), channel_id=1, source_target_pairs={{0,32},{8,232},{16,48},{24,248},{32,64},{40,8},{48,80},{56,24},{64... | collective-permute-start | bytes 393224 | tf_op jit(solution)/shard_map/ppermute | solution.py:150
  69.4 4.8 %collective-permute-start.17 = (bf16[1,16,32,128]{3,2,1,0:T(8,128)(2,1)S(1)}, bf16[1,16,32,128]{3,2,1,0:T(8,128)(2,1)S(1)}, u32[]{:S(2)}, u32[]{:S(2)}) collective-permute-start(bf16[1,16,32,128]{3,2,1,0:T(8,128)(2,1)S(1)} %collective-permute-done.3.rest_4_), channel_id=1, source_target_pairs={{0,8},{8,0},{16,24},{24,16},{32,40},{40,32},{48,56},{56,48},{64,72... | collective-permute-start | bytes 393224 | tf_op jit(solution)/shard_map/ppermute | solution.py:161
  71.5 3.5 %collective-permute-start.18 = (bf16[1,16,32,128]{3,2,1,0:T(8,128)(2,1)S(1)}, bf16[1,16,32,128]{3,2,1,0:T(8,128)(2,1)S(1)}, u32[]{:S(2)}, u32[]{:S(2)}) collective-permute-start(bf16[1,16,32,128]{3,2,1,0:T(8,128)(2,1)S(1)} %collective-permute-done.4.rest_5_), channel_id=1, source_target_pairs={{0,8},{8,0},{16,24},{24,16},{32,40},{40,32},{48,56},{56,48},{64,72... | collective-permute-start | bytes 393224 | tf_op jit(solution)/shard_map/ppermute | solution.py:161
  72.9 3.5 %collective-permute-start.19 = (bf16[1,16,32,128]{3,2,1,0:T(8,128)(2,1)S(1)}, bf16[1,16,32,128]{3,2,1,0:T(8,128)(2,1)S(1)}, u32[]{:S(2)}, u32[]{:S(2)}) collective-permute-start(bf16[1,16,32,128]{3,2,1,0:T(8,128)(2,1)S(1)} %collective-permute-done.5.rest_6_), channel_id=1, source_target_pairs={{0,8},{8,0},{16,24},{24,16},{32,40},{40,32},{48,56},{56,48},{64,72... | collective-permute-start | bytes 393224 | tf_op jit(solution)/shard_map/ppermute | solution.py:161
  73.5 8.3 %collective-permute-start.20 = (bf16[1,16,32,128]{3,2,1,0:T(8,128)(2,1)S(1)}, bf16[1,16,32,128]{3,2,1,0:T(8,128)(2,1)S(1)}, u32[]{:S(2)}, u32[]{:S(2)}) collective-permute-start(bf16[1,16,32,128]{3,2,1,0:T(8,128)(2,1)S(1)} %collective-permute-done.6.rest_7_), channel_id=1, source_target_pairs={{0,8},{8,0},{16,24},{24,16},{32,40},{40,32},{48,56},{56,48},{64,72... | collective-permute-start | bytes 393224 | tf_op jit(solution)/shard_map/ppermute | solution.py:161
  74.1 7.9 %collective-permute-start.21 = (bf16[1,16,32,128]{3,2,1,0:T(8,128)(2,1)S(1)}, bf16[1,16,32,128]{3,2,1,0:T(8,128)(2,1)S(1)}, u32[]{:S(2)}, u32[]{:S(2)}) collective-permute-start(bf16[1,16,32,128]{3,2,1,0:T(8,128)(2,1)S(1)} %collective-permute-done.7.rest_8_), channel_id=1, source_target_pairs={{0,8},{8,0},{16,24},{24,16},{32,40},{40,32},{48,56},{56,48},{64,72... | collective-permute-start | bytes 393224 | tf_op jit(solution)/shard_map/ppermute | solution.py:161
  74.1 8.3 %collective-permute-start.13 = (bf16[1,16,32,128]{3,2,1,0:T(8,128)(2,1)}, bf16[1,16,32,128]{3,2,1,0:T(8,128)(2,1)S(1)}, u32[]{:S(2)}, u32[]{:S(2)}) collective-permute-start(bf16[1,16,32,128]{3,2,1,0:T(8,128)(2,1)} %broadcast_select_fusion), channel_id=1, source_target_pairs={{0,32},{8,232},{16,48},{24,248},{32,64},{40,8},{48,80},{56,24},{64... | collective-permute-start | bytes 393224 | tf_op jit(solution)/shard_map/ppermute | solution.py:155
  75.0 7.6 %collective-permute-start.12 = (bf16[1,16,32,128]{3,2,1,0:T(8,128)(2,1)}, bf16[1,16,32,128]{3,2,1,0:T(8,128)(2,1)S(1)}, u32[]{:S(2)}, u32[]{:S(2)}) collective-permute-start(bf16[1,16,32,128]{3,2,1,0:T(8,128)(2,1)} %broadcast_select_fusion.1), channel_id=1, source_target_pairs={{0,32},{8,232},{16,48},{24,248},{32,64},{40,8},{48,80},{56,24},{64... | collective-permute-start | bytes 393224 | tf_op jit(solution)/shard_map/ppermute | solution.py:155
  76.4 6.6 %collective-permute-start.22 = (bf16[1,16,32,128]{3,2,1,0:T(8,128)(2,1)S(1)}, bf16[1,16,32,128]{3,2,1,0:T(8,128)(2,1)}, u32[]{:S(2)}, u32[]{:S(2)}) collective-permute-start(bf16[1,16,32,128]{3,2,1,0:T(8,128)(2,1)S(1)} %collective-permute-done.8.rest_9_), channel_id=1, source_target_pairs={{0,8},{8,0},{16,24},{24,16},{32,40},{40,32},{48,56},{56,48},{64,72... | collective-permute-start | bytes 393224 | tf_op jit(solution)/shard_map/ppermute | solution.py:161
  81.9 1.9 %collective-permute-start.23 = (bf16[1,16,32,128]{3,2,1,0:T(8,128)(2,1)S(1)}, bf16[1,16,32,128]{3,2,1,0:T(8,128)(2,1)S(1)}, u32[]{:S(2)}, u32[]{:S(2)}) collective-permute-start(bf16[1,16,32,128]{3,2,1,0:T(8,128)(2,1)S(1)} %collective-permute-done.9.rest_10_), channel_id=1, source_target_pairs={{0,8},{8,0},{16,24},{24,16},{32,40},{40,32},{48,56},{56,48},{64,72... | collective-permute-start | bytes 393224 | tf_op jit(solution)/shard_map/ppermute | solution.py:161
  82.0 1.8 %collective-permute-start.24 = (bf16[1,16,32,128]{3,2,1,0:T(8,128)(2,1)S(1)}, bf16[1,16,32,128]{3,2,1,0:T(8,128)(2,1)S(1)}, u32[]{:S(2)}, u32[]{:S(2)}) collective-permute-start(bf16[1,16,32,128]{3,2,1,0:T(8,128)(2,1)S(1)} %collective-permute-done.10.rest_11_), channel_id=1, source_target_pairs={{0,8},{8,0},{16,24},{24,16},{32,40},{40,32},{48,56},{56,48},{64,72... | collective-permute-start | bytes 393224 | tf_op jit(solution)/shard_map/ppermute | solution.py:161
  82.5 1.3 %collective-permute-start.25 = (bf16[1,16,32,128]{3,2,1,0:T(8,128)(2,1)S(1)}, bf16[1,16,32,128]{3,2,1,0:T(8,128)(2,1)S(1)}, u32[]{:S(2)}, u32[]{:S(2)}) collective-permute-start(bf16[1,16,32,128]{3,2,1,0:T(8,128)(2,1)S(1)} %collective-permute-done.11.rest_12_), channel_id=1, source_target_pairs={{0,8},{8,0},{16,24},{24,16},{32,40},{40,32},{48,56},{56,48},{64,72... | collective-permute-start | bytes 393224 | tf_op jit(solution)/shard_map/ppermute | solution.py:161
  82.6 1.4 %collective-permute-start.27 = (bf16[1,16,32,128]{3,2,1,0:T(8,128)(2,1)S(1)}, bf16[1,16,32,128]{3,2,1,0:T(8,128)(2,1)S(1)}, u32[]{:S(2)}, u32[]{:S(2)}) collective-permute-start(bf16[1,16,32,128]{3,2,1,0:T(8,128)(2,1)S(1)} %collective-permute-done.13.rest_14_), channel_id=1, source_target_pairs={{0,8},{8,0},{16,24},{24,16},{32,40},{40,32},{48,56},{56,48},{64,72... | collective-permute-start | bytes 393224 | tf_op jit(solution)/shard_map/ppermute | solution.py:161
  83.0 1.3 %collective-permute-start.26 = (bf16[1,16,32,128]{3,2,1,0:T(8,128)(2,1)S(1)}, bf16[1,16,32,128]{3,2,1,0:T(8,128)(2,1)S(1)}, u32[]{:S(2)}, u32[]{:S(2)}) collective-permute-start(bf16[1,16,32,128]{3,2,1,0:T(8,128)(2,1)S(1)} %collective-permute-done.12.rest_13_), channel_id=1, source_target_pairs={{0,8},{8,0},{16,24},{24,16},{32,40},{40,32},{48,56},{56,48},{64,72... | collective-permute-start | bytes 393224 | tf_op jit(solution)/shard_map/ppermute | solution.py:161
  84.3 3.4 %copy-start.1 = (bf16[1,32,8,128,128]{4,3,2,1,0:T(8,128)(2,1)S(1)}, bf16[1,32,8,128,128]{4,3,2,1,0:T(8,128)(2,1)}, u32[]{:S(2)}) copy-start(bf16[1,32,8,128,128]{4,3,2,1,0:T(8,128)(2,1)} %param.14) | copy-start | bytes 25165828
  104.1 12.2 %all-to-all-start.1 = ((f32[8,2,32,128]{3,1,2,0:T(2,128)}), f32[8,2,32,128]{3,1,2,0:T(2,128)S(1)}, u32[]{:S(2)}, u32[]{:S(2)}) async-start(f32[8,2,32,128]{3,1,2,0:T(2,128)} %copy.17), calls=%async_computation.1 | async-start | bytes 524288 | tf_op jit(solution)/shard_map/all_to_all | solution.py:175

commit v2 on v0

v2 whole, which is shorter than its diff:
```python
import functools

import jax
import jax.numpy as jnp
from jax import lax
from jax.experimental import pallas as pl
from jax.experimental.pallas import tpu as pltpu
from jax.sharding import PartitionSpec as P

PLANE = 4
HALF = PLANE // 2
BOTH = ("blk", "rep")
AS_SHORT = pl.CostEstimate(flops=1, bytes_accessed=0, transcendentals=0)
AS_LONG = pl.CostEstimate(flops=20000000000, bytes_accessed=0, transcendentals=0)
VMEM = pl.BlockSpec(memory_space=pltpu.VMEM)
SMEM = pl.BlockSpec(memory_space=pltpu.SMEM)
ROOM = pltpu.CompilerParams(vmem_limit_bytes=16 * 2**20)
BY_LAST = (((1,), (1,)), ((), ()))


def exchange(x, axes, groups=None):
    return lax.all_to_all(x, axes, 0, 0, axis_index_groups=groups, tiled=True)


def opening_kernel(features, aggregated, grad, weight, out):
    share = lax.dot_general(
        weight[...], grad[...], BY_LAST, preferred_element_type=jnp.float32
    ).astype(out.dtype)
    again, slices, held, width, side = out.shape
    tiles = held - 2
    for s in range(slices):
        for t in range(tiles):
            part = share[s * width : (s + 1) * width, t * side : (t + 1) * side]
            for q in range(again):
                out[q, s, t] = part
    depth = width // 2
    rows = slices * depth
    for q in range(again):
        source = (features, aggregated)[q // HALF]
        first = q % HALF * rows
        terms = lax.dot_general(
            source[:, first : first + rows],
            grad[...],
            (((0,), (0,)), ((), ())),
            preferred_element_type=jnp.float32,
        )
        upper = terms.astype(out.dtype)
        lower = (terms - upper.astype(jnp.float32)).astype(out.dtype)
        for s in range(slices):
            here = slice(s * depth, (s + 1) * depth)
            for place, half in ((tiles, upper), (tiles + 1, lower)):
                out[q, s, place, :depth] = half[here, :side]
                out[q, s, place, depth:] = half[here, side:]


def opening(features, aggregated, out_grad, w_neigh, copies, side):
    rows, width = out_grad.shape
    shape = (PLANE, copies, rows // side + 2, width // copies, side)
    return pl.pallas_call(
        opening_kernel,
        out_shape=jax.ShapeDtypeStruct(shape, jnp.bfloat16),
        compiler_params=pltpu.CompilerParams(vmem_limit_bytes=60 * 2**20),
        name="opening",
    )(features, aggregated, out_grad, w_neigh)


def plane_sum_kernel(arrived, out):
    tiles = arrived.shape[1] - 2
    total = jnp.zeros(out.shape[1:], jnp.float32)
    for m in range(arrived.shape[0]):
        total = total + (
            arrived[m, tiles].astype(jnp.float32) + arrived[m, tiles + 1].astype(jnp.float32)
        )
    for copy in range(out.shape[0]):
        out[copy] = total


def plane_sum(arrived, again):
    return pl.pallas_call(
        plane_sum_kernel,
        out_shape=jax.ShapeDtypeStruct((again, *arrived.shape[2:]), jnp.float32),
        compiler_params=ROOM,
        name="plane_sum",
    )(arrived)


def codes_kernel(tiles_side, rows, cols, counts, out):
    slot = lax.broadcasted_iota(jnp.int32, out.shape, 0)
    code = rows[0] * tiles_side + cols[0]
    out[...] = jnp.where(slot < counts[...], code, tiles_side * tiles_side)


def slot_codes(tile_rows, tile_cols, tile_counts, tiles_side):
    _, blocks, slots = tile_rows.shape
    return pl.pallas_call(
        functools.partial(codes_kernel, tiles_side),
        out_shape=jax.ShapeDtypeStruct((slots, blocks), jnp.int32),
        cost_estimate=AS_LONG,
        compiler_params=ROOM,
        name="codes",
    )(tile_rows.swapaxes(1, 2), tile_cols.swapaxes(1, 2), tile_counts)


def summed_kernel(scale, parts, out):
    total = parts[0]
    for p in range(1, parts.shape[0]):
        total = total + parts[p]
    if scale != 1.0:
        total = total * scale
    for copy in range(out.shape[0]):
        out[copy] = total


def summed(parts, again, scale):
    return pl.pallas_call(
        functools.partial(summed_kernel, scale),
        out_shape=jax.ShapeDtypeStruct((again, *parts.shape[1:]), parts.dtype),
        compiler_params=ROOM,
        name="summed",
    )(parts)


def result_kernel(parts, whole, grad, weight, out, self_out, neigh_out):
    straight = lax.dot_general(
        grad[...], weight[...], BY_LAST, preferred_element_type=jnp.float32
    )
    slices, tiles, width, side = parts.shape
    for t in range(tiles):
        rows = slice(t * side, (t + 1) * side)
        spread = parts[:, t].reshape(slices * width, side)
        out[rows] = straight[rows] + spread.T
    members, depth = whole.shape[0], whole.shape[1] // 2
    for m in range(members):
        target = (self_out, neigh_out)[2 * m // members]
        top = m % (members // 2) * depth
        target[top : top + depth, :side] = whole[m, :depth]
        target[top : top + depth, side:] = whole[m, depth:]


def result(parts, whole, out_grad, w_self):
    rows, width = out_grad.shape
    return pl.pallas_call(
        result_kernel,
        out_shape=[
            jax.ShapeDtypeStruct((rows, width), jnp.float32),
            jax.ShapeDtypeStruct((width, width), jnp.float32),
            jax.ShapeDtypeStruct((width, width), jnp.float32),
        ],
        compiler_params=ROOM,
        name="result",
    )(parts, whole, out_grad, w_self)


def spread_kernel(sources, resumed, codes, tiles, *refs):
    pieces, refs = refs[: len(sources)], refs[len(sources) :]
    begun, refs = (refs[0], refs[1:]) if resumed else (None, refs)
    out, acc = refs
    tiles_side, width, side = out.shape
    slots = tiles.shape[2]
    shift = tiles_side.bit_length() - 1
    block = lax.axis_index("blk")
    acc[:tiles_side] = begun[...] if resumed else jnp.zeros(out.shape, jnp.float32)
    acc[tiles_side] = jnp.zeros(out.shape[1:], jnp.float32)
    for piece, source_of in zip(pieces, sources):
        for m in range(piece.shape[0]):
            source = source_of(block, m)
            code = [codes[k, source] for k in range(slots)]
            row = [lax.shift_right_logical(c, shift) for c in code]
            col = [lax.bitwise_and(c, tiles_side - 1) for c in code]
            for k in range(0, slots, 2):
                pair = jnp.concatenate([piece[m, col[k]], piece[m, col[k + 1]]], axis=0)
                both = tiles[0, source, k : k + 2].reshape(2 * side, side)
                product = lax.dot_general(
                    pair, both, BY_LAST, preferred_element_type=jnp.float32
                )
                acc[row[k]] = acc[row[k]] + product[:width, :side]
                acc[row[k + 1]] = acc[row[k + 1]] + product[width:, side:]
    out[...] = acc[:tiles_side]


def spread_over(pieces, sources, codes, tiles, begun=None):
    _, tiles_side, width, side = pieces[0].shape
    shape = (tiles_side, width, side)
    resumed = begun is not None
    operands = [tiles, *pieces, *([begun] if resumed else [])]
    return pl.pallas_call(
        functools.partial(spread_kernel, sources, resumed),
        out_shape=jax.ShapeDtypeStruct(shape, jnp.float32),
        in_specs=[SMEM] + [VMEM] * len(operands),
        out_specs=VMEM,
        scratch_shapes=[pltpu.VMEM((tiles_side + 1, width, side), jnp.float32)],
        compiler_params=ROOM,
        cost_estimate=AS_SHORT if resumed else AS_LONG,
        name="spread_on" if resumed else "spread",
    )(codes, *operands)


def on_device(
    features, aggregated, out_grad, w_self, w_neigh, tiles, tile_rows, tile_cols, tile_counts
):
    block_total = lax.axis_size("blk")
    copies = lax.axis_size("rep")
    planes = block_total // PLANE
    core = lax.rem(lax.axis_index("blk"), 2)
    share_rows, width = out_grad.shape
    side = tiles.shape[-1]
    tiles_side = share_rows // side * copies
    member = PLANE * copies
    in_plane = [[p * member + m for m in range(member)] for p in range(planes)]
    over_planes = [[p * PLANE + q for p in range(planes)] for q in range(PLANE)]

    sent = opening(features, aggregated, out_grad, w_neigh, copies, side)
    arrived = exchange(sent.reshape(member, *sent.shape[2:]), BOTH, in_plane)
    own = arrived[:, :-2].reshape(PLANE, tiles_side, *sent.shape[3:])

    onward = [
        (b, (b + PLANE) % block_total if b % 2 == 0 else (b - PLANE) % block_total)
        for b in range(block_total)
    ]
    partner = [(b, b ^ 1) for b in range(block_total)]
    near = jnp.where(core == 0, own[:HALF], own[HALF:])
    other = jnp.where(core == 0, own[HALF:], own[:HALF])
    steps = planes // 2
    def source(step, flip, swap):
        def of(block, m):
            core = lax.rem(block, 2)
            core = 1 - core if swap else core
            away = jnp.where(core == 0, planes - step, step)
            plane = lax.rem(block // PLANE + away, planes)
            return plane * PLANE + (1 - core if flip else core) * HALF + m

        return of

    codes = slot_codes(tile_rows, tile_cols, tile_counts, tiles_side)

    def summed_on(total, *work):
        pieces = [p for p, *_ in work]
        return spread_over(pieces, [source(*w[1:]) for w in work], codes, tiles, total)

    scale = (share_rows * block_total * copies) ** (-0.5)
    part = plane_sum(arrived, planes)
    nears, others, swaps = [near], [other], [[]]
    total, waiting = None, []

    part = exchange(part, "blk", over_planes)
    for step in range(steps):
        near, other = nears[-1], others[-1]
        if step == 2:
            near, codes = lax.optimization_barrier((near, codes))
        if step == 2:
            near, part = lax.optimization_barrier((near, part))
            whole = exchange(summed(part, member, scale), BOTH, in_plane)
        nears[-1] = near
        nears.append(lax.ppermute(near, "blk", onward))
        if step < steps - 1:
            others.append(lax.ppermute(other, "blk", onward))
        waiting += [(near, step, False, False), (other, step, True, False)]
        if step == steps - 1:
            total = summed_on(None, *waiting)
            waiting = []
        if step > 0:
            waiting += [
                (lax.ppermute(near, "blk", partner), step, False, True),
                (lax.ppermute(other, "blk", partner), step, True, True),
            ]
    final, total = lax.optimization_barrier((nears[-1], total))
    last = (lax.ppermute(final, "blk", partner), steps, False, True)
    spread = summed_on(total, *waiting, (final, steps, False, False), last)
    spread, whole = lax.optimization_barrier((spread, whole))
    parts = exchange(spread.reshape(copies, -1, *spread.shape[1:]), "rep")
    return result(parts, whole, out_grad, w_self)


def solution(mesh):
    placed = (
        P(("blk", "rep"), None),
        P(("blk", "rep"), None),
        P(("blk", "rep"), None),
        P(),
        P(),
        P("blk", None, None, None, None),
        P("blk", None, None),
        P("blk", None, None),
        P("blk", None),
    )
    return jax.shard_map(
        on_device,
        mesh=mesh,
        in_specs=placed,
        out_specs=(P(("blk", "rep"), None), P(), P()),
        check_vma=False,
    )
```

time: 229 us -> 85.4 us (0.37)
  waiting for transfers between devices: 156 us -> 24 us
  other arithmetic: 13.7 us -> 0.04 us
  blocking collectives: 0 us -> 11.9 us
  Pallas kernels: 0 us -> 9.87 us
  starting transfers between devices: 40.1 us -> 31.8 us
  matrix products: 7.95 us -> 0 us
    all_to_all x7 -> x3, waiting for transfers between devices: 156 us -> 15.3 us  [exchange(): return lax.all_to_all(x, axes, 0, 0, axis_index_groups=groups, tiled=True)]
    all_to_all x7 -> x3, starting transfers between devices: 40.1 us -> 20.2 us  [exchange(): return lax.all_to_all(x, axes, 0, 0, axis_index_groups=groups, tiled=True)]
    all_to_all x0 -> x1, blocking collectives: none -> 11.9 us  [exchange(): return lax.all_to_all(x, axes, 0, 0, axis_index_groups=groups, tiled=True)]
    ppermute x0 -> x14, starting transfers between devices: none -> 11.6 us  [the longest x3 4.49 us: on_device(): others.append(lax.ppermute(other, 'blk', onward))]
    pallas_call x0 -> x7, Pallas kernels: none -> 9.87 us  [the longest x2 4.85 us: spread_over(): pl.pallas_call(functools.partial(spread_kernel, sources, resumed), out_sh...]
    scatter-add x1 -> x0, other arithmetic: 9.65 us -> none  [on_device(): accumulated.at[target_rows].add(products.reshape(-1, side, width))]
    ppermute x0 -> x14, waiting for transfers between devices: none -> 8.68 us  [the longest x4 7.18 us: on_device(): nears.append(lax.ppermute(near, 'blk', onward))]
    dot_general x5 -> x0, matrix products: 7.95 us -> none  [the longest x1 4.56 us: on_device(): jnp.einsum('ikpq,ikqf->ikpf', chosen_tiles, fetched, preferred_element_ty...]
  transfers between devices with their start and end apart: 7 -> 17, of which waited for: 6 -> 4; matrix products, arithmetic and copies ran while one was open for 10% -> 0% of each run, Pallas kernels for 0% -> 8%
where the time goes in v2:
time: 85.4 us; the launch traced here: 83.7 us
  starting transfers between devices  31.8 us (37%)
  waiting for transfers between devices  24 us (28%)
  blocking collectives  11.9 us (14%)
  Pallas kernels  9.87 us (12%)
  local copies, waits for them, and re-layouts  5.42 us (6%)
    all_to_all x3, starting transfers between devices, exchange(): return lax.all_to_all(x, axes, 0, 0, axis_index_groups=groups, tiled=True)  20.2 us
    all_to_all x3, waiting for transfers between devices, exchange(): return lax.all_to_all(x, axes, 0, 0, axis_index_groups=groups, tiled=True)  15.3 us
    all_to_all x1, blocking collectives, exchange(): return lax.all_to_all(x, axes, 0, 0, axis_index_groups=groups, tiled=True)  11.9 us
    ppermute x4, waiting for transfers between devices, on_device(): nears.append(lax.ppermute(near, 'blk', onward))  7.18 us
    unnamed x12, local copies, waits for them, and re-layouts  5.42 us
    pallas_call x2, Pallas kernels, spread_over(): pl.pallas_call(functools.partial(spread_kernel, sources, resumed), out_sh...  4.85 us
    ppermute x3, starting transfers between devices, on_device(): others.append(lax.ppermute(other, 'blk', onward))  4.49 us
    ppermute x4, starting transfers between devices, on_device(): nears.append(lax.ppermute(near, 'blk', onward))  3.25 us
  transfers between devices with their start and end apart: 17, of which 4 were waited for; matrix products, arithmetic and copies ran while one was open for 0% of the time, Pallas kernels for 8%

profile of v2, /device:TPU:8, one launch (start us, length us, event | category | flops | bytes accessed | tf_op | source)
XLA Modules:
  0.0 83.7 jit_solution(1624017587802206772)
XLA Ops:
  0.6 2.4 %opening.1 = bf16[4,8,4,32,128]{4,3,2,1,0:T(8,128)(2,1)} custom-call(bf16[256,256]{1,0:T(8,128)(2,1)} %features.1, bf16[256,256]{1,0:T(8,128)(2,1)} %aggregated.1, bf16[256,256]{1,0:T(8,128)(2,1)} %grad.3, bf16[256,256]{1,0:T(8,128)(2,1)} %weight.2), custom_call_target="tpu_custom_call" | custom-call | tf_op jit(solution)/shard_map/opening/pallas_call | solution.py:59
  3.0 7.5 %all-to-all-start = ((bf16[32,4,32,128]{3,2,1,0:T(8,128)(2,1)}), bf16[32,4,32,128]{3,2,1,0:T(8,128)(2,1)S(1)}, u32[]{:S(2)}, u32[]{:S(2)}) async-start(bf16[32,4,32,128]{3,2,1,0:T(8,128)(2,1)} %bitcast.13), calls=%async_computation | async-start | bytes 2097152 | tf_op jit(solution)/shard_map/all_to_all | solution.py:22
  10.6 15.3 %all-to-all-done.arrived = bf16[32,4,32,128]{3,2,1,0:T(8,128)(2,1)S(1)} async-done(((bf16[32,4,32,128]{3,2,1,0:T(8,128)(2,1)}), bf16[32,4,32,128]{3,2,1,0:T(8,128)(2,1)S(1)}, u32[]{:S(2)}, u32[]{:S(2)}) %all-to-all-start) | async-done | bytes 1048608 | tf_op jit(solution)/shard_map/all_to_all | solution.py:22
  25.9 2.0 %collective-permute-start.4 = (bf16[2,16,32,128]{3,2,1,0:T(8,128)(2,1)S(1)}, bf16[2,16,32,128]{3,2,1,0:T(8,128)(2,1)S(1)}, u32[]{:S(2)}, u32[]{:S(2)}) collective-permute-start(bf16[2,16,32,128]{3,2,1,0:T(8,128)(2,1)S(1)} %bitcast.7), channel_id=1, source_target_pairs={{0,32},{8,232},{16,48},{24,248},{32,64},{40,8},{48,80},{56,24},{64... | collective-permute-start | bytes 786440 | tf_op jit(solution)/shard_map/ppermute | solution.py:256
  27.9 1.9 %collective-permute-start = (bf16[2,16,32,128]{3,2,1,0:T(8,128)(2,1)S(1)}, bf16[2,16,32,128]{3,2,1,0:T(8,128)(2,1)S(1)}, u32[]{:S(2)}, u32[]{:S(2)}) collective-permute-start(bf16[2,16,32,128]{3,2,1,0:T(8,128)(2,1)S(1)} %bitcast.9), channel_id=1, source_target_pairs={{0,32},{8,232},{16,48},{24,248},{32,64},{40,8},{48,80},{56,24},{64... | collective-permute-start | bytes 786440 | tf_op jit(solution)/shard_map/ppermute | solution.py:254
  29.8 0.7 plane_sum.1
  30.6 6.7 %all-to-all-start.1 = ((f32[8,32,128]{2,1,0:T(8,128)}), f32[8,32,128]{2,1,0:T(8,128)S(1)}, u32[]{:S(2)}, u32[]{:S(2)}) async-start(f32[8,32,128]{2,1,0:T(8,128)} %plane_sum.1), calls=%async_computation.1 | async-start | bytes 262144 | tf_op jit(solution)/shard_map/all_to_all | solution.py:22
  37.2 0.0 collective-permute-done.4.refs_3_
  37.2 2.0 %collective-permute-start.5 = (bf16[2,16,32,128]{3,2,1,0:T(8,128)(2,1)S(1)}, bf16[2,16,32,128]{3,2,1,0:T(8,128)(2,1)S(1)}, u32[]{:S(2)}, u32[]{:S(2)}) collective-permute-start(bf16[2,16,32,128]{3,2,1,0:T(8,128)(2,1)S(1)} %collective-permute-done.4.refs_3_), channel_id=1, source_target_pairs={{0,32},{8,232},{16,48},{24,248},{32,64},{40,8},{48,80},{56,24},{64... | collective-permute-start | bytes 786440 | tf_op jit(solution)/shard_map/ppermute | solution.py:256
  39.3 0.2 collective-permute-start.10
  39.5 0.0 collective-permute-done.refs_2_
  39.5 1.2 %collective-permute-start.1 = (bf16[2,16,32,128]{3,2,1,0:T(8,128)(2,1)S(1)}, bf16[2,16,32,128]{3,2,1,0:T(8,128)(2,1)S(1)}, u32[]{:S(2)}, u32[]{:S(2)}) collective-permute-start(bf16[2,16,32,128]{3,2,1,0:T(8,128)(2,1)S(1)} %collective-permute-done.refs_2_), channel_id=1, source_target_pairs={{0,32},{8,232},{16,48},{24,248},{32,64},{40,8},{48,80},{56,24},{64... | collective-permute-start | bytes 786440 | tf_op jit(solution)/shard_map/ppermute | solution.py:254
  40.7 0.7 copy-done.3
  41.4 0.7 copy-done.4
  42.1 0.7 copy-done.5
  42.8 7.0 %collective-permute-done.1.refs_6_ = bf16[2,16,32,128]{3,2,1,0:T(8,128)(2,1)S(1)} collective-permute-done((bf16[2,16,32,128]{3,2,1,0:T(8,128)(2,1)S(1)}, bf16[2,16,32,128]{3,2,1,0:T(8,128)(2,1)S(1)}, u32[]{:S(2)}, u32[]{:S(2)}) %collective-permute-start.1) | collective-permute-done | bytes 262176 | tf_op jit(solution)/shard_map/ppermute | solution.py:254
  49.8 0.0 all-to-all-done.1.parts
  49.8 0.0 collective-permute-start.2
  49.8 0.2 collective-permute-start.9
  50.0 0.0 collective-permute-done.5.refs_7_
  50.0 0.5 collective-permute-start.6
  50.5 2.8 %collective-permute-start.11 = (bf16[2,16,32,128]{3,2,1,0:T(8,128)(2,1)S(1)}, bf16[2,16,32,128]{3,2,1,0:T(8,128)(2,1)S(1)}, u32[]{:S(2)}, u32[]{:S(2)}) collective-permute-start(bf16[2,16,32,128]{3,2,1,0:T(8,128)(2,1)S(1)} %collective-permute-done.1.refs_6_), channel_id=1, source_target_pairs={{0,8},{8,0},{16,24},{24,16},{32,40},{40,32},{48,56},{56,48},{64,72... | collective-permute-start | bytes 786440 | tf_op jit(solution)/shard_map/ppermute | solution.py:263
  53.2 0.0 collective-permute-done.10.refs_5_
  53.3 0.0 collective-permute-start.12
  53.3 0.9 %summed.1 = f32[32,32,128]{2,1,0:T(8,128)} custom-call(f32[8,32,128]{2,1,0:T(8,128)S(1)} %all-to-all-done.1.parts), custom_call_target="tpu_custom_call" | custom-call | tf_op jit(solution)/shard_map/summed/pallas_call | solution.py:115
  54.1 6.0 %all-to-all-start.2 = ((f32[32,32,128]{2,1,0:T(8,128)}), f32[32,32,128]{2,1,0:T(8,128)S(1)}, u32[]{:S(2)}, u32[]{:S(2)}) async-start(f32[32,32,128]{2,1,0:T(8,128)} %summed.1), calls=%async_computation.2 | async-start | bytes 1048576 | tf_op jit(solution)/shard_map/all_to_all | solution.py:22
  60.1 0.0 collective-permute-done.2.refs_10_
  60.1 0.1 collective-permute-start.8
  60.2 0.0 collective-permute-done.9.refs_4_
  60.2 0.2 collective-permute-start.3
  60.4 0.0 collective-permute-done.6.refs_11_
  60.4 0.4 collective-permute-start.7
  60.8 0.0 collective-permute-done.11.refs_8_
  60.8 0.0 collective-permute-done.12.refs_9_
  60.8 3.4 %copy-done = bf16[1,32,8,128,128]{4,3,2,1,0:T(8,128)(2,1)S(1)} copy-done((bf16[1,32,8,128,128]{4,3,2,1,0:T(8,128)(2,1)S(1)}, bf16[1,32,8,128,128]{4,3,2,1,0:T(8,128)(2,1)}, u32[]{:S(2)}) %copy-start) | copy-done | bytes 8388632
  64.2 3.4 %spread.1.refs_4_ = f32[16,32,128]{2,1,0:T(8,128)S(1)} custom-call(s32[8,32]{1,0:T(8,128)S(1)} %codes.1, bf16[1,32,8,128,128]{4,3,2,1,0:T(8,128)(2,1)S(1)} %copy-done, bf16[2,16,32,128]{3,2,1,0:T(8,128)(2,1)S(1)} %bitcast.10, bf16[2,16,32,128]{3,2,1,0:T(8,128)(2,1)S(1)} %bitcast.8, bf16[2,16,32,128]{3,2,1,0:T(8,128)(2,1)S(1)} %collective-permute-done.refs_2_, ...), custom_call_target="tpu_custom_call" | custom-call | flops 20000000000 | tf_op jit(solution)/shard_map/spread/pallas_call | solution.py:186
  67.6 0.0 copy-start.1
  67.6 0.0 copy-start.2
  67.6 0.2 collective-permute-done.8.refs_2_
  67.8 0.1 collective-permute-start.13
  67.8 0.0 collective-permute-done.3.refs_0_
  67.8 0.0 collective-permute-done.7.refs_1_
  67.8 1.5 %collective-permute-done.13.refs_3_ = bf16[2,16,32,128]{3,2,1,0:T(8,128)(2,1)S(1)} collective-permute-done((bf16[2,16,32,128]{3,2,1,0:T(8,128)(2,1)S(1)}, bf16[2,16,32,128]{3,2,1,0:T(8,128)(2,1)S(1)}, u32[]{:S(2)}, u32[]{:S(2)}) %collective-permute-start.13) | collective-permute-done | bytes 262176 | tf_op jit(solution)/shard_map/ppermute | solution.py:267
  69.3 1.5 %spread_on.1 = f32[16,32,128]{2,1,0:T(8,128)S(1)} custom-call(s32[8,32]{1,0:T(8,128)S(1)} %codes.1, bf16[1,32,8,128,128]{4,3,2,1,0:T(8,128)(2,1)S(1)} %copy-done, bf16[2,16,32,128]{3,2,1,0:T(8,128)(2,1)S(1)} %collective-permute-done.3.refs_0_, bf16[2,16,32,128]{3,2,1,0:T(8,128)(2,1)S(1)} %collective-permute-done.7.refs_1_, ...), custom_call_target="tpu_custom_call" | custom-call | flops 1 | tf_op jit(solution)/shard_map/spread_on/pallas_call | solution.py:186
  70.8 0.0 all-to-all-done.2.whole
  70.8 11.9 %all_to_all.20.parts = f32[8,2,32,128]{3,2,1,0:T(8,128)S(1)} all-to-all(f32[8,2,32,128]{3,2,1,0:T(8,128)S(1)} %bitcast.6), channel_id=1, replica_groups=mesh['blk'=32,'rep'=8] {'rep'}, dimensions={0} | all-to-all | bytes 524288 | tf_op jit(solution)/shard_map/all_to_all | solution.py:22
  82.7 0.0 copy-done.1
  82.7 1.0 %result.1 = (f32[256,256]{1,0:T(8,128)}, f32[256,256]{1,0:T(8,128)}, f32[256,256]{1,0:T(8,128)}) custom-call(f32[8,2,32,128]{3,2,1,0:T(8,128)S(1)} %all_to_all.20.parts, f32[32,32,128]{2,1,0:T(8,128)S(1)} %all-to-all-done.2.whole, bf16[256,256]{1,0:T(8,128)(2,1)S(1)} %copy-done.1, bf16[256,256]{1,0:T(8,128)(2,1)S(1)} %copy-done.2), custom_call_target="tpu_custom_call" | custom-call | tf_op jit(solution)/shard_map/result/pallas_call | solution.py:142
  (7 shorter events, 0.1 us)
Async XLA Ops:
  3.0 22.8 %all-to-all-start = ((bf16[32,4,32,128]{3,2,1,0:T(8,128)(2,1)}), bf16[32,4,32,128]{3,2,1,0:T(8,128)(2,1)S(1)}, u32[]{:S(2)}, u32[]{:S(2)}) async-start(bf16[32,4,32,128]{3,2,1,0:T(8,128)(2,1)} %bitcast.13), calls=%async_computation | async-start | bytes 2097152 | tf_op jit(solution)/shard_map/all_to_all | solution.py:22
  25.9 11.3 %collective-permute-start.4 = (bf16[2,16,32,128]{3,2,1,0:T(8,128)(2,1)S(1)}, bf16[2,16,32,128]{3,2,1,0:T(8,128)(2,1)S(1)}, u32[]{:S(2)}, u32[]{:S(2)}) collective-permute-start(bf16[2,16,32,128]{3,2,1,0:T(8,128)(2,1)S(1)} %bitcast.7), channel_id=1, source_target_pairs={{0,32},{8,232},{16,48},{24,248},{32,64},{40,8},{48,80},{56,24},{64... | collective-permute-start | bytes 786440 | tf_op jit(solution)/shard_map/ppermute | solution.py:256
  27.9 11.6 %collective-permute-start = (bf16[2,16,32,128]{3,2,1,0:T(8,128)(2,1)S(1)}, bf16[2,16,32,128]{3,2,1,0:T(8,128)(2,1)S(1)}, u32[]{:S(2)}, u32[]{:S(2)}) collective-permute-start(bf16[2,16,32,128]{3,2,1,0:T(8,128)(2,1)S(1)} %bitcast.9), channel_id=1, source_target_pairs={{0,32},{8,232},{16,48},{24,248},{32,64},{40,8},{48,80},{56,24},{64... | collective-permute-start | bytes 786440 | tf_op jit(solution)/shard_map/ppermute | solution.py:254
  30.6 19.2 %all-to-all-start.1 = ((f32[8,32,128]{2,1,0:T(8,128)}), f32[8,32,128]{2,1,0:T(8,128)S(1)}, u32[]{:S(2)}, u32[]{:S(2)}) async-start(f32[8,32,128]{2,1,0:T(8,128)} %plane_sum.1), calls=%async_computation.1 | async-start | bytes 262144 | tf_op jit(solution)/shard_map/all_to_all | solution.py:22
  37.2 12.7 %collective-permute-start.5 = (bf16[2,16,32,128]{3,2,1,0:T(8,128)(2,1)S(1)}, bf16[2,16,32,128]{3,2,1,0:T(8,128)(2,1)S(1)}, u32[]{:S(2)}, u32[]{:S(2)}) collective-permute-start(bf16[2,16,32,128]{3,2,1,0:T(8,128)(2,1)S(1)} %collective-permute-done.4.refs_3_), channel_id=1, source_target_pairs={{0,32},{8,232},{16,48},{24,248},{32,64},{40,8},{48,80},{56,24},{64... | collective-permute-start | bytes 786440 | tf_op jit(solution)/shard_map/ppermute | solution.py:256
  39.3 14.0 %collective-permute-start.10 = (bf16[2,16,32,128]{3,2,1,0:T(8,128)(2,1)S(1)}, bf16[2,16,32,128]{3,2,1,0:T(8,128)(2,1)S(1)}, u32[]{:S(2)}, u32[]{:S(2)}) collective-permute-start(bf16[2,16,32,128]{3,2,1,0:T(8,128)(2,1)S(1)} %collective-permute-done.4.refs_3_), channel_id=1, source_target_pairs={{0,8},{8,0},{16,24},{24,16},{32,40},{40,32},{48,56},{56,48},{64,72... | collective-permute-start | bytes 786440 | tf_op jit(solution)/shard_map/ppermute | solution.py:264
  39.5 10.3 %collective-permute-start.1 = (bf16[2,16,32,128]{3,2,1,0:T(8,128)(2,1)S(1)}, bf16[2,16,32,128]{3,2,1,0:T(8,128)(2,1)S(1)}, u32[]{:S(2)}, u32[]{:S(2)}) collective-permute-start(bf16[2,16,32,128]{3,2,1,0:T(8,128)(2,1)S(1)} %collective-permute-done.refs_2_), channel_id=1, source_target_pairs={{0,32},{8,232},{16,48},{24,248},{32,64},{40,8},{48,80},{56,24},{64... | collective-permute-start | bytes 786440 | tf_op jit(solution)/shard_map/ppermute | solution.py:254
  40.7 0.7 copy-start.3
  41.4 0.7 copy-start.4
  42.1 0.7 copy-start.5
  49.8 10.3 %collective-permute-start.2 = (bf16[2,16,32,128]{3,2,1,0:T(8,128)(2,1)S(1)}, bf16[2,16,32,128]{3,2,1,0:T(8,128)(2,1)S(1)}, u32[]{:S(2)}, u32[]{:S(2)}) collective-permute-start(bf16[2,16,32,128]{3,2,1,0:T(8,128)(2,1)S(1)} %collective-permute-done.1.refs_6_), channel_id=1, source_target_pairs={{0,32},{8,232},{16,48},{24,248},{32,64},{40,8},{48,80},{56,24},{64... | collective-permute-start | bytes 786440 | tf_op jit(solution)/shard_map/ppermute | solution.py:254
  49.8 10.4 %collective-permute-start.9 = (bf16[2,16,32,128]{3,2,1,0:T(8,128)(2,1)S(1)}, bf16[2,16,32,128]{3,2,1,0:T(8,128)(2,1)S(1)}, u32[]{:S(2)}, u32[]{:S(2)}) collective-permute-start(bf16[2,16,32,128]{3,2,1,0:T(8,128)(2,1)S(1)} %collective-permute-done.refs_2_), channel_id=1, source_target_pairs={{0,8},{8,0},{16,24},{24,16},{32,40},{40,32},{48,56},{56,48},{64,72... | collective-permute-start | bytes 786440 | tf_op jit(solution)/shard_map/ppermute | solution.py:263
  50.0 10.5 %collective-permute-start.6 = (bf16[2,16,32,128]{3,2,1,0:T(8,128)(2,1)S(1)}, bf16[2,16,32,128]{3,2,1,0:T(8,128)(2,1)S(1)}, u32[]{:S(2)}, u32[]{:S(2)}) collective-permute-start(bf16[2,16,32,128]{3,2,1,0:T(8,128)(2,1)S(1)} %collective-permute-done.5.refs_7_), channel_id=1, source_target_pairs={{0,32},{8,232},{16,48},{24,248},{32,64},{40,8},{48,80},{56,24},{64... | collective-permute-start | bytes 786440 | tf_op jit(solution)/shard_map/ppermute | solution.py:256
  50.5 10.4 %collective-permute-start.11 = (bf16[2,16,32,128]{3,2,1,0:T(8,128)(2,1)S(1)}, bf16[2,16,32,128]{3,2,1,0:T(8,128)(2,1)S(1)}, u32[]{:S(2)}, u32[]{:S(2)}) collective-permute-start(bf16[2,16,32,128]{3,2,1,0:T(8,128)(2,1)S(1)} %collective-permute-done.1.refs_6_), channel_id=1, source_target_pairs={{0,8},{8,0},{16,24},{24,16},{32,40},{40,32},{48,56},{56,48},{64,72... | collective-permute-start | bytes 786440 | tf_op jit(solution)/shard_map/ppermute | solution.py:263
  53.3 7.6 %collective-permute-start.12 = (bf16[2,16,32,128]{3,2,1,0:T(8,128)(2,1)S(1)}, bf16[2,16,32,128]{3,2,1,0:T(8,128)(2,1)}, u32[]{:S(2)}, u32[]{:S(2)}) collective-permute-start(bf16[2,16,32,128]{3,2,1,0:T(8,128)(2,1)S(1)} %collective-permute-done.5.refs_7_), channel_id=1, source_target_pairs={{0,8},{8,0},{16,24},{24,16},{32,40},{40,32},{48,56},{56,48},{64,72... | collective-permute-start | bytes 786440 | tf_op jit(solution)/shard_map/ppermute | solution.py:264
  54.1 16.7 %all-to-all-start.2 = ((f32[32,32,128]{2,1,0:T(8,128)}), f32[32,32,128]{2,1,0:T(8,128)S(1)}, u32[]{:S(2)}, u32[]{:S(2)}) async-start(f32[32,32,128]{2,1,0:T(8,128)} %summed.1), calls=%async_computation.2 | async-start | bytes 1048576 | tf_op jit(solution)/shard_map/all_to_all | solution.py:22
  60.1 7.7 %collective-permute-start.8 = (bf16[2,16,32,128]{3,2,1,0:T(8,128)(2,1)S(1)}, bf16[2,16,32,128]{3,2,1,0:T(8,128)(2,1)S(1)}, u32[]{:S(2)}, u32[]{:S(2)}) collective-permute-start(bf16[2,16,32,128]{3,2,1,0:T(8,128)(2,1)S(1)} %collective-permute-done.2.refs_10_), channel_id=1, source_target_pairs={{0,32},{8,232},{16,48},{24,248},{32,64},{40,8},{48,80},{56,24},{64... | collective-permute-start | bytes 786440 | tf_op jit(solution)/shard_map/ppermute | solution.py:254
  60.2 7.6 %collective-permute-start.3 = (bf16[2,16,32,128]{3,2,1,0:T(8,128)(2,1)S(1)}, bf16[2,16,32,128]{3,2,1,0:T(8,128)(2,1)S(1)}, u32[]{:S(2)}, u32[]{:S(2)}) collective-permute-start(bf16[2,16,32,128]{3,2,1,0:T(8,128)(2,1)S(1)} %collective-permute-done.2.refs_10_), channel_id=1, source_target_pairs={{0,8},{8,0},{16,24},{24,16},{32,40},{40,32},{48,56},{56,48},{64,72... | collective-permute-start | bytes 786440 | tf_op jit(solution)/shard_map/ppermute | solution.py:263
  60.4 7.4 %collective-permute-start.7 = (bf16[2,16,32,128]{3,2,1,0:T(8,128)(2,1)S(1)}, bf16[2,16,32,128]{3,2,1,0:T(8,128)(2,1)S(1)}, u32[]{:S(2)}, u32[]{:S(2)}) collective-permute-start(bf16[2,16,32,128]{3,2,1,0:T(8,128)(2,1)S(1)} %collective-permute-done.6.refs_11_), channel_id=1, source_target_pairs={{0,8},{8,0},{16,24},{24,16},{32,40},{40,32},{48,56},{56,48},{64,72... | collective-permute-start | bytes 786440 | tf_op jit(solution)/shard_map/ppermute | solution.py:264
  60.8 3.4 %copy-start = (bf16[1,32,8,128,128]{4,3,2,1,0:T(8,128)(2,1)S(1)}, bf16[1,32,8,128,128]{4,3,2,1,0:T(8,128)(2,1)}, u32[]{:S(2)}) copy-start(bf16[1,32,8,128,128]{4,3,2,1,0:T(8,128)(2,1)} %tiles.3) | copy-start | bytes 25165828
  67.6 15.2 %copy-start.1 = (bf16[256,256]{1,0:T(8,128)(2,1)S(1)}, bf16[256,256]{1,0:T(8,128)(2,1)}, u32[]{:S(2)}) copy-start(bf16[256,256]{1,0:T(8,128)(2,1)} %grad.3) | copy-start | bytes 393220
  67.6 15.2 %copy-start.2 = (bf16[256,256]{1,0:T(8,128)(2,1)S(1)}, bf16[256,256]{1,0:T(8,128)(2,1)}, u32[]{:S(2)}) copy-start(bf16[256,256]{1,0:T(8,128)(2,1)} %weight.3) | copy-start | bytes 393220
  67.8 1.5 %collective-permute-start.13 = (bf16[2,16,32,128]{3,2,1,0:T(8,128)(2,1)S(1)}, bf16[2,16,32,128]{3,2,1,0:T(8,128)(2,1)S(1)}, u32[]{:S(2)}, u32[]{:S(2)}) collective-permute-start(bf16[2,16,32,128]{3,2,1,0:T(8,128)(2,1)S(1)} %collective-permute-done.8.refs_2_), channel_id=1, source_target_pairs={{0,8},{8,0},{16,24},{24,16},{32,40},{40,32},{48,56},{56,48},{64,72... | collective-permute-start | bytes 786440 | tf_op jit(solution)/shard_map/ppermute | solution.py:267

commit v3 on v2

v3 whole, which is shorter than its diff:
```python
import functools

import jax
import jax.numpy as jnp
from jax import lax
from jax.experimental import pallas as pl
from jax.experimental.pallas import tpu as pltpu
from jax.sharding import PartitionSpec as P

PLANE = 4
HALF = PLANE // 2
LOW = 2
MEMBERS = 32
RUN = 4
TOGETHER = 4
BOTH = ("blk", "rep")
AS_SHORT = pl.CostEstimate(flops=1, bytes_accessed=0, transcendentals=0)
AS_LONG = pl.CostEstimate(flops=20000000000, bytes_accessed=0, transcendentals=0)
VMEM = pl.BlockSpec(memory_space=pltpu.VMEM)
SMEM = pl.BlockSpec(memory_space=pltpu.SMEM)
ROOM = pltpu.CompilerParams(vmem_limit_bytes=16 * 2**20)
BY_LAST = (((1,), (1,)), ((), ()))


def exchange(x, axes, groups=None):
    return lax.all_to_all(x, axes, 0, 0, axis_index_groups=groups, tiled=True)


def opening_kernel(features, aggregated, grad, weight, out):
    share = lax.dot_general(
        weight[...], grad[...], BY_LAST, preferred_element_type=jnp.float32
    ).astype(out.dtype)
    members, held, width, side = out.shape
    tiles = held - 2
    for p in range(members):
        s = slice_of(p)
        for t in range(tiles):
            out[p, t] = share[s * width : (s + 1) * width, t * side : (t + 1) * side]
    depth = width // 2
    half = members // 2
    for which, source in enumerate((features, aggregated)):
        terms = lax.dot_general(
            source[...], grad[...], (((0,), (0,)), ((), ())), preferred_element_type=jnp.float32
        )
        upper = terms.astype(out.dtype)
        lower = (terms - upper.astype(jnp.float32)).astype(out.dtype)
        for p in range(half):
            here = slice(p * depth, (p + 1) * depth)
            for place, part in ((tiles, upper), (tiles + 1, lower)):
                out[which * half + p, place, :depth] = part[here, :side]
                out[which * half + p, place, depth:] = part[here, side:]


def slice_of(p):
    return p // (HALF * LOW) % (MEMBERS // (PLANE * LOW)) * LOW + p % LOW


def opening(features, aggregated, out_grad, w_neigh, copies, side):
    rows, width = out_grad.shape
    shape = (PLANE * copies, rows // side + 2, width // copies, side)
    return pl.pallas_call(
        opening_kernel,
        out_shape=jax.ShapeDtypeStruct(shape, jnp.bfloat16),
        compiler_params=pltpu.CompilerParams(vmem_limit_bytes=60 * 2**20),
        name="opening",
    )(features, aggregated, out_grad, w_neigh)


def plane_sum_kernel(arrived, out):
    tiles = arrived.shape[1] - 2
    total = jnp.zeros(out.shape[1:], jnp.float32)
    for m in range(arrived.shape[0]):
        total = total + (
            arrived[m, tiles].astype(jnp.float32) + arrived[m, tiles + 1].astype(jnp.float32)
        )
    for copy in range(out.shape[0]):
        out[copy] = total


def plane_sum(arrived, again):
    return pl.pallas_call(
        plane_sum_kernel,
        out_shape=jax.ShapeDtypeStruct((again, *arrived.shape[2:]), jnp.float32),
        compiler_params=ROOM,
        name="plane_sum",
    )(arrived)


def codes_kernel(tiles_side, rows, cols, counts, out):
    slot = lax.broadcasted_iota(jnp.int32, out.shape, 0)
    code = rows[0] * tiles_side + cols[0]
    out[...] = jnp.where(slot < counts[...], code, tiles_side * tiles_side)


def slot_codes(tile_rows, tile_cols, tile_counts, tiles_side):
    _, blocks, slots = tile_rows.shape
    return pl.pallas_call(
        functools.partial(codes_kernel, tiles_side),
        out_shape=jax.ShapeDtypeStruct((slots, blocks), jnp.int32),
        cost_estimate=AS_LONG,
        compiler_params=ROOM,
        name="codes",
    )(tile_rows.swapaxes(1, 2), tile_cols.swapaxes(1, 2), tile_counts)


def summed_kernel(scale, parts, out):
    total = parts[0]
    for p in range(1, parts.shape[0]):
        total = total + parts[p]
    if scale != 1.0:
        total = total * scale
    for copy in range(out.shape[0]):
        out[copy] = total


def summed(parts, again, scale):
    return pl.pallas_call(
        functools.partial(summed_kernel, scale),
        out_shape=jax.ShapeDtypeStruct((again, *parts.shape[1:]), parts.dtype),
        compiler_params=ROOM,
        name="summed",
    )(parts)


def result_kernel(parts, whole, grad, weight, out, self_out, neigh_out):
    straight = lax.dot_general(
        grad[...], weight[...], BY_LAST, preferred_element_type=jnp.float32
    )
    slices, tiles, width, side = parts.shape
    for t in range(tiles):
        rows = slice(t * side, (t + 1) * side)
        spread = parts[:, t].reshape(slices * width, side)
        out[rows] = straight[rows] + spread.T
    members, depth = whole.shape[0], whole.shape[1] // 2
    for m in range(members):
        target = (self_out, neigh_out)[2 * m // members]
        top = m % (members // 2) * depth
        target[top : top + depth, :side] = whole[m, :depth]
        target[top : top + depth, side:] = whole[m, depth:]


def result(parts, whole, out_grad, w_self):
    rows, width = out_grad.shape
    return pl.pallas_call(
        result_kernel,
        out_shape=[
            jax.ShapeDtypeStruct((rows, width), jnp.float32),
            jax.ShapeDtypeStruct((width, width), jnp.float32),
            jax.ShapeDtypeStruct((width, width), jnp.float32),
        ],
        compiler_params=ROOM,
        name="result",
    )(parts, whole, out_grad, w_self)


def add_products(acc, codes, tiles, piece, source, m, shift):
    slots = tiles.shape[1]
    _, width, side = acc.shape
    code = [codes[k, source] for k in range(slots)]
    row = [lax.shift_right_logical(c, shift) for c in code]
    col = [lax.bitwise_and(c, (1 << shift) - 1) for c in code]
    at = [c + lax.bitwise_and(c, -RUN) + RUN * m for c in col]
    for k in range(0, slots, 2):
        pair = jnp.concatenate([piece[at[k]], piece[at[k + 1]]], axis=0)
        both = tiles[source, k : k + 2].reshape(2 * side, side)
        product = lax.dot_general(pair, both, BY_LAST, preferred_element_type=jnp.float32)
        acc[row[k]] = acc[row[k]] + product[:width, :side]
        acc[row[k + 1]] = acc[row[k + 1]] + product[width:, side:]


def spread_kernel(sources, later, codes, tiles, *refs):
    pieces, (out, held, acc, sems) = refs[: len(sources)], refs[len(sources) :]
    tiles_side = out.shape[0]
    shift = tiles_side.bit_length() - 1
    block = lax.axis_index("blk")
    work = [(p, of(block, m), m) for p, of in zip(pieces, sources) for m in range(HALF)]
    rest = [of(block, m) for of in later for m in range(HALF)]
    copies = [
        pltpu.make_async_copy(tiles.at[0, source], held.at[source], sems.at[n])
        for n, source in enumerate([source for _, source, _ in work] + rest)
    ]
    for copy in copies:
        copy.start()
    acc[...] = jnp.zeros_like(acc)
    for n in range(0, len(work), TOGETHER):
        for copy in copies[n : n + TOGETHER]:
            copy.wait()
        for piece, source, m in work[n : n + TOGETHER]:
            add_products(acc, codes, held, piece, source, m, shift)
    for copy in copies[len(work) :]:
        copy.wait()
    out[...] = acc[:tiles_side]


def spread_over(pieces, sources, later, codes, tiles, tiles_side):
    _, width, side = pieces[0].shape
    shape = (tiles_side, width, side)
    return pl.pallas_call(
        functools.partial(spread_kernel, sources, later),
        out_shape=[
            jax.ShapeDtypeStruct(shape, jnp.float32),
            jax.ShapeDtypeStruct(tiles.shape[1:], tiles.dtype),
        ],
        in_specs=[SMEM, pl.BlockSpec(memory_space=pltpu.HBM)] + [VMEM] * len(pieces),
        out_specs=[VMEM, VMEM],
        scratch_shapes=[
            pltpu.VMEM((tiles_side + 1, width, side), jnp.float32),
            pltpu.SemaphoreType.DMA((tiles.shape[1],)),
        ],
        compiler_params=pltpu.CompilerParams(vmem_limit_bytes=40 * 2**20),
        cost_estimate=AS_LONG,
        name="spread",
    )(codes, tiles, *pieces)


def spread_on_kernel(sources, codes, tiles, begun, *refs):
    pieces, (out, acc) = refs[: len(sources)], refs[len(sources) :]
    tiles_side = out.shape[0]
    block = lax.axis_index("blk")
    acc[:tiles_side] = begun[...]
    acc[tiles_side] = jnp.zeros(out.shape[1:], jnp.float32)
    for piece, of in zip(pieces, sources):
        for m in range(HALF):
            source = of(block, m)
            add_products(acc, codes, tiles, piece, source, m, tiles_side.bit_length() - 1)
    out[...] = acc[:tiles_side]


def spread_on(pieces, sources, codes, tiles, begun):
    return pl.pallas_call(
        functools.partial(spread_on_kernel, sources),
        out_shape=jax.ShapeDtypeStruct(begun.shape, jnp.float32),
        in_specs=[SMEM] + [VMEM] * (2 + len(pieces)),
        out_specs=VMEM,
        scratch_shapes=[pltpu.VMEM((begun.shape[0] + 1, *begun.shape[1:]), jnp.float32)],
        compiler_params=ROOM,
        cost_estimate=AS_SHORT,
        name="spread_on",
    )(codes, tiles, begun, *pieces)


def on_device(
    features, aggregated, out_grad, w_self, w_neigh, tiles, tile_rows, tile_cols, tile_counts
):
    block_total = lax.axis_size("blk")
    copies = lax.axis_size("rep")
    planes = block_total // PLANE
    core = lax.rem(lax.axis_index("blk"), 2)
    share_rows, width = out_grad.shape
    side = tiles.shape[-1]
    tiles_side = share_rows // side * copies
    member = PLANE * copies
    in_plane = [
        [
            ((z * HALF + high) * HALF + c) * copies + x * LOW + low
            for c in range(HALF)
            for x in range(copies // LOW)
            for high in range(HALF)
            for low in range(LOW)
        ]
        for z in range(planes)
    ]
    over_planes = [[p * PLANE + q for p in range(planes)] for q in range(PLANE)]

    sent = opening(features, aggregated, out_grad, w_neigh, copies, side)
    arrived = exchange(sent, BOTH, in_plane)
    own = arrived[:, :-2].reshape(2, member, *sent.shape[2:])

    onward = [
        (b, (b + PLANE) % block_total if b % 2 == 0 else (b - PLANE) % block_total)
        for b in range(block_total)
    ]
    partner = [(b, b ^ 1) for b in range(block_total)]
    near = jnp.where(core == 0, own[0], own[1])
    other = jnp.where(core == 0, own[1], own[0])
    steps = planes // 2
    def source(step, flip, swap):
        def of(block, m):
            core = lax.rem(block, 2)
            core = 1 - core if swap else core
            away = jnp.where(core == 0, planes - step, step)
            plane = lax.rem(block // PLANE + away, planes)
            return plane * PLANE + m * HALF + (1 - core if flip else core)

        return of

    codes = slot_codes(tile_rows, tile_cols, tile_counts, tiles_side)

    scale = (share_rows * block_total * copies) ** (-0.5)
    part = plane_sum(arrived, planes)
    nears, others, swaps = [near], [other], [[]]
    part = exchange(part, "blk", over_planes)
    swaps = []
    for step in range(steps):
        near, other = nears[-1], others[-1]
        if step == 2:
            near, codes, part = lax.optimization_barrier((near, codes, part))
            whole = exchange(summed(part, member, scale), BOTH, in_plane)
        nears[-1] = near
        nears.append(lax.ppermute(near, "blk", onward))
        if step < steps - 1:
            others.append(lax.ppermute(other, "blk", onward))
        if step > 0:
            swaps += [
                (lax.ppermute(near, "blk", partner), source(step, False, True)),
                (lax.ppermute(other, "blk", partner), source(step, True, True)),
            ]
    early = [(p, source(s, False, False)) for s, p in enumerate(nears[:-1])]
    early += [(p, source(s, True, False)) for s, p in enumerate(others)]
    later = [of for _, of in swaps] + [source(steps, False, swap) for swap in (False, True)]
    total, held = spread_over(*zip(*early), later, codes, tiles, tiles_side)
    final, total = lax.optimization_barrier((nears[-1], total))
    late = [p for p, _ in swaps] + [final, lax.ppermute(final, "blk", partner)]
    spread = spread_on(late, later, codes, held, total)
    spread, whole = lax.optimization_barrier((spread, whole))
    parts = exchange(spread.reshape(copies, -1, *spread.shape[1:]), "rep")
    return result(parts, whole, out_grad, w_self)


def solution(mesh):
    placed = (
        P(("blk", "rep"), None),
        P(("blk", "rep"), None),
        P(("blk", "rep"), None),
        P(),
        P(),
        P("blk", None, None, None, None),
        P("blk", None, None),
        P("blk", None, None),
        P("blk", None),
    )
    return jax.shard_map(
        on_device,
        mesh=mesh,
        in_specs=placed,
        out_specs=(P(("blk", "rep"), None), P(), P()),
        check_vma=False,
    )
```

time: 85.4 us -> 82.7 us (0.968); the launches traced: 83.7 us -> 82.2 us
  local copies, waits for them, and re-layouts: 5.42 us -> 2.04 us
  waiting for transfers between devices: 24 us -> 26.6 us
  starting transfers between devices: 31.8 us -> 29.7 us
  Pallas kernels: 9.87 us -> 11.6 us
    all_to_all x3, waiting for transfers between devices: 15.3 us -> 19.3 us  [exchange(): return lax.all_to_all(x, axes, 0, 0, axis_index_groups=groups, tiled=True)]
    ppermute x4, waiting for transfers between devices: 7.18 us -> 3.24 us  [on_device(): nears.append(lax.ppermute(near, 'blk', onward))]
    unnamed x12 -> x10, local copies, waits for them, and re-layouts: 5.42 us -> 2.04 us
    ppermute x3, starting transfers between devices: 3.22 us -> 0.06 us  [on_device(): lax.ppermute(near, 'blk', partner)]
    ppermute x3, waiting for transfers between devices: 0.01 us -> 2.4 us  [on_device(): others.append(lax.ppermute(other, 'blk', onward))]
    ppermute x4, starting transfers between devices: 3.25 us -> 5.26 us  [on_device(): nears.append(lax.ppermute(near, 'blk', onward))]
    pallas_call x2, Pallas kernels: 4.85 us -> 6.53 us  [the longest x1 4.29 us: spread_over(): pl.pallas_call(functools.partial(spread_kernel, sources, later), out_shap...]
    ppermute x3, starting transfers between devices: 4.49 us -> 3.38 us  [on_device(): others.append(lax.ppermute(other, 'blk', onward))]
  transfers between devices with their start and end apart: 17 -> 17, of which waited for: 4 -> 9; matrix products, arithmetic and copies ran while one was open for 0% -> 0% of each run, Pallas kernels for 8% -> 10%
where the time goes in v3:
time: 82.7 us; the launch traced here: 82.2 us
  starting transfers between devices  29.7 us (36%)
  waiting for transfers between devices  26.6 us (32%)
  Pallas kernels  11.6 us (14%)
  blocking collectives  11.5 us (14%)
  local copies, waits for them, and re-layouts  2.04 us (2%)
    all_to_all x3, starting transfers between devices, exchange(): return lax.all_to_all(x, axes, 0, 0, axis_index_groups=groups, tiled=True)  19.6 us
    all_to_all x3, waiting for transfers between devices, exchange(): return lax.all_to_all(x, axes, 0, 0, axis_index_groups=groups, tiled=True)  19.3 us
    all_to_all x1, blocking collectives, exchange(): return lax.all_to_all(x, axes, 0, 0, axis_index_groups=groups, tiled=True)  11.5 us
    ppermute x4, starting transfers between devices, on_device(): nears.append(lax.ppermute(near, 'blk', onward))  5.26 us
    pallas_call x1, Pallas kernels, spread_over(): pl.pallas_call(functools.partial(spread_kernel, sources, later), out_shap...  4.29 us
    ppermute x3, starting transfers between devices, on_device(): others.append(lax.ppermute(other, 'blk', onward))  3.38 us
    ppermute x4, waiting for transfers between devices, on_device(): nears.append(lax.ppermute(near, 'blk', onward))  3.24 us
    pallas_call x1, Pallas kernels, opening(): pl.pallas_call(opening_kernel, out_shape=jax.ShapeDtypeStruct(shape, jnp....  2.43 us
  transfers between devices with their start and end apart: 17, of which 9 were waited for; matrix products, arithmetic and copies ran while one was open for 0% of the time, Pallas kernels for 10%

profile of v3, /device:TPU:8, one launch (start us, length us, event | category | flops | bytes accessed | tf_op | source)
XLA Modules:
  0.0 82.2 jit_solution(1431434454594992002)
XLA Ops:
  0.6 2.4 %opening.1 = bf16[32,4,32,128]{3,2,1,0:T(8,128)(2,1)} custom-call(bf16[256,256]{1,0:T(8,128)(2,1)} %features.1, bf16[256,256]{1,0:T(8,128)(2,1)} %aggregated.1, bf16[256,256]{1,0:T(8,128)(2,1)} %grad.3, bf16[256,256]{1,0:T(8,128)(2,1)} %weight.2), custom_call_target="tpu_custom_call" | custom-call | tf_op jit(solution)/shard_map/opening/pallas_call | solution.py:61
  3.1 7.5 %all-to-all-start = ((bf16[32,4,32,128]{3,2,1,0:T(8,128)(2,1)}), bf16[32,4,32,128]{3,2,1,0:T(8,128)(2,1)S(1)}, u32[]{:S(2)}, u32[]{:S(2)}) async-start(bf16[32,4,32,128]{3,2,1,0:T(8,128)(2,1)} %opening.1), calls=%async_computation | async-start | bytes 2097152 | tf_op jit(solution)/shard_map/all_to_all | solution.py:26
  10.6 15.7 %all-to-all-done.arrived = bf16[32,4,32,128]{3,2,1,0:T(8,128)(2,1)S(1)} async-done(((bf16[32,4,32,128]{3,2,1,0:T(8,128)(2,1)}), bf16[32,4,32,128]{3,2,1,0:T(8,128)(2,1)S(1)}, u32[]{:S(2)}, u32[]{:S(2)}) %all-to-all-start) | async-done | bytes 1048608 | tf_op jit(solution)/shard_map/all_to_all | solution.py:26
  26.3 2.0 %collective-permute-start = (bf16[32,32,128]{2,1,0:T(8,128)(2,1)S(1)}, bf16[32,32,128]{2,1,0:T(8,128)(2,1)S(1)}, u32[]{:S(2)}, u32[]{:S(2)}) collective-permute-start(bf16[32,32,128]{2,1,0:T(8,128)(2,1)S(1)} %bitcast.8), channel_id=1, source_target_pairs={{0,32},{8,232},{16,48},{24,248},{32,64},{40,8},{48,80},{56,24},{64... | collective-permute-start | bytes 786440 | tf_op jit(solution)/shard_map/ppermute | solution.py:300
  28.3 1.9 %collective-permute-start.3 = (bf16[32,32,128]{2,1,0:T(8,128)(2,1)S(1)}, bf16[32,32,128]{2,1,0:T(8,128)(2,1)S(1)}, u32[]{:S(2)}, u32[]{:S(2)}) collective-permute-start(bf16[32,32,128]{2,1,0:T(8,128)(2,1)S(1)} %bitcast.6), channel_id=1, source_target_pairs={{0,32},{8,232},{16,48},{24,248},{32,64},{40,8},{48,80},{56,24},{64... | collective-permute-start | bytes 786440 | tf_op jit(solution)/shard_map/ppermute | solution.py:302
  30.2 0.7 plane_sum.1
  31.0 6.7 %all-to-all-start.1 = ((f32[8,32,128]{2,1,0:T(8,128)}), f32[8,32,128]{2,1,0:T(8,128)S(1)}, u32[]{:S(2)}, u32[]{:S(2)}) async-start(f32[8,32,128]{2,1,0:T(8,128)} %plane_sum.1), calls=%async_computation.1 | async-start | bytes 262144 | tf_op jit(solution)/shard_map/all_to_all | solution.py:26
  37.6 0.0 collective-permute-done.refs_1_
  37.6 2.0 %collective-permute-start.1 = (bf16[32,32,128]{2,1,0:T(8,128)(2,1)S(1)}, bf16[32,32,128]{2,1,0:T(8,128)(2,1)S(1)}, u32[]{:S(2)}, u32[]{:S(2)}) collective-permute-start(bf16[32,32,128]{2,1,0:T(8,128)(2,1)S(1)} %collective-permute-done.refs_1_), channel_id=1, source_target_pairs={{0,32},{8,232},{16,48},{24,248},{32,64},{40,8},{48,80},{56,24},{64... | collective-permute-start | bytes 786440 | tf_op jit(solution)/shard_map/ppermute | solution.py:300
  39.6 0.0 collective-permute-done.3.refs_5_
  39.7 1.5 %collective-permute-start.4 = (bf16[32,32,128]{2,1,0:T(8,128)(2,1)S(1)}, bf16[32,32,128]{2,1,0:T(8,128)(2,1)S(1)}, u32[]{:S(2)}, u32[]{:S(2)}) collective-permute-start(bf16[32,32,128]{2,1,0:T(8,128)(2,1)S(1)} %collective-permute-done.3.refs_5_), channel_id=1, source_target_pairs={{0,32},{8,232},{16,48},{24,248},{32,64},{40,8},{48,80},{56,24},{64... | collective-permute-start | bytes 786440 | tf_op jit(solution)/shard_map/ppermute | solution.py:302
  41.1 0.7 copy-done.2
  41.8 0.7 copy-done.3
  42.5 0.7 copy-done.4
  43.2 3.7 %all-to-all-done.1.parts = f32[8,32,128]{2,1,0:T(8,128)S(1)} async-done(((f32[8,32,128]{2,1,0:T(8,128)}), f32[8,32,128]{2,1,0:T(8,128)S(1)}, u32[]{:S(2)}, u32[]{:S(2)}) %all-to-all-start.1) | async-done | bytes 131104 | tf_op jit(solution)/shard_map/all_to_all | solution.py:26
  46.8 0.3 collective-permute-done.1.refs_2_
  47.2 0.9 %collective-permute-start.2 = (bf16[32,32,128]{2,1,0:T(8,128)(2,1)S(1)}, bf16[32,32,128]{2,1,0:T(8,128)(2,1)S(1)}, u32[]{:S(2)}, u32[]{:S(2)}) collective-permute-start(bf16[32,32,128]{2,1,0:T(8,128)(2,1)S(1)} %collective-permute-done.1.refs_2_), channel_id=1, source_target_pairs={{0,32},{8,232},{16,48},{24,248},{32,64},{40,8},{48,80},{56,24},{64... | collective-permute-start | bytes 786440 | tf_op jit(solution)/shard_map/ppermute | solution.py:300
  48.0 1.9 %collective-permute-done.4.refs_6_ = bf16[32,32,128]{2,1,0:T(8,128)(2,1)S(1)} collective-permute-done((bf16[32,32,128]{2,1,0:T(8,128)(2,1)S(1)}, bf16[32,32,128]{2,1,0:T(8,128)(2,1)S(1)}, u32[]{:S(2)}, u32[]{:S(2)}) %collective-permute-start.4) | collective-permute-done | bytes 262176 | tf_op jit(solution)/shard_map/ppermute | solution.py:302
  50.0 0.0 collective-permute-start.5
  50.0 0.0 collective-permute-start.7
  50.0 0.5 collective-permute-start.8
  50.5 0.0 collective-permute-start.9
  50.5 0.9 %summed.1 = f32[32,32,128]{2,1,0:T(8,128)} custom-call(f32[8,32,128]{2,1,0:T(8,128)S(1)} %all-to-all-done.1.parts), custom_call_target="tpu_custom_call" | custom-call | tf_op jit(solution)/shard_map/summed/pallas_call | solution.py:117
  51.4 5.4 %all-to-all-start.2 = ((f32[32,32,128]{2,1,0:T(8,128)}), f32[32,32,128]{2,1,0:T(8,128)S(1)}, u32[]{:S(2)}, u32[]{:S(2)}) async-start(f32[32,32,128]{2,1,0:T(8,128)} %summed.1), calls=%async_computation.2 | async-start | bytes 1048576 | tf_op jit(solution)/shard_map/all_to_all | solution.py:26
  56.8 0.0 collective-permute-done.2.refs_3_
  56.8 0.3 collective-permute-start.10
  57.1 0.5 collective-permute-done.5.refs_7_
  57.6 0.4 collective-permute-start.6
  57.9 4.3 %spread.1 = (f32[16,32,128]{2,1,0:T(8,128)S(1)}, bf16[32,8,128,128]{3,2,1,0:T(8,128)(2,1)S(1)}) custom-call(s32[8,32]{1,0:T(8,128)S(1)} %codes.1, bf16[1,32,8,128,128]{4,3,2,1,0:T(8,128)(2,1)} %tiles.1, bf16[32,32,128]{2,1,0:T(8,128)(2,1)S(1)} %bitcast.9, bf16[32,32,128]{2,1,0:T(8,128)(2,1)S(1)} %collective-permute-done.refs_1_, ...), custom_call_target="tpu_custom_call" | custom-call | flops 20000000000 | tf_op jit(solution)/shard_map/spread/pallas_call | solution.py:198
  62.2 0.0 copy-start
  62.2 0.0 copy-start.1
  62.3 2.9 %collective-permute-done.6.refs_6_ = bf16[32,32,128]{2,1,0:T(8,128)(2,1)S(1)} collective-permute-done((bf16[32,32,128]{2,1,0:T(8,128)(2,1)S(1)}, bf16[32,32,128]{2,1,0:T(8,128)(2,1)S(1)}, u32[]{:S(2)}, u32[]{:S(2)}) %collective-permute-start.6) | collective-permute-done | bytes 262176 | tf_op jit(solution)/shard_map/ppermute | solution.py:300
  65.1 0.0 collective-permute-start.11
  65.1 0.0 collective-permute-done.7.refs_0_
  65.1 0.5 collective-permute-start.12
  65.7 0.0 collective-permute-done.8.refs_1_
  65.7 0.1 collective-permute-start.13
  65.8 0.0 collective-permute-done.9.refs_2_
  65.8 0.0 collective-permute-done.10.refs_3_
  65.8 0.9 %collective-permute-done.11.refs_4_ = bf16[32,32,128]{2,1,0:T(8,128)(2,1)S(1)} collective-permute-done((bf16[32,32,128]{2,1,0:T(8,128)(2,1)S(1)}, bf16[32,32,128]{2,1,0:T(8,128)(2,1)S(1)}, u32[]{:S(2)}, u32[]{:S(2)}) %collective-permute-start.11) | collective-permute-done | bytes 262176 | tf_op jit(solution)/shard_map/ppermute | solution.py:305
  66.7 0.4 collective-permute-done.12.refs_5_
  67.1 0.4 collective-permute-done.13.refs_7_
  67.4 2.2 %spread_on.1 = f32[16,32,128]{2,1,0:T(8,128)S(1)} custom-call(s32[8,32]{1,0:T(8,128)S(1)} %codes.1, bf16[32,8,128,128]{3,2,1,0:T(8,128)(2,1)S(1)} %get-tuple-element.14.tiles, f32[16,32,128]{2,1,0:T(8,128)S(1)} %get-tuple-element.16.begun, bf16[32,32,128]{2,1,0:T(8,128)(2,1)S(1)} %collective-permute-done.7.refs_0_, ...), custom_call_target="tpu_custom_call" | custom-call | flops 1 | tf_op jit(solution)/shard_map/spread_on/pallas_call | solution.py:230
  69.7 0.0 all-to-all-done.2.whole
  69.7 11.5 %all_to_all.20.parts = f32[8,2,32,128]{3,2,1,0:T(8,128)S(1)} all-to-all(f32[8,2,32,128]{3,2,1,0:T(8,128)S(1)} %bitcast.5), channel_id=1, replica_groups=mesh['blk'=32,'rep'=8] {'rep'}, dimensions={0} | all-to-all | bytes 524288 | tf_op jit(solution)/shard_map/all_to_all | solution.py:26
  81.2 0.0 copy-done
  81.2 0.0 copy-done.1
  81.2 1.0 %result.1 = (f32[256,256]{1,0:T(8,128)}, f32[256,256]{1,0:T(8,128)}, f32[256,256]{1,0:T(8,128)}) custom-call(f32[8,2,32,128]{3,2,1,0:T(8,128)S(1)} %all_to_all.20.parts, f32[32,32,128]{2,1,0:T(8,128)S(1)} %all-to-all-done.2.whole, bf16[256,256]{1,0:T(8,128)(2,1)S(1)} %copy-done, bf16[256,256]{1,0:T(8,128)(2,1)S(1)} %copy-done.1), custom_call_target="tpu_custom_call" | custom-call | tf_op jit(solution)/shard_map/result/pallas_call | solution.py:144
  (5 shorter events, 0.0 us)
Async XLA Ops:
  3.1 23.2 %all-to-all-start = ((bf16[32,4,32,128]{3,2,1,0:T(8,128)(2,1)}), bf16[32,4,32,128]{3,2,1,0:T(8,128)(2,1)S(1)}, u32[]{:S(2)}, u32[]{:S(2)}) async-start(bf16[32,4,32,128]{3,2,1,0:T(8,128)(2,1)} %opening.1), calls=%async_computation | async-start | bytes 2097152 | tf_op jit(solution)/shard_map/all_to_all | solution.py:26
  26.3 11.3 %collective-permute-start = (bf16[32,32,128]{2,1,0:T(8,128)(2,1)S(1)}, bf16[32,32,128]{2,1,0:T(8,128)(2,1)S(1)}, u32[]{:S(2)}, u32[]{:S(2)}) collective-permute-start(bf16[32,32,128]{2,1,0:T(8,128)(2,1)S(1)} %bitcast.8), channel_id=1, source_target_pairs={{0,32},{8,232},{16,48},{24,248},{32,64},{40,8},{48,80},{56,24},{64... | collective-permute-start | bytes 786440 | tf_op jit(solution)/shard_map/ppermute | solution.py:300
  28.3 11.4 %collective-permute-start.3 = (bf16[32,32,128]{2,1,0:T(8,128)(2,1)S(1)}, bf16[32,32,128]{2,1,0:T(8,128)(2,1)S(1)}, u32[]{:S(2)}, u32[]{:S(2)}) collective-permute-start(bf16[32,32,128]{2,1,0:T(8,128)(2,1)S(1)} %bitcast.6), channel_id=1, source_target_pairs={{0,32},{8,232},{16,48},{24,248},{32,64},{40,8},{48,80},{56,24},{64... | collective-permute-start | bytes 786440 | tf_op jit(solution)/shard_map/ppermute | solution.py:302
  31.0 15.9 %all-to-all-start.1 = ((f32[8,32,128]{2,1,0:T(8,128)}), f32[8,32,128]{2,1,0:T(8,128)S(1)}, u32[]{:S(2)}, u32[]{:S(2)}) async-start(f32[8,32,128]{2,1,0:T(8,128)} %plane_sum.1), calls=%async_computation.1 | async-start | bytes 262144 | tf_op jit(solution)/shard_map/all_to_all | solution.py:26
  37.6 9.5 %collective-permute-start.1 = (bf16[32,32,128]{2,1,0:T(8,128)(2,1)S(1)}, bf16[32,32,128]{2,1,0:T(8,128)(2,1)S(1)}, u32[]{:S(2)}, u32[]{:S(2)}) collective-permute-start(bf16[32,32,128]{2,1,0:T(8,128)(2,1)S(1)} %collective-permute-done.refs_1_), channel_id=1, source_target_pairs={{0,32},{8,232},{16,48},{24,248},{32,64},{40,8},{48,80},{56,24},{64... | collective-permute-start | bytes 786440 | tf_op jit(solution)/shard_map/ppermute | solution.py:300
  39.7 10.3 %collective-permute-start.4 = (bf16[32,32,128]{2,1,0:T(8,128)(2,1)S(1)}, bf16[32,32,128]{2,1,0:T(8,128)(2,1)S(1)}, u32[]{:S(2)}, u32[]{:S(2)}) collective-permute-start(bf16[32,32,128]{2,1,0:T(8,128)(2,1)S(1)} %collective-permute-done.3.refs_5_), channel_id=1, source_target_pairs={{0,32},{8,232},{16,48},{24,248},{32,64},{40,8},{48,80},{56,24},{64... | collective-permute-start | bytes 786440 | tf_op jit(solution)/shard_map/ppermute | solution.py:302
  41.1 0.7 copy-start.2
  41.8 0.7 copy-start.3
  42.5 0.7 copy-start.4
  47.2 9.6 %collective-permute-start.2 = (bf16[32,32,128]{2,1,0:T(8,128)(2,1)S(1)}, bf16[32,32,128]{2,1,0:T(8,128)(2,1)S(1)}, u32[]{:S(2)}, u32[]{:S(2)}) collective-permute-start(bf16[32,32,128]{2,1,0:T(8,128)(2,1)S(1)} %collective-permute-done.1.refs_2_), channel_id=1, source_target_pairs={{0,32},{8,232},{16,48},{24,248},{32,64},{40,8},{48,80},{56,24},{64... | collective-permute-start | bytes 786440 | tf_op jit(solution)/shard_map/ppermute | solution.py:300
  50.0 7.6 %collective-permute-start.5 = (bf16[32,32,128]{2,1,0:T(8,128)(2,1)S(1)}, bf16[32,32,128]{2,1,0:T(8,128)(2,1)S(1)}, u32[]{:S(2)}, u32[]{:S(2)}) collective-permute-start(bf16[32,32,128]{2,1,0:T(8,128)(2,1)S(1)} %collective-permute-done.4.refs_6_), channel_id=1, source_target_pairs={{0,32},{8,232},{16,48},{24,248},{32,64},{40,8},{48,80},{56,24},{64... | collective-permute-start | bytes 786440 | tf_op jit(solution)/shard_map/ppermute | solution.py:302
  50.0 15.2 %collective-permute-start.7 = (bf16[32,32,128]{2,1,0:T(8,128)(2,1)S(1)}, bf16[32,32,128]{2,1,0:T(8,128)(2,1)S(1)}, u32[]{:S(2)}, u32[]{:S(2)}) collective-permute-start(bf16[32,32,128]{2,1,0:T(8,128)(2,1)S(1)} %collective-permute-done.refs_1_), channel_id=1, source_target_pairs={{0,8},{8,0},{16,24},{24,16},{32,40},{40,32},{48,56},{56,48},{64,72... | collective-permute-start | bytes 786440 | tf_op jit(solution)/shard_map/ppermute | solution.py:305
  50.0 15.7 %collective-permute-start.8 = (bf16[32,32,128]{2,1,0:T(8,128)(2,1)S(1)}, bf16[32,32,128]{2,1,0:T(8,128)(2,1)S(1)}, u32[]{:S(2)}, u32[]{:S(2)}) collective-permute-start(bf16[32,32,128]{2,1,0:T(8,128)(2,1)S(1)} %collective-permute-done.3.refs_5_), channel_id=1, source_target_pairs={{0,8},{8,0},{16,24},{24,16},{32,40},{40,32},{48,56},{56,48},{64,72... | collective-permute-start | bytes 786440 | tf_op jit(solution)/shard_map/ppermute | solution.py:306
  50.5 15.3 %collective-permute-start.9 = (bf16[32,32,128]{2,1,0:T(8,128)(2,1)S(1)}, bf16[32,32,128]{2,1,0:T(8,128)(2,1)S(1)}, u32[]{:S(2)}, u32[]{:S(2)}) collective-permute-start(bf16[32,32,128]{2,1,0:T(8,128)(2,1)S(1)} %collective-permute-done.1.refs_2_), channel_id=1, source_target_pairs={{0,8},{8,0},{16,24},{24,16},{32,40},{40,32},{48,56},{56,48},{64,72... | collective-permute-start | bytes 786440 | tf_op jit(solution)/shard_map/ppermute | solution.py:305
  51.4 18.3 %all-to-all-start.2 = ((f32[32,32,128]{2,1,0:T(8,128)}), f32[32,32,128]{2,1,0:T(8,128)S(1)}, u32[]{:S(2)}, u32[]{:S(2)}) async-start(f32[32,32,128]{2,1,0:T(8,128)} %summed.1), calls=%async_computation.2 | async-start | bytes 1048576 | tf_op jit(solution)/shard_map/all_to_all | solution.py:26
  56.8 9.0 %collective-permute-start.10 = (bf16[32,32,128]{2,1,0:T(8,128)(2,1)S(1)}, bf16[32,32,128]{2,1,0:T(8,128)(2,1)S(1)}, u32[]{:S(2)}, u32[]{:S(2)}) collective-permute-start(bf16[32,32,128]{2,1,0:T(8,128)(2,1)S(1)} %collective-permute-done.4.refs_6_), channel_id=1, source_target_pairs={{0,8},{8,0},{16,24},{24,16},{32,40},{40,32},{48,56},{56,48},{64,72... | collective-permute-start | bytes 786440 | tf_op jit(solution)/shard_map/ppermute | solution.py:306
  57.6 7.6 %collective-permute-start.6 = (bf16[32,32,128]{2,1,0:T(8,128)(2,1)S(1)}, bf16[32,32,128]{2,1,0:T(8,128)(2,1)S(1)}, u32[]{:S(2)}, u32[]{:S(2)}) collective-permute-start(bf16[32,32,128]{2,1,0:T(8,128)(2,1)S(1)} %collective-permute-done.2.refs_3_), channel_id=1, source_target_pairs={{0,32},{8,232},{16,48},{24,248},{32,64},{40,8},{48,80},{56,24},{64... | collective-permute-start | bytes 786440 | tf_op jit(solution)/shard_map/ppermute | solution.py:300
  62.2 19.0 %copy-start = (bf16[256,256]{1,0:T(8,128)(2,1)S(1)}, bf16[256,256]{1,0:T(8,128)(2,1)}, u32[]{:S(2)}) copy-start(bf16[256,256]{1,0:T(8,128)(2,1)} %grad.3) | copy-start | bytes 393220
  62.2 19.0 %copy-start.1 = (bf16[256,256]{1,0:T(8,128)(2,1)S(1)}, bf16[256,256]{1,0:T(8,128)(2,1)}, u32[]{:S(2)}) copy-start(bf16[256,256]{1,0:T(8,128)(2,1)} %weight.3) | copy-start | bytes 393220
  65.1 1.5 %collective-permute-start.11 = (bf16[32,32,128]{2,1,0:T(8,128)(2,1)S(1)}, bf16[32,32,128]{2,1,0:T(8,128)(2,1)S(1)}, u32[]{:S(2)}, u32[]{:S(2)}) collective-permute-start(bf16[32,32,128]{2,1,0:T(8,128)(2,1)S(1)} %collective-permute-done.2.refs_3_), channel_id=1, source_target_pairs={{0,8},{8,0},{16,24},{24,16},{32,40},{40,32},{48,56},{56,48},{64,72... | collective-permute-start | bytes 786440 | tf_op jit(solution)/shard_map/ppermute | solution.py:305
  65.1 1.9 %collective-permute-start.12 = (bf16[32,32,128]{2,1,0:T(8,128)(2,1)S(1)}, bf16[32,32,128]{2,1,0:T(8,128)(2,1)S(1)}, u32[]{:S(2)}, u32[]{:S(2)}) collective-permute-start(bf16[32,32,128]{2,1,0:T(8,128)(2,1)S(1)} %collective-permute-done.5.refs_7_), channel_id=1, source_target_pairs={{0,8},{8,0},{16,24},{24,16},{32,40},{40,32},{48,56},{56,48},{64,72... | collective-permute-start | bytes 786440 | tf_op jit(solution)/shard_map/ppermute | solution.py:306
  65.7 1.8 %collective-permute-start.13 = (bf16[32,32,128]{2,1,0:T(8,128)(2,1)S(1)}, bf16[32,32,128]{2,1,0:T(8,128)(2,1)S(1)}, u32[]{:S(2)}, u32[]{:S(2)}) collective-permute-start(bf16[32,32,128]{2,1,0:T(8,128)(2,1)S(1)} %collective-permute-done.6.refs_6_), channel_id=1, source_target_pairs={{0,8},{8,0},{16,24},{24,16},{32,40},{40,32},{48,56},{56,48},{64,72... | collective-permute-start | bytes 786440 | tf_op jit(solution)/shard_map/ppermute | solution.py:313

commit v4 on v3

--- a/solution.py
+++ b/solution.py
@@ -14,6 +14,7 @@
 RUN = 4
 TOGETHER = 4
 BOTH = ("blk", "rep")
+AS_A_HOP = pl.CostEstimate(flops=100000000, bytes_accessed=0, transcendentals=0)
 AS_SHORT = pl.CostEstimate(flops=1, bytes_accessed=0, transcendentals=0)
 AS_LONG = pl.CostEstimate(flops=20000000000, bytes_accessed=0, transcendentals=0)
 VMEM = pl.BlockSpec(memory_space=pltpu.VMEM)
@@ -31,24 +32,23 @@
         weight[...], grad[...], BY_LAST, preferred_element_type=jnp.float32
     ).astype(out.dtype)
     members, held, width, side = out.shape
-    tiles = held - 2
+    tiles = held - 4
     for p in range(members):
         s = slice_of(p)
         for t in range(tiles):
             out[p, t] = share[s * width : (s + 1) * width, t * side : (t + 1) * side]
     depth = width // 2
-    half = members // 2
     for which, source in enumerate((features, aggregated)):
         terms = lax.dot_general(
             source[...], grad[...], (((0,), (0,)), ((), ())), preferred_element_type=jnp.float32
         )
         upper = terms.astype(out.dtype)
         lower = (terms - upper.astype(jnp.float32)).astype(out.dtype)
-        for p in range(half):
+        for p in range(members):
             here = slice(p * depth, (p + 1) * depth)
-            for place, part in ((tiles, upper), (tiles + 1, lower)):
-                out[which * half + p, place, :depth] = part[here, :side]
-                out[which * half + p, place, depth:] = part[here, side:]
+            for place, part in enumerate((upper, lower), tiles + 2 * which):
+                out[p, place, :depth] = part[here, :side]
+                out[p, place, depth:] = part[here, side:]
 
 
 def slice_of(p):
@@ -57,7 +57,7 @@
 
 def opening(features, aggregated, out_grad, w_neigh, copies, side):
     rows, width = out_grad.shape
-    shape = (PLANE * copies, rows // side + 2, width // copies, side)
+    shape = (HALF * copies, rows // side + 4, width // copies, side)
     return pl.pallas_call(
         opening_kernel,
         out_shape=jax.ShapeDtypeStruct(shape, jnp.bfloat16),
@@ -66,24 +66,60 @@
     )(features, aggregated, out_grad, w_neigh)
 
 
-def plane_sum_kernel(arrived, out):
-    tiles = arrived.shape[1] - 2
-    total = jnp.zeros(out.shape[1:], jnp.float32)
-    for m in range(arrived.shape[0]):
-        total = total + (
-            arrived[m, tiles].astype(jnp.float32) + arrived[m, tiles + 1].astype(jnp.float32)
-        )
+def half_sums_kernel(arrived, keep, give):
+    members, held, _, _ = arrived.shape
+    core = lax.rem(lax.axis_index("blk"), 2)
+    sums = []
+    for first in range(held - 4, held, 2):
+        total = jnp.zeros(keep.shape, jnp.float32)
+        for m in range(members):
+            total = total + (
+                arrived[m, first].astype(jnp.float32) + arrived[m, first + 1].astype(jnp.float32)
+            )
+        sums.append(total)
+    keep[...] = jnp.where(core == 0, sums[0], sums[1])
+    give[...] = jnp.where(core == 0, sums[1], sums[0])
+
+
+def half_sums(arrived):
+    shape = jax.ShapeDtypeStruct(arrived.shape[2:], jnp.float32)
+    return pl.pallas_call(
+        half_sums_kernel,
+        out_shape=[shape, shape],
+        compiler_params=ROOM,
+        name="half_sums",
+    )(arrived)
+
+
+def joined_kernel(keep, got, out):
+    total = keep[...] + got[...]
     for copy in range(out.shape[0]):
         out[copy] = total
 
 
-def plane_sum(arrived, again):
-    return pl.pallas_call(
-        plane_sum_kernel,
-        out_shape=jax.ShapeDtypeStruct((again, *arrived.shape[2:]), jnp.float32),
-        compiler_params=ROOM,
-        name="plane_sum",
-    )(arrived)
+def joined(keep, got, again):
+    return pl.pallas_call(
+        joined_kernel,
+        out_shape=jax.ShapeDtypeStruct((again, *keep.shape), keep.dtype),
+        compiler_params=ROOM,
+        name="joined",
+    )(keep, got)
+
+
+def gate_kernel(block, before, out):
+    out[...] = jnp.zeros_like(out)
+
+
+def gate(block, before):
+    anywhere = pl.BlockSpec(memory_space=pl.ANY)
+    return pl.pallas_call(
+        gate_kernel,
+        out_shape=jax.ShapeDtypeStruct((8, 128), jnp.int32),
+        in_specs=[anywhere, anywhere],
+        compiler_params=ROOM,
+        cost_estimate=AS_A_HOP,
+        name="gate",
+    )(block, before)
 
 
 def codes_kernel(tiles_side, rows, cols, counts, out):
@@ -122,7 +158,7 @@
     )(parts)
 
 
-def result_kernel(parts, whole, grad, weight, out, self_out, neigh_out):
+def result_kernel(parts, whole, grad, weight, token, out, self_out, neigh_out):
     straight = lax.dot_general(
         grad[...], weight[...], BY_LAST, preferred_element_type=jnp.float32
     )
@@ -139,7 +175,7 @@
         target[top : top + depth, side:] = whole[m, depth:]
 
 
-def result(parts, whole, out_grad, w_self):
+def result(parts, whole, out_grad, w_self, token):
     rows, width = out_grad.shape
     return pl.pallas_call(
         result_kernel,
@@ -150,7 +186,7 @@
         ],
         compiler_params=ROOM,
         name="result",
-    )(parts, whole, out_grad, w_self)
+    )(parts, whole, out_grad, w_self, token)
 
 
 def add_products(acc, codes, tiles, piece, source, m, shift):
@@ -183,7 +219,7 @@
         copy.start()
     acc[...] = jnp.zeros_like(acc)
     for n in range(0, len(work), TOGETHER):
-        for copy in copies[n : n + TOGETHER]:
+        for copy in copies[n : min(n + TOGETHER, len(work))]:
             copy.wait()
         for piece, source, m in work[n : n + TOGETHER]:
             add_products(acc, codes, held, piece, source, m, shift)
@@ -245,7 +281,6 @@
     block_total = lax.axis_size("blk")
     copies = lax.axis_size("rep")
     planes = block_total // PLANE
-    core = lax.rem(lax.axis_index("blk"), 2)
     share_rows, width = out_grad.shape
     side = tiles.shape[-1]
     tiles_side = share_rows // side * copies
@@ -263,16 +298,16 @@
     over_planes = [[p * PLANE + q for p in range(planes)] for q in range(PLANE)]
 
     sent = opening(features, aggregated, out_grad, w_neigh, copies, side)
-    arrived = exchange(sent, BOTH, in_plane)
-    own = arrived[:, :-2].reshape(2, member, *sent.shape[2:])
+    half = member // HALF
+    arrived = exchange(sent, BOTH, [g[c * half :][:half] for g in in_plane for c in range(HALF)])
 
     onward = [
         (b, (b + PLANE) % block_total if b % 2 == 0 else (b - PLANE) % block_total)
         for b in range(block_total)
     ]
     partner = [(b, b ^ 1) for b in range(block_total)]
-    near = jnp.where(core == 0, own[0], own[1])
-    other = jnp.where(core == 0, own[1], own[0])
+    near = arrived[:, :-4].reshape(member, *sent.shape[2:])
+    other = lax.ppermute(near, "blk", partner)
     steps = planes // 2
     def source(step, flip, swap):
         def of(block, m):
@@ -287,34 +322,47 @@
     codes = slot_codes(tile_rows, tile_cols, tile_counts, tiles_side)
 
     scale = (share_rows * block_total * copies) ** (-0.5)
-    part = plane_sum(arrived, planes)
-    nears, others, swaps = [near], [other], [[]]
-    part = exchange(part, "blk", over_planes)
-    swaps = []
+    keep, give = half_sums(arrived)
+    given = lax.ppermute(give, "blk", partner)
+    nears, others = [near], [other]
+    swaps, token = [], None
+    part = exchange(joined(keep, given, planes), "blk", over_planes)
     for step in range(steps):
         near, other = nears[-1], others[-1]
         if step == 2:
             near, codes, part = lax.optimization_barrier((near, codes, part))
             whole = exchange(summed(part, member, scale), BOTH, in_plane)
+            token = codes
+        if step > 2:
+            near, token = lax.optimization_barrier((near, token))
         nears[-1] = near
         nears.append(lax.ppermute(near, "blk", onward))
-        if step < steps - 1:
-            others.append(lax.ppermute(other, "blk", onward))
+        if step >= 2:
+            token = gate(near, token)
+            other, token = lax.optimization_barrier((other, token))
+            others[-1] = other
         if step > 0:
             swaps += [
                 (lax.ppermute(near, "blk", partner), source(step, False, True)),
                 (lax.ppermute(other, "blk", partner), source(step, True, True)),
             ]
+        if step < steps - 1:
+            others.append(lax.ppermute(other, "blk", onward))
+            if step >= 2:
+                token = gate(other, token)
     early = [(p, source(s, False, False)) for s, p in enumerate(nears[:-1])]
-    early += [(p, source(s, True, False)) for s, p in enumerate(others)]
-    later = [of for _, of in swaps] + [source(steps, False, swap) for swap in (False, True)]
+    early += [(p, source(s, True, False)) for s, p in enumerate(others[:-1])]
+    middle = [(others[-1], source(steps - 1, True, False)), *swaps]
+    ends = [source(steps, False, False), source(steps, False, True)]
+    later = [of for _, of in middle] + ends
     total, held = spread_over(*zip(*early), later, codes, tiles, tiles_side)
+    total = spread_on(*zip(*middle), codes, held, total)
     final, total = lax.optimization_barrier((nears[-1], total))
-    late = [p for p, _ in swaps] + [final, lax.ppermute(final, "blk", partner)]
-    spread = spread_on(late, later, codes, held, total)
+    late = [final, lax.ppermute(final, "blk", partner)]
+    spread = spread_on(late, ends, codes, held, total)
     spread, whole = lax.optimization_barrier((spread, whole))
     parts = exchange(spread.reshape(copies, -1, *spread.shape[1:]), "rep")
-    return result(parts, whole, out_grad, w_self)
+    return result(parts, whole, out_grad, w_self, token)
 
 
 def solution(mesh):

time: 82.7 us -> 82.1 us (level)
  blocking collectives: 11.5 us -> 32 us
  waiting for transfers between devices: 26.6 us -> 8.61 us
  starting transfers between devices: 29.7 us -> 25.7 us
    all_to_all x1 -> x2, blocking collectives: 11.5 us -> 32 us  [exchange(): return lax.all_to_all(x, axes, 0, 0, axis_index_groups=groups, tiled=True)]
    all_to_all x3 -> x2, waiting for transfers between devices: 19.3 us -> 4.01 us  [exchange(): return lax.all_to_all(x, axes, 0, 0, axis_index_groups=groups, tiled=True)]
    all_to_all x3 -> x2, starting transfers between devices: 19.6 us -> 9.48 us  [exchange(): return lax.all_to_all(x, axes, 0, 0, axis_index_groups=groups, tiled=True)]
    ppermute x1 -> x3, starting transfers between devices: 0.09 us -> 3.86 us  [the longest x1 3.4 us: on_device(): given = lax.ppermute(give, 'blk', partner)]
    ppermute x4, waiting for transfers between devices: 3.24 us -> 0.36 us  [on_device(): nears.append(lax.ppermute(near, 'blk', onward))]
    ppermute x3, starting transfers between devices: 1.3 us -> 3.07 us  [on_device(): lax.ppermute(other, 'blk', partner)]
    ppermute x1 -> x3, waiting for transfers between devices: 0.37 us -> 2.1 us  [the longest x1 1.26 us: on_device(): late = [final, lax.ppermute(final, 'blk', partner)]]
    pallas_call x1 -> x2, Pallas kernels: 2.24 us -> 3.21 us  [spread_on(): pl.pallas_call(functools.partial(spread_on_kernel, sources), out_shape=ja...]
  transfers between devices with their start and end apart: 17 -> 18, of which waited for: 9 -> 6; matrix products, arithmetic and copies ran while one was open for 0% -> 0% of each run, Pallas kernels for 10% -> 11%
where the time goes in v4:
time: 82.1 us; the launch traced here: 81.6 us
  blocking collectives  32 us (39%)
  starting transfers between devices  25.7 us (31%)
  Pallas kernels  12.4 us (15%)
  waiting for transfers between devices  8.61 us (10%)
  local copies, waits for them, and re-layouts  2.06 us (3%)
    all_to_all x2, blocking collectives, exchange(): return lax.all_to_all(x, axes, 0, 0, axis_index_groups=groups, tiled=True)  32 us
    all_to_all x2, starting transfers between devices, exchange(): return lax.all_to_all(x, axes, 0, 0, axis_index_groups=groups, tiled=True)  9.48 us
    ppermute x4, starting transfers between devices, on_device(): nears.append(lax.ppermute(near, 'blk', onward))  5.17 us
    pallas_call x1, Pallas kernels, spread_over(): pl.pallas_call(functools.partial(spread_kernel, sources, later), out_shap...  4.29 us
    all_to_all x2, waiting for transfers between devices, exchange(): return lax.all_to_all(x, axes, 0, 0, axis_index_groups=groups, tiled=True)  4.01 us
    ppermute x1, starting transfers between devices, on_device(): given = lax.ppermute(give, 'blk', partner)  3.4 us
    ppermute x3, starting transfers between devices, on_device(): others.append(lax.ppermute(other, 'blk', onward))  3.39 us
    pallas_call x2, Pallas kernels, spread_on(): pl.pallas_call(functools.partial(spread_on_kernel, sources), out_shape=ja...  3.21 us
  transfers between devices with their start and end apart: 18, of which 6 were waited for; matrix products, arithmetic and copies ran while one was open for 0% of the time, Pallas kernels for 11%

profile of v4, /device:TPU:8, one launch (start us, length us, event | category | flops | bytes accessed | tf_op | source)
XLA Modules:
  0.0 81.6 jit_solution(5869793439862498674)
XLA Ops:
  0.6 2.3 %opening.1 = bf16[16,6,32,128]{3,2,1,0:T(8,128)(2,1)} custom-call(bf16[256,256]{1,0:T(8,128)(2,1)} %features.1, bf16[256,256]{1,0:T(8,128)(2,1)} %aggregated.1, bf16[256,256]{1,0:T(8,128)(2,1)} %grad.3, bf16[256,256]{1,0:T(8,128)(2,1)} %weight.2), custom_call_target="tpu_custom_call" | custom-call | tf_op jit(solution)/shard_map/opening/pallas_call | solution.py:61
  2.9 20.0 %all_to_all.20.arrived = bf16[16,6,32,128]{3,2,1,0:T(8,128)(2,1)S(1)} all-to-all(bf16[16,6,32,128]{3,2,1,0:T(8,128)(2,1)} %opening.1), channel_id=1, replica_groups={{0,1,16,17,2,3,18,19,4,5,20,21,6,7,22,23},{8,9,24,25,10,11,26,27,12,13,..., dimensions={0} | all-to-all | bytes 1572864 | tf_op jit(solution)/shard_map/all_to_all | solution.py:27
  22.9 0.1 collective-permute-start.4
  23.0 2.0 %collective-permute-start = (bf16[32,32,128]{2,1,0:T(8,128)(2,1)S(1)}, bf16[32,32,128]{2,1,0:T(8,128)(2,1)S(1)}, u32[]{:S(2)}, u32[]{:S(2)}) collective-permute-start(bf16[32,32,128]{2,1,0:T(8,128)(2,1)S(1)} %bitcast.6), channel_id=1, source_target_pairs={{0,32},{8,232},{16,48},{24,248},{32,64},{40,8},{48,80},{56,24},{64... | collective-permute-start | bytes 786440 | tf_op jit(solution)/shard_map/ppermute | solution.py:339
  25.0 0.0 collective-permute-done.4.refs_4_
  25.0 1.9 %collective-permute-start.5 = (bf16[32,32,128]{2,1,0:T(8,128)(2,1)S(1)}, bf16[32,32,128]{2,1,0:T(8,128)(2,1)S(1)}, u32[]{:S(2)}, u32[]{:S(2)}) collective-permute-start(bf16[32,32,128]{2,1,0:T(8,128)(2,1)S(1)} %collective-permute-done.4.refs_4_), channel_id=1, source_target_pairs={{0,32},{8,232},{16,48},{24,248},{32,64},{40,8},{48,80},{56,24},{64... | collective-permute-start | bytes 786440 | tf_op jit(solution)/shard_map/ppermute | solution.py:350
  26.9 0.1 half_sums.1
  27.0 3.4 %collective-permute-start.2 = (f32[32,128]{1,0:T(8,128)S(1)}, f32[32,128]{1,0:T(8,128)S(1)}, u32[]{:S(2)}, u32[]{:S(2)}) collective-permute-start(f32[32,128]{1,0:T(8,128)S(1)} %get-tuple-element.21), channel_id=1, source_target_pairs={{0,8},{8,0},{16,24},{24,16},{32,40},{40,32},{48,56},{56,48},{64,72... | collective-permute-start | bytes 49160 | tf_op jit(solution)/shard_map/ppermute | solution.py:326
  30.4 0.8 %collective-permute-done.2.got = f32[32,128]{1,0:T(8,128)S(1)} collective-permute-done((f32[32,128]{1,0:T(8,128)S(1)}, f32[32,128]{1,0:T(8,128)S(1)}, u32[]{:S(2)}, u32[]{:S(2)}) %collective-permute-start.2) | collective-permute-done | bytes 16416 | tf_op jit(solution)/shard_map/ppermute | solution.py:326
  31.3 0.7 joined.1
  31.9 4.1 %all-to-all-start.1 = ((f32[8,32,128]{2,1,0:T(8,128)}), f32[8,32,128]{2,1,0:T(8,128)S(1)}, u32[]{:S(2)}, u32[]{:S(2)}) async-start(f32[8,32,128]{2,1,0:T(8,128)} %joined.1), calls=%async_computation.1 | async-start | bytes 262144 | tf_op jit(solution)/shard_map/all_to_all | solution.py:27
  36.1 0.0 collective-permute-done.refs_1_
  36.1 2.0 %collective-permute-start.1 = (bf16[32,32,128]{2,1,0:T(8,128)(2,1)S(1)}, bf16[32,32,128]{2,1,0:T(8,128)(2,1)S(1)}, u32[]{:S(2)}, u32[]{:S(2)}) collective-permute-start(bf16[32,32,128]{2,1,0:T(8,128)(2,1)S(1)} %collective-permute-done.refs_1_), channel_id=1, source_target_pairs={{0,32},{8,232},{16,48},{24,248},{32,64},{40,8},{48,80},{56,24},{64... | collective-permute-start | bytes 786440 | tf_op jit(solution)/shard_map/ppermute | solution.py:339
  38.1 0.0 collective-permute-done.5.refs_5_
  38.1 1.5 %collective-permute-start.6 = (bf16[32,32,128]{2,1,0:T(8,128)(2,1)S(1)}, bf16[32,32,128]{2,1,0:T(8,128)(2,1)S(1)}, u32[]{:S(2)}, u32[]{:S(2)}) collective-permute-start(bf16[32,32,128]{2,1,0:T(8,128)(2,1)S(1)} %collective-permute-done.5.refs_5_), channel_id=1, source_target_pairs={{0,32},{8,232},{16,48},{24,248},{32,64},{40,8},{48,80},{56,24},{64... | collective-permute-start | bytes 786440 | tf_op jit(solution)/shard_map/ppermute | solution.py:350
  39.5 0.7 copy-done.2
  40.2 0.7 copy-done.3
  40.9 0.7 copy-done.4
  41.6 4.0 %all-to-all-done.1.parts = f32[8,32,128]{2,1,0:T(8,128)S(1)} async-done(((f32[8,32,128]{2,1,0:T(8,128)}), f32[8,32,128]{2,1,0:T(8,128)S(1)}, u32[]{:S(2)}, u32[]{:S(2)}) %all-to-all-start.1) | async-done | bytes 131104 | tf_op jit(solution)/shard_map/all_to_all | solution.py:27
  45.6 0.4 collective-permute-done.1.block.refs_2_
  45.9 0.8 collective-permute-start.3
  46.7 2.0 %collective-permute-done.6.block.refs_6_ = bf16[32,32,128]{2,1,0:T(8,128)(2,1)S(1)} collective-permute-done((bf16[32,32,128]{2,1,0:T(8,128)(2,1)S(1)}, bf16[32,32,128]{2,1,0:T(8,128)(2,1)S(1)}, u32[]{:S(2)}, u32[]{:S(2)}) %collective-permute-start.6) | collective-permute-done | bytes 262176 | tf_op jit(solution)/shard_map/ppermute | solution.py:350
  48.7 0.0 collective-permute-start.8
  48.7 0.3 collective-permute-start.9
  49.1 0.2 collective-permute-start.10
  49.3 0.3 collective-permute-start.11
  49.6 0.9 %summed.1 = f32[32,32,128]{2,1,0:T(8,128)} custom-call(f32[8,32,128]{2,1,0:T(8,128)S(1)} %all-to-all-done.1.parts), custom_call_target="tpu_custom_call" | custom-call | tf_op jit(solution)/shard_map/summed/pallas_call | solution.py:153
  50.5 5.4 %all-to-all-start.2 = ((f32[32,32,128]{2,1,0:T(8,128)}), f32[32,32,128]{2,1,0:T(8,128)S(1)}, u32[]{:S(2)}, u32[]{:S(2)}) async-start(f32[32,32,128]{2,1,0:T(8,128)} %summed.1), calls=%async_computation.2 | async-start | bytes 1048576 | tf_op jit(solution)/shard_map/all_to_all | solution.py:27
  55.8 0.0 collective-permute-done.3.refs_3_.block
  55.9 0.4 collective-permute-start.7
  56.2 0.1 collective-permute-done.8.refs_0_
  56.3 2.5 %collective-permute-start.12 = (bf16[32,32,128]{2,1,0:T(8,128)(2,1)S(1)}, bf16[32,32,128]{2,1,0:T(8,128)(2,1)S(1)}, u32[]{:S(2)}, u32[]{:S(2)}) collective-permute-start(bf16[32,32,128]{2,1,0:T(8,128)(2,1)S(1)} %collective-permute-done.6.block.refs_6_), channel_id=1, source_target_pairs={{0,8},{8,0},{16,24},{24,16},{32,40},{40,32},{48,56},{56,48},{64,72... | collective-permute-start | bytes 786440 | tf_op jit(solution)/shard_map/ppermute | solution.py:347
  58.8 0.0 collective-permute-done.9.refs_1_
  58.8 0.1 collective-permute-start.13
  58.9 0.4 collective-permute-start.14
  59.3 4.3 %spread.1 = (f32[16,32,128]{2,1,0:T(8,128)S(1)}, bf16[32,8,128,128]{3,2,1,0:T(8,128)(2,1)S(1)}) custom-call(s32[8,32]{1,0:T(8,128)S(1)} %codes.1.before, bf16[1,32,8,128,128]{4,3,2,1,0:T(8,128)(2,1)} %tiles.1, bf16[32,32,128]{2,1,0:T(8,128)(2,1)S(1)} %bitcast.7, bf16[32,32,128]{2,1,0:T(8,128)(2,1)S(1)} %collective-permute-done.refs_1_, ...), custom_call_target="tpu_custom_call" | custom-call | flops 20000000000 | tf_op jit(solution)/shard_map/spread/pallas_call | solution.py:234
  63.6 0.0 collective-permute-done.11.refs_3_
  63.6 0.0 collective-permute-done.13.refs_5_
  63.7 0.0 collective-permute-done.14.refs_6_
  63.7 0.0 copy-start
  63.7 0.0 copy-start.1
  63.7 2.1 %spread_on.2.begun = f32[16,32,128]{2,1,0:T(8,128)S(1)} custom-call(s32[8,32]{1,0:T(8,128)S(1)} %codes.1.before, bf16[32,8,128,128]{3,2,1,0:T(8,128)(2,1)S(1)} %get-tuple-element.27.tiles, f32[16,32,128]{2,1,0:T(8,128)S(1)} %get-tuple-element.28.begun, bf16[32,32,128]{2,1,0:T(8,128)(2,1)S(1)} %collective-permute-done.8.refs_0_, ...), custom_call_target="tpu_custom_call" | custom-call | flops 1 | tf_op jit(solution)/shard_map/spread_on/pallas_call | solution.py:266
  65.8 0.4 collective-permute-start.15
  66.1 1.3 %collective-permute-done.15.refs_1_ = bf16[32,32,128]{2,1,0:T(8,128)(2,1)S(1)} collective-permute-done((bf16[32,32,128]{2,1,0:T(8,128)(2,1)S(1)}, bf16[32,32,128]{2,1,0:T(8,128)(2,1)S(1)}, u32[]{:S(2)}, u32[]{:S(2)}) %collective-permute-start.15) | collective-permute-done | bytes 262176 | tf_op jit(solution)/shard_map/ppermute | solution.py:361
  67.4 1.1 %spread_on.3 = f32[16,32,128]{2,1,0:T(8,128)S(1)} custom-call(s32[8,32]{1,0:T(8,128)S(1)} %codes.1.before, bf16[32,8,128,128]{3,2,1,0:T(8,128)(2,1)S(1)} %get-tuple-element.27.tiles, f32[16,32,128]{2,1,0:T(8,128)S(1)} %spread_on.2.begun, bf16[32,32,128]{2,1,0:T(8,128)(2,1)S(1)} %collective-permute-done.7.refs_0_, ...), custom_call_target="tpu_custom_call" | custom-call | flops 1 | tf_op jit(solution)/shard_map/spread_on/pallas_call | solution.py:266
  68.6 0.0 all-to-all-done.2.whole
  68.6 12.1 %all_to_all.21.parts = f32[8,2,32,128]{3,2,1,0:T(8,128)S(1)} all-to-all(f32[8,2,32,128]{3,2,1,0:T(8,128)S(1)} %bitcast.4), channel_id=1, replica_groups=mesh['blk'=32,'rep'=8] {'rep'}, dimensions={0} | all-to-all | bytes 524288 | tf_op jit(solution)/shard_map/all_to_all | solution.py:27
  80.6 1.0 %result.1 = (f32[256,256]{1,0:T(8,128)}, f32[256,256]{1,0:T(8,128)}, f32[256,256]{1,0:T(8,128)}) custom-call(f32[8,2,32,128]{3,2,1,0:T(8,128)S(1)} %all_to_all.21.parts, f32[32,32,128]{2,1,0:T(8,128)S(1)} %all-to-all-done.2.whole, bf16[256,256]{1,0:T(8,128)(2,1)S(1)} %copy-done, bf16[256,256]{1,0:T(8,128)(2,1)S(1)} %copy-done.1, s32[8,128]{1,0:T(8,128)S(1)} %gate.5.token), custom_call_target="tpu_custom_call" | custom-call | tf_op jit(solution)/shard_map/result/pallas_call | solution.py:180
  (13 shorter events, 0.0 us)
Async XLA Ops:
  22.9 2.1 %collective-permute-start.4 = (bf16[32,32,128]{2,1,0:T(8,128)(2,1)S(1)}, bf16[32,32,128]{2,1,0:T(8,128)(2,1)S(1)}, u32[]{:S(2)}, u32[]{:S(2)}) collective-permute-start(bf16[32,32,128]{2,1,0:T(8,128)(2,1)S(1)} %bitcast.5), channel_id=1, source_target_pairs={{0,8},{8,0},{16,24},{24,16},{32,40},{40,32},{48,56},{56,48},{64,72... | collective-permute-start | bytes 786440 | tf_op jit(solution)/shard_map/ppermute | solution.py:310
  23.0 13.0 %collective-permute-start = (bf16[32,32,128]{2,1,0:T(8,128)(2,1)S(1)}, bf16[32,32,128]{2,1,0:T(8,128)(2,1)S(1)}, u32[]{:S(2)}, u32[]{:S(2)}) collective-permute-start(bf16[32,32,128]{2,1,0:T(8,128)(2,1)S(1)} %bitcast.6), channel_id=1, source_target_pairs={{0,32},{8,232},{16,48},{24,248},{32,64},{40,8},{48,80},{56,24},{64... | collective-permute-start | bytes 786440 | tf_op jit(solution)/shard_map/ppermute | solution.py:339
  25.0 13.1 %collective-permute-start.5 = (bf16[32,32,128]{2,1,0:T(8,128)(2,1)S(1)}, bf16[32,32,128]{2,1,0:T(8,128)(2,1)S(1)}, u32[]{:S(2)}, u32[]{:S(2)}) collective-permute-start(bf16[32,32,128]{2,1,0:T(8,128)(2,1)S(1)} %collective-permute-done.4.refs_4_), channel_id=1, source_target_pairs={{0,32},{8,232},{16,48},{24,248},{32,64},{40,8},{48,80},{56,24},{64... | collective-permute-start | bytes 786440 | tf_op jit(solution)/shard_map/ppermute | solution.py:350
  27.0 4.2 %collective-permute-start.2 = (f32[32,128]{1,0:T(8,128)S(1)}, f32[32,128]{1,0:T(8,128)S(1)}, u32[]{:S(2)}, u32[]{:S(2)}) collective-permute-start(f32[32,128]{1,0:T(8,128)S(1)} %get-tuple-element.21), channel_id=1, source_target_pairs={{0,8},{8,0},{16,24},{24,16},{32,40},{40,32},{48,56},{56,48},{64,72... | collective-permute-start | bytes 49160 | tf_op jit(solution)/shard_map/ppermute | solution.py:326
  31.9 13.7 %all-to-all-start.1 = ((f32[8,32,128]{2,1,0:T(8,128)}), f32[8,32,128]{2,1,0:T(8,128)S(1)}, u32[]{:S(2)}, u32[]{:S(2)}) async-start(f32[8,32,128]{2,1,0:T(8,128)} %joined.1), calls=%async_computation.1 | async-start | bytes 262144 | tf_op jit(solution)/shard_map/all_to_all | solution.py:27
  36.1 9.9 %collective-permute-start.1 = (bf16[32,32,128]{2,1,0:T(8,128)(2,1)S(1)}, bf16[32,32,128]{2,1,0:T(8,128)(2,1)S(1)}, u32[]{:S(2)}, u32[]{:S(2)}) collective-permute-start(bf16[32,32,128]{2,1,0:T(8,128)(2,1)S(1)} %collective-permute-done.refs_1_), channel_id=1, source_target_pairs={{0,32},{8,232},{16,48},{24,248},{32,64},{40,8},{48,80},{56,24},{64... | collective-permute-start | bytes 786440 | tf_op jit(solution)/shard_map/ppermute | solution.py:339
  38.1 10.7 %collective-permute-start.6 = (bf16[32,32,128]{2,1,0:T(8,128)(2,1)S(1)}, bf16[32,32,128]{2,1,0:T(8,128)(2,1)S(1)}, u32[]{:S(2)}, u32[]{:S(2)}) collective-permute-start(bf16[32,32,128]{2,1,0:T(8,128)(2,1)S(1)} %collective-permute-done.5.refs_5_), channel_id=1, source_target_pairs={{0,32},{8,232},{16,48},{24,248},{32,64},{40,8},{48,80},{56,24},{64... | collective-permute-start | bytes 786440 | tf_op jit(solution)/shard_map/ppermute | solution.py:350
  39.5 0.7 copy-start.2
  40.2 0.7 copy-start.3
  40.9 0.7 copy-start.4
  45.9 9.9 %collective-permute-start.3 = (bf16[32,32,128]{2,1,0:T(8,128)(2,1)S(1)}, bf16[32,32,128]{2,1,0:T(8,128)(2,1)S(1)}, u32[]{:S(2)}, u32[]{:S(2)}) collective-permute-start(bf16[32,32,128]{2,1,0:T(8,128)(2,1)S(1)} %collective-permute-done.1.block.refs_2_), channel_id=1, source_target_pairs={{0,32},{8,232},{16,48},{24,248},{32,64},{40,8},{48,80},{56,24},{64... | collective-permute-start | bytes 786440 | tf_op jit(solution)/shard_map/ppermute | solution.py:339
  48.7 7.6 %collective-permute-start.8 = (bf16[32,32,128]{2,1,0:T(8,128)(2,1)S(1)}, bf16[32,32,128]{2,1,0:T(8,128)(2,1)S(1)}, u32[]{:S(2)}, u32[]{:S(2)}) collective-permute-start(bf16[32,32,128]{2,1,0:T(8,128)(2,1)S(1)} %collective-permute-done.6.block.refs_6_), channel_id=1, source_target_pairs={{0,32},{8,232},{16,48},{24,248},{32,64},{40,8},{48,80},{56,24},{64... | collective-permute-start | bytes 786440 | tf_op jit(solution)/shard_map/ppermute | solution.py:350
  48.7 10.1 %collective-permute-start.9 = (bf16[32,32,128]{2,1,0:T(8,128)(2,1)S(1)}, bf16[32,32,128]{2,1,0:T(8,128)(2,1)S(1)}, u32[]{:S(2)}, u32[]{:S(2)}) collective-permute-start(bf16[32,32,128]{2,1,0:T(8,128)(2,1)S(1)} %collective-permute-done.refs_1_), channel_id=1, source_target_pairs={{0,8},{8,0},{16,24},{24,16},{32,40},{40,32},{48,56},{56,48},{64,72... | collective-permute-start | bytes 786440 | tf_op jit(solution)/shard_map/ppermute | solution.py:346
  49.1 9.8 %collective-permute-start.10 = (bf16[32,32,128]{2,1,0:T(8,128)(2,1)S(1)}, bf16[32,32,128]{2,1,0:T(8,128)(2,1)S(1)}, u32[]{:S(2)}, u32[]{:S(2)}) collective-permute-start(bf16[32,32,128]{2,1,0:T(8,128)(2,1)S(1)} %collective-permute-done.5.refs_5_), channel_id=1, source_target_pairs={{0,8},{8,0},{16,24},{24,16},{32,40},{40,32},{48,56},{56,48},{64,72... | collective-permute-start | bytes 786440 | tf_op jit(solution)/shard_map/ppermute | solution.py:347
  49.3 14.4 %collective-permute-start.11 = (bf16[32,32,128]{2,1,0:T(8,128)(2,1)S(1)}, bf16[32,32,128]{2,1,0:T(8,128)(2,1)S(1)}, u32[]{:S(2)}, u32[]{:S(2)}) collective-permute-start(bf16[32,32,128]{2,1,0:T(8,128)(2,1)S(1)} %collective-permute-done.1.block.refs_2_), channel_id=1, source_target_pairs={{0,8},{8,0},{16,24},{24,16},{32,40},{40,32},{48,56},{56,48},{64,72... | collective-permute-start | bytes 786440 | tf_op jit(solution)/shard_map/ppermute | solution.py:346
  50.5 18.1 %all-to-all-start.2 = ((f32[32,32,128]{2,1,0:T(8,128)}), f32[32,32,128]{2,1,0:T(8,128)S(1)}, u32[]{:S(2)}, u32[]{:S(2)}) async-start(f32[32,32,128]{2,1,0:T(8,128)} %summed.1), calls=%async_computation.2 | async-start | bytes 1048576 | tf_op jit(solution)/shard_map/all_to_all | solution.py:27
  55.9 9.9 %collective-permute-start.7 = (bf16[32,32,128]{2,1,0:T(8,128)(2,1)S(1)}, bf16[32,32,128]{2,1,0:T(8,128)(2,1)S(1)}, u32[]{:S(2)}, u32[]{:S(2)}) collective-permute-start(bf16[32,32,128]{2,1,0:T(8,128)(2,1)S(1)} %collective-permute-done.3.refs_3_.block), channel_id=1, source_target_pairs={{0,32},{8,232},{16,48},{24,248},{32,64},{40,8},{48,80},{56,24},{64... | collective-permute-start | bytes 786440 | tf_op jit(solution)/shard_map/ppermute | solution.py:339
  56.3 7.3 %collective-permute-start.12 = (bf16[32,32,128]{2,1,0:T(8,128)(2,1)S(1)}, bf16[32,32,128]{2,1,0:T(8,128)(2,1)S(1)}, u32[]{:S(2)}, u32[]{:S(2)}) collective-permute-start(bf16[32,32,128]{2,1,0:T(8,128)(2,1)S(1)} %collective-permute-done.6.block.refs_6_), channel_id=1, source_target_pairs={{0,8},{8,0},{16,24},{24,16},{32,40},{40,32},{48,56},{56,48},{64,72... | collective-permute-start | bytes 786440 | tf_op jit(solution)/shard_map/ppermute | solution.py:347
  58.8 4.8 %collective-permute-start.13 = (bf16[32,32,128]{2,1,0:T(8,128)(2,1)S(1)}, bf16[32,32,128]{2,1,0:T(8,128)(2,1)S(1)}, u32[]{:S(2)}, u32[]{:S(2)}) collective-permute-start(bf16[32,32,128]{2,1,0:T(8,128)(2,1)S(1)} %collective-permute-done.3.refs_3_.block), channel_id=1, source_target_pairs={{0,8},{8,0},{16,24},{24,16},{32,40},{40,32},{48,56},{56,48},{64,72... | collective-permute-start | bytes 786440 | tf_op jit(solution)/shard_map/ppermute | solution.py:346
  58.9 4.7 %collective-permute-start.14 = (bf16[32,32,128]{2,1,0:T(8,128)(2,1)S(1)}, bf16[32,32,128]{2,1,0:T(8,128)(2,1)S(1)}, u32[]{:S(2)}, u32[]{:S(2)}) collective-permute-start(bf16[32,32,128]{2,1,0:T(8,128)(2,1)S(1)} %collective-permute-done.8.refs_0_), channel_id=1, source_target_pairs={{0,8},{8,0},{16,24},{24,16},{32,40},{40,32},{48,56},{56,48},{64,72... | collective-permute-start | bytes 786440 | tf_op jit(solution)/shard_map/ppermute | solution.py:347
  63.7 17.0 %copy-start = (bf16[256,256]{1,0:T(8,128)(2,1)S(1)}, bf16[256,256]{1,0:T(8,128)(2,1)}, u32[]{:S(2)}) copy-start(bf16[256,256]{1,0:T(8,128)(2,1)} %grad.3) | copy-start | bytes 393220
  63.7 17.0 %copy-start.1 = (bf16[256,256]{1,0:T(8,128)(2,1)S(1)}, bf16[256,256]{1,0:T(8,128)(2,1)}, u32[]{:S(2)}) copy-start(bf16[256,256]{1,0:T(8,128)(2,1)} %weight.3) | copy-start | bytes 393220
  65.8 1.6 %collective-permute-start.15 = (bf16[32,32,128]{2,1,0:T(8,128)(2,1)S(1)}, bf16[32,32,128]{2,1,0:T(8,128)(2,1)S(1)}, u32[]{:S(2)}, u32[]{:S(2)}) collective-permute-start(bf16[32,32,128]{2,1,0:T(8,128)(2,1)S(1)} %collective-permute-done.7.refs_0_), channel_id=1, source_target_pairs={{0,8},{8,0},{16,24},{24,16},{32,40},{40,32},{48,56},{56,48},{64,72... | collective-permute-start | bytes 786440 | tf_op jit(solution)/shard_map/ppermute | solution.py:361

commit v5 on v4

--- a/solution.py
+++ b/solution.py
@@ -324,6 +324,7 @@
     scale = (share_rows * block_total * copies) ** (-0.5)
     keep, give = half_sums(arrived)
     given = lax.ppermute(give, "blk", partner)
+    near, given = lax.optimization_barrier((near, given))
     nears, others = [near], [other]
     swaps, token = [], None
     part = exchange(joined(keep, given, planes), "blk", over_planes)

time: 82.1 us -> 81.6 us (level)
    ppermute x1, starting transfers between devices: 3.4 us -> 0.58 us  [on_device(): given = lax.ppermute(give, 'blk', partner)]
    all_to_all x2, starting transfers between devices: 9.48 us -> 12 us  [exchange(): return lax.all_to_all(x, axes, 0, 0, axis_index_groups=groups, tiled=True)]
    ppermute x3, starting transfers between devices: 3.07 us -> 0.85 us  [on_device(): lax.ppermute(other, 'blk', partner)]
    ppermute x3, starting transfers between devices: 0.78 us -> 2.86 us  [on_device(): lax.ppermute(near, 'blk', partner)]
where the time goes in v5:
time: 81.6 us; the launch traced here: 81.1 us
  blocking collectives  32 us (39%)
  starting transfers between devices  25.2 us (31%)
  Pallas kernels  12.4 us (15%)
  waiting for transfers between devices  8.64 us (11%)
  local copies, waits for them, and re-layouts  2.06 us (3%)
    all_to_all x2, blocking collectives, exchange(): return lax.all_to_all(x, axes, 0, 0, axis_index_groups=groups, tiled=True)  32 us
    all_to_all x2, starting transfers between devices, exchange(): return lax.all_to_all(x, axes, 0, 0, axis_index_groups=groups, tiled=True)  12 us
    ppermute x4, starting transfers between devices, on_device(): nears.append(lax.ppermute(near, 'blk', onward))  5.11 us
    pallas_call x1, Pallas kernels, spread_over(): pl.pallas_call(functools.partial(spread_kernel, sources, later), out_shap...  4.29 us
    all_to_all x2, waiting for transfers between devices, exchange(): return lax.all_to_all(x, axes, 0, 0, axis_index_groups=groups, tiled=True)  3.68 us
    ppermute x3, starting transfers between devices, on_device(): others.append(lax.ppermute(other, 'blk', onward))  3.38 us
    pallas_call x2, Pallas kernels, spread_on(): pl.pallas_call(functools.partial(spread_on_kernel, sources), out_shape=ja...  3.18 us
    ppermute x3, starting transfers between devices, on_device(): lax.ppermute(near, 'blk', partner)  2.86 us
  transfers between devices with their start and end apart: 18, of which 6 were waited for; matrix products, arithmetic and copies ran while one was open for 0% of the time, Pallas kernels for 11%

profile of v5, /device:TPU:8, one launch (start us, length us, event | category | flops | bytes accessed | tf_op | source)
XLA Modules:
  0.0 81.1 jit_solution(1531106833812806287)
XLA Ops:
  0.6 2.3 %opening.1 = bf16[16,6,32,128]{3,2,1,0:T(8,128)(2,1)} custom-call(bf16[256,256]{1,0:T(8,128)(2,1)} %features.1, bf16[256,256]{1,0:T(8,128)(2,1)} %aggregated.1, bf16[256,256]{1,0:T(8,128)(2,1)} %grad.3, bf16[256,256]{1,0:T(8,128)(2,1)} %weight.2), custom_call_target="tpu_custom_call" | custom-call | tf_op jit(solution)/shard_map/opening/pallas_call | solution.py:61
  2.9 20.0 %all_to_all.20.arrived = bf16[16,6,32,128]{3,2,1,0:T(8,128)(2,1)S(1)} all-to-all(bf16[16,6,32,128]{3,2,1,0:T(8,128)(2,1)} %opening.1), channel_id=1, replica_groups={{0,1,16,17,2,3,18,19,4,5,20,21,6,7,22,23},{8,9,24,25,10,11,26,27,12,13,..., dimensions={0} | all-to-all | bytes 1572864 | tf_op jit(solution)/shard_map/all_to_all | solution.py:27
  22.9 0.1 collective-permute-start.4
  23.0 0.1 half_sums.1
  23.1 0.6 collective-permute-start
  23.7 0.9 %collective-permute-done.got = f32[32,128]{1,0:T(8,128)S(1)} collective-permute-done((f32[32,128]{1,0:T(8,128)S(1)}, f32[32,128]{1,0:T(8,128)S(1)}, u32[]{:S(2)}, u32[]{:S(2)}) %collective-permute-start) | collective-permute-done | bytes 16416 | tf_op jit(solution)/shard_map/ppermute | solution.py:326
  24.6 1.9 %collective-permute-start.1 = (bf16[32,32,128]{2,1,0:T(8,128)(2,1)S(1)}, bf16[32,32,128]{2,1,0:T(8,128)(2,1)S(1)}, u32[]{:S(2)}, u32[]{:S(2)}) collective-permute-start(bf16[32,32,128]{2,1,0:T(8,128)(2,1)S(1)} %bitcast.6), channel_id=1, source_target_pairs={{0,32},{8,232},{16,48},{24,248},{32,64},{40,8},{48,80},{56,24},{64... | collective-permute-start | bytes 786440 | tf_op jit(solution)/shard_map/ppermute | solution.py:340
  26.5 0.0 collective-permute-done.4.refs_4_
  26.5 1.9 %collective-permute-start.5 = (bf16[32,32,128]{2,1,0:T(8,128)(2,1)S(1)}, bf16[32,32,128]{2,1,0:T(8,128)(2,1)S(1)}, u32[]{:S(2)}, u32[]{:S(2)}) collective-permute-start(bf16[32,32,128]{2,1,0:T(8,128)(2,1)S(1)} %collective-permute-done.4.refs_4_), channel_id=1, source_target_pairs={{0,32},{8,232},{16,48},{24,248},{32,64},{40,8},{48,80},{56,24},{64... | collective-permute-start | bytes 786440 | tf_op jit(solution)/shard_map/ppermute | solution.py:351
  28.4 0.7 joined.1
  29.1 6.7 %all-to-all-start.1 = ((f32[8,32,128]{2,1,0:T(8,128)}), f32[8,32,128]{2,1,0:T(8,128)S(1)}, u32[]{:S(2)}, u32[]{:S(2)}) async-start(f32[8,32,128]{2,1,0:T(8,128)} %joined.1), calls=%async_computation.1 | async-start | bytes 262144 | tf_op jit(solution)/shard_map/all_to_all | solution.py:27
  35.7 0.0 collective-permute-done.1.refs_1_
  35.8 2.0 %collective-permute-start.2 = (bf16[32,32,128]{2,1,0:T(8,128)(2,1)S(1)}, bf16[32,32,128]{2,1,0:T(8,128)(2,1)S(1)}, u32[]{:S(2)}, u32[]{:S(2)}) collective-permute-start(bf16[32,32,128]{2,1,0:T(8,128)(2,1)S(1)} %collective-permute-done.1.refs_1_), channel_id=1, source_target_pairs={{0,32},{8,232},{16,48},{24,248},{32,64},{40,8},{48,80},{56,24},{64... | collective-permute-start | bytes 786440 | tf_op jit(solution)/shard_map/ppermute | solution.py:340
  37.8 0.0 collective-permute-done.5.refs_5_
  37.8 1.5 %collective-permute-start.6 = (bf16[32,32,128]{2,1,0:T(8,128)(2,1)S(1)}, bf16[32,32,128]{2,1,0:T(8,128)(2,1)S(1)}, u32[]{:S(2)}, u32[]{:S(2)}) collective-permute-start(bf16[32,32,128]{2,1,0:T(8,128)(2,1)S(1)} %collective-permute-done.5.refs_5_), channel_id=1, source_target_pairs={{0,32},{8,232},{16,48},{24,248},{32,64},{40,8},{48,80},{56,24},{64... | collective-permute-start | bytes 786440 | tf_op jit(solution)/shard_map/ppermute | solution.py:351
  39.2 0.7 copy-done.2
  39.9 0.7 copy-done.3
  40.6 0.7 copy-done.4
  41.3 3.7 %all-to-all-done.1.parts = f32[8,32,128]{2,1,0:T(8,128)S(1)} async-done(((f32[8,32,128]{2,1,0:T(8,128)}), f32[8,32,128]{2,1,0:T(8,128)S(1)}, u32[]{:S(2)}, u32[]{:S(2)}) %all-to-all-start.1) | async-done | bytes 131104 | tf_op jit(solution)/shard_map/all_to_all | solution.py:27
  44.9 0.4 collective-permute-done.2.block.refs_2_
  45.3 0.8 %collective-permute-start.3 = (bf16[32,32,128]{2,1,0:T(8,128)(2,1)S(1)}, bf16[32,32,128]{2,1,0:T(8,128)(2,1)S(1)}, u32[]{:S(2)}, u32[]{:S(2)}) collective-permute-start(bf16[32,32,128]{2,1,0:T(8,128)(2,1)S(1)} %collective-permute-done.2.block.refs_2_), channel_id=1, source_target_pairs={{0,32},{8,232},{16,48},{24,248},{32,64},{40,8},{48,80},{56,24},{64... | collective-permute-start | bytes 786440 | tf_op jit(solution)/shard_map/ppermute | solution.py:340
  46.2 2.0 %collective-permute-done.6.block.refs_6_ = bf16[32,32,128]{2,1,0:T(8,128)(2,1)S(1)} collective-permute-done((bf16[32,32,128]{2,1,0:T(8,128)(2,1)S(1)}, bf16[32,32,128]{2,1,0:T(8,128)(2,1)S(1)}, u32[]{:S(2)}, u32[]{:S(2)}) %collective-permute-start.6) | collective-permute-done | bytes 262176 | tf_op jit(solution)/shard_map/ppermute | solution.py:351
  48.1 0.0 collective-permute-start.8
  48.1 0.2 collective-permute-start.9
  48.3 0.3 collective-permute-start.10
  48.7 0.2 collective-permute-start.11
  48.8 0.9 %summed.1 = f32[32,32,128]{2,1,0:T(8,128)} custom-call(f32[8,32,128]{2,1,0:T(8,128)S(1)} %all-to-all-done.1.parts), custom_call_target="tpu_custom_call" | custom-call | tf_op jit(solution)/shard_map/summed/pallas_call | solution.py:153
  49.7 5.4 %all-to-all-start.2 = ((f32[32,32,128]{2,1,0:T(8,128)}), f32[32,32,128]{2,1,0:T(8,128)S(1)}, u32[]{:S(2)}, u32[]{:S(2)}) async-start(f32[32,32,128]{2,1,0:T(8,128)} %summed.1), calls=%async_computation.2 | async-start | bytes 1048576 | tf_op jit(solution)/shard_map/all_to_all | solution.py:27
  55.1 0.0 collective-permute-done.3.refs_3_.block
  55.1 0.2 collective-permute-start.12
  55.3 0.4 collective-permute-done.8.refs_0_
  55.7 0.3 collective-permute-start.7
  56.1 0.0 collective-permute-done.9.refs_1_
  56.1 2.5 %collective-permute-start.13 = (bf16[32,32,128]{2,1,0:T(8,128)(2,1)S(1)}, bf16[32,32,128]{2,1,0:T(8,128)(2,1)S(1)}, u32[]{:S(2)}, u32[]{:S(2)}) collective-permute-start(bf16[32,32,128]{2,1,0:T(8,128)(2,1)S(1)} %collective-permute-done.3.refs_3_.block), channel_id=1, source_target_pairs={{0,8},{8,0},{16,24},{24,16},{32,40},{40,32},{48,56},{56,48},{64,72... | collective-permute-start | bytes 786440 | tf_op jit(solution)/shard_map/ppermute | solution.py:347
  58.6 0.3 collective-permute-start.14
  58.9 4.3 %spread.1 = (f32[16,32,128]{2,1,0:T(8,128)S(1)}, bf16[32,8,128,128]{3,2,1,0:T(8,128)(2,1)S(1)}) custom-call(s32[8,32]{1,0:T(8,128)S(1)} %codes.1.before, bf16[1,32,8,128,128]{4,3,2,1,0:T(8,128)(2,1)} %tiles.1, bf16[32,32,128]{2,1,0:T(8,128)(2,1)S(1)} %bitcast.7, bf16[32,32,128]{2,1,0:T(8,128)(2,1)S(1)} %collective-permute-done.1.refs_1_, ...), custom_call_target="tpu_custom_call" | custom-call | flops 20000000000 | tf_op jit(solution)/shard_map/spread/pallas_call | solution.py:234
  63.2 0.0 collective-permute-done.11.refs_3_
  63.2 0.0 collective-permute-done.12.refs_4_
  63.2 0.0 collective-permute-done.14.refs_6_
  63.2 0.0 copy-start
  63.2 0.0 copy-start.1
  63.2 2.1 %spread_on.2.begun = f32[16,32,128]{2,1,0:T(8,128)S(1)} custom-call(s32[8,32]{1,0:T(8,128)S(1)} %codes.1.before, bf16[32,8,128,128]{3,2,1,0:T(8,128)(2,1)S(1)} %get-tuple-element.31.tiles, f32[16,32,128]{2,1,0:T(8,128)S(1)} %get-tuple-element.32.begun, bf16[32,32,128]{2,1,0:T(8,128)(2,1)S(1)} %collective-permute-done.8.refs_0_, ...), custom_call_target="tpu_custom_call" | custom-call | flops 1 | tf_op jit(solution)/shard_map/spread_on/pallas_call | solution.py:266
  65.3 0.3 collective-permute-start.15
  65.6 1.3 %collective-permute-done.15.refs_1_ = bf16[32,32,128]{2,1,0:T(8,128)(2,1)S(1)} collective-permute-done((bf16[32,32,128]{2,1,0:T(8,128)(2,1)S(1)}, bf16[32,32,128]{2,1,0:T(8,128)(2,1)S(1)}, u32[]{:S(2)}, u32[]{:S(2)}) %collective-permute-start.15) | collective-permute-done | bytes 262176 | tf_op jit(solution)/shard_map/ppermute | solution.py:362
  66.9 1.1 %spread_on.3 = f32[16,32,128]{2,1,0:T(8,128)S(1)} custom-call(s32[8,32]{1,0:T(8,128)S(1)} %codes.1.before, bf16[32,8,128,128]{3,2,1,0:T(8,128)(2,1)S(1)} %get-tuple-element.31.tiles, f32[16,32,128]{2,1,0:T(8,128)S(1)} %spread_on.2.begun, bf16[32,32,128]{2,1,0:T(8,128)(2,1)S(1)} %collective-permute-done.7.refs_0_, ...), custom_call_target="tpu_custom_call" | custom-call | flops 1 | tf_op jit(solution)/shard_map/spread_on/pallas_call | solution.py:266
  68.1 0.0 all-to-all-done.2.whole
  68.1 12.0 %all_to_all.21.parts = f32[8,2,32,128]{3,2,1,0:T(8,128)S(1)} all-to-all(f32[8,2,32,128]{3,2,1,0:T(8,128)S(1)} %bitcast.4), channel_id=1, replica_groups=mesh['blk'=32,'rep'=8] {'rep'}, dimensions={0} | all-to-all | bytes 524288 | tf_op jit(solution)/shard_map/all_to_all | solution.py:27
  80.1 1.0 %result.1 = (f32[256,256]{1,0:T(8,128)}, f32[256,256]{1,0:T(8,128)}, f32[256,256]{1,0:T(8,128)}) custom-call(f32[8,2,32,128]{3,2,1,0:T(8,128)S(1)} %all_to_all.21.parts, f32[32,32,128]{2,1,0:T(8,128)S(1)} %all-to-all-done.2.whole, bf16[256,256]{1,0:T(8,128)(2,1)S(1)} %copy-done, bf16[256,256]{1,0:T(8,128)(2,1)S(1)} %copy-done.1, s32[8,128]{1,0:T(8,128)S(1)} %gate.5.token), custom_call_target="tpu_custom_call" | custom-call | tf_op jit(solution)/shard_map/result/pallas_call | solution.py:180
  (13 shorter events, 0.0 us)
Async XLA Ops:
  22.9 3.6 %collective-permute-start.4 = (bf16[32,32,128]{2,1,0:T(8,128)(2,1)S(1)}, bf16[32,32,128]{2,1,0:T(8,128)(2,1)S(1)}, u32[]{:S(2)}, u32[]{:S(2)}) collective-permute-start(bf16[32,32,128]{2,1,0:T(8,128)(2,1)S(1)} %bitcast.5), channel_id=1, source_target_pairs={{0,8},{8,0},{16,24},{24,16},{32,40},{40,32},{48,56},{56,48},{64,72... | collective-permute-start | bytes 786440 | tf_op jit(solution)/shard_map/ppermute | solution.py:310
  23.1 1.5 %collective-permute-start = (f32[32,128]{1,0:T(8,128)S(1)}, f32[32,128]{1,0:T(8,128)S(1)}, u32[]{:S(2)}, u32[]{:S(2)}) collective-permute-start(f32[32,128]{1,0:T(8,128)S(1)} %get-tuple-element.22), channel_id=1, source_target_pairs={{0,8},{8,0},{16,24},{24,16},{32,40},{40,32},{48,56},{56,48},{64,72... | collective-permute-start | bytes 49160 | tf_op jit(solution)/shard_map/ppermute | solution.py:326
  24.6 11.2 %collective-permute-start.1 = (bf16[32,32,128]{2,1,0:T(8,128)(2,1)S(1)}, bf16[32,32,128]{2,1,0:T(8,128)(2,1)S(1)}, u32[]{:S(2)}, u32[]{:S(2)}) collective-permute-start(bf16[32,32,128]{2,1,0:T(8,128)(2,1)S(1)} %bitcast.6), channel_id=1, source_target_pairs={{0,32},{8,232},{16,48},{24,248},{32,64},{40,8},{48,80},{56,24},{64... | collective-permute-start | bytes 786440 | tf_op jit(solution)/shard_map/ppermute | solution.py:340
  26.5 11.3 %collective-permute-start.5 = (bf16[32,32,128]{2,1,0:T(8,128)(2,1)S(1)}, bf16[32,32,128]{2,1,0:T(8,128)(2,1)S(1)}, u32[]{:S(2)}, u32[]{:S(2)}) collective-permute-start(bf16[32,32,128]{2,1,0:T(8,128)(2,1)S(1)} %collective-permute-done.4.refs_4_), channel_id=1, source_target_pairs={{0,32},{8,232},{16,48},{24,248},{32,64},{40,8},{48,80},{56,24},{64... | collective-permute-start | bytes 786440 | tf_op jit(solution)/shard_map/ppermute | solution.py:351
  29.1 15.9 %all-to-all-start.1 = ((f32[8,32,128]{2,1,0:T(8,128)}), f32[8,32,128]{2,1,0:T(8,128)S(1)}, u32[]{:S(2)}, u32[]{:S(2)}) async-start(f32[8,32,128]{2,1,0:T(8,128)} %joined.1), calls=%async_computation.1 | async-start | bytes 262144 | tf_op jit(solution)/shard_map/all_to_all | solution.py:27
  35.8 9.6 %collective-permute-start.2 = (bf16[32,32,128]{2,1,0:T(8,128)(2,1)S(1)}, bf16[32,32,128]{2,1,0:T(8,128)(2,1)S(1)}, u32[]{:S(2)}, u32[]{:S(2)}) collective-permute-start(bf16[32,32,128]{2,1,0:T(8,128)(2,1)S(1)} %collective-permute-done.1.refs_1_), channel_id=1, source_target_pairs={{0,32},{8,232},{16,48},{24,248},{32,64},{40,8},{48,80},{56,24},{64... | collective-permute-start | bytes 786440 | tf_op jit(solution)/shard_map/ppermute | solution.py:340
  37.8 10.4 %collective-permute-start.6 = (bf16[32,32,128]{2,1,0:T(8,128)(2,1)S(1)}, bf16[32,32,128]{2,1,0:T(8,128)(2,1)S(1)}, u32[]{:S(2)}, u32[]{:S(2)}) collective-permute-start(bf16[32,32,128]{2,1,0:T(8,128)(2,1)S(1)} %collective-permute-done.5.refs_5_), channel_id=1, source_target_pairs={{0,32},{8,232},{16,48},{24,248},{32,64},{40,8},{48,80},{56,24},{64... | collective-permute-start | bytes 786440 | tf_op jit(solution)/shard_map/ppermute | solution.py:351
  39.2 0.7 copy-start.2
  39.9 0.7 copy-start.3
  40.6 0.7 copy-start.4
  45.3 9.7 %collective-permute-start.3 = (bf16[32,32,128]{2,1,0:T(8,128)(2,1)S(1)}, bf16[32,32,128]{2,1,0:T(8,128)(2,1)S(1)}, u32[]{:S(2)}, u32[]{:S(2)}) collective-permute-start(bf16[32,32,128]{2,1,0:T(8,128)(2,1)S(1)} %collective-permute-done.2.block.refs_2_), channel_id=1, source_target_pairs={{0,32},{8,232},{16,48},{24,248},{32,64},{40,8},{48,80},{56,24},{64... | collective-permute-start | bytes 786440 | tf_op jit(solution)/shard_map/ppermute | solution.py:340
  48.1 7.6 %collective-permute-start.8 = (bf16[32,32,128]{2,1,0:T(8,128)(2,1)S(1)}, bf16[32,32,128]{2,1,0:T(8,128)(2,1)S(1)}, u32[]{:S(2)}, u32[]{:S(2)}) collective-permute-start(bf16[32,32,128]{2,1,0:T(8,128)(2,1)S(1)} %collective-permute-done.6.block.refs_6_), channel_id=1, source_target_pairs={{0,32},{8,232},{16,48},{24,248},{32,64},{40,8},{48,80},{56,24},{64... | collective-permute-start | bytes 786440 | tf_op jit(solution)/shard_map/ppermute | solution.py:351
  48.1 7.9 %collective-permute-start.9 = (bf16[32,32,128]{2,1,0:T(8,128)(2,1)S(1)}, bf16[32,32,128]{2,1,0:T(8,128)(2,1)S(1)}, u32[]{:S(2)}, u32[]{:S(2)}) collective-permute-start(bf16[32,32,128]{2,1,0:T(8,128)(2,1)S(1)} %collective-permute-done.1.refs_1_), channel_id=1, source_target_pairs={{0,8},{8,0},{16,24},{24,16},{32,40},{40,32},{48,56},{56,48},{64,72... | collective-permute-start | bytes 786440 | tf_op jit(solution)/shard_map/ppermute | solution.py:347
  48.3 10.3 %collective-permute-start.10 = (bf16[32,32,128]{2,1,0:T(8,128)(2,1)S(1)}, bf16[32,32,128]{2,1,0:T(8,128)(2,1)S(1)}, u32[]{:S(2)}, u32[]{:S(2)}) collective-permute-start(bf16[32,32,128]{2,1,0:T(8,128)(2,1)S(1)} %collective-permute-done.5.refs_5_), channel_id=1, source_target_pairs={{0,8},{8,0},{16,24},{24,16},{32,40},{40,32},{48,56},{56,48},{64,72... | collective-permute-start | bytes 786440 | tf_op jit(solution)/shard_map/ppermute | solution.py:348
  48.7 14.5 %collective-permute-start.11 = (bf16[32,32,128]{2,1,0:T(8,128)(2,1)S(1)}, bf16[32,32,128]{2,1,0:T(8,128)(2,1)S(1)}, u32[]{:S(2)}, u32[]{:S(2)}) collective-permute-start(bf16[32,32,128]{2,1,0:T(8,128)(2,1)S(1)} %collective-permute-done.2.block.refs_2_), channel_id=1, source_target_pairs={{0,8},{8,0},{16,24},{24,16},{32,40},{40,32},{48,56},{56,48},{64,72... | collective-permute-start | bytes 786440 | tf_op jit(solution)/shard_map/ppermute | solution.py:347
  49.7 18.4 %all-to-all-start.2 = ((f32[32,32,128]{2,1,0:T(8,128)}), f32[32,32,128]{2,1,0:T(8,128)S(1)}, u32[]{:S(2)}, u32[]{:S(2)}) async-start(f32[32,32,128]{2,1,0:T(8,128)} %summed.1), calls=%async_computation.2 | async-start | bytes 1048576 | tf_op jit(solution)/shard_map/all_to_all | solution.py:27
  55.1 8.1 %collective-permute-start.12 = (bf16[32,32,128]{2,1,0:T(8,128)(2,1)S(1)}, bf16[32,32,128]{2,1,0:T(8,128)(2,1)S(1)}, u32[]{:S(2)}, u32[]{:S(2)}) collective-permute-start(bf16[32,32,128]{2,1,0:T(8,128)(2,1)S(1)} %collective-permute-done.6.block.refs_6_), channel_id=1, source_target_pairs={{0,8},{8,0},{16,24},{24,16},{32,40},{40,32},{48,56},{56,48},{64,72... | collective-permute-start | bytes 786440 | tf_op jit(solution)/shard_map/ppermute | solution.py:348
  55.7 9.6 %collective-permute-start.7 = (bf16[32,32,128]{2,1,0:T(8,128)(2,1)S(1)}, bf16[32,32,128]{2,1,0:T(8,128)(2,1)S(1)}, u32[]{:S(2)}, u32[]{:S(2)}) collective-permute-start(bf16[32,32,128]{2,1,0:T(8,128)(2,1)S(1)} %collective-permute-done.3.refs_3_.block), channel_id=1, source_target_pairs={{0,32},{8,232},{16,48},{24,248},{32,64},{40,8},{48,80},{56,24},{64... | collective-permute-start | bytes 786440 | tf_op jit(solution)/shard_map/ppermute | solution.py:340
  56.1 7.1 %collective-permute-start.13 = (bf16[32,32,128]{2,1,0:T(8,128)(2,1)S(1)}, bf16[32,32,128]{2,1,0:T(8,128)(2,1)S(1)}, u32[]{:S(2)}, u32[]{:S(2)}) collective-permute-start(bf16[32,32,128]{2,1,0:T(8,128)(2,1)S(1)} %collective-permute-done.3.refs_3_.block), channel_id=1, source_target_pairs={{0,8},{8,0},{16,24},{24,16},{32,40},{40,32},{48,56},{56,48},{64,72... | collective-permute-start | bytes 786440 | tf_op jit(solution)/shard_map/ppermute | solution.py:347
  58.6 4.6 %collective-permute-start.14 = (bf16[32,32,128]{2,1,0:T(8,128)(2,1)S(1)}, bf16[32,32,128]{2,1,0:T(8,128)(2,1)S(1)}, u32[]{:S(2)}, u32[]{:S(2)}) collective-permute-start(bf16[32,32,128]{2,1,0:T(8,128)(2,1)S(1)} %collective-permute-done.8.refs_0_), channel_id=1, source_target_pairs={{0,8},{8,0},{16,24},{24,16},{32,40},{40,32},{48,56},{56,48},{64,72... | collective-permute-start | bytes 786440 | tf_op jit(solution)/shard_map/ppermute | solution.py:348
  63.2 16.9 %copy-start = (bf16[256,256]{1,0:T(8,128)(2,1)S(1)}, bf16[256,256]{1,0:T(8,128)(2,1)}, u32[]{:S(2)}) copy-start(bf16[256,256]{1,0:T(8,128)(2,1)} %grad.3) | copy-start | bytes 393220
  63.2 16.9 %copy-start.1 = (bf16[256,256]{1,0:T(8,128)(2,1)S(1)}, bf16[256,256]{1,0:T(8,128)(2,1)}, u32[]{:S(2)}) copy-start(bf16[256,256]{1,0:T(8,128)(2,1)} %weight.3) | copy-start | bytes 393220
  65.3 1.6 %collective-permute-start.15 = (bf16[32,32,128]{2,1,0:T(8,128)(2,1)S(1)}, bf16[32,32,128]{2,1,0:T(8,128)(2,1)S(1)}, u32[]{:S(2)}, u32[]{:S(2)}) collective-permute-start(bf16[32,32,128]{2,1,0:T(8,128)(2,1)S(1)} %collective-permute-done.7.refs_0_), channel_id=1, source_target_pairs={{0,8},{8,0},{16,24},{24,16},{32,40},{40,32},{48,56},{56,48},{64,72... | collective-permute-start | bytes 786440 | tf_op jit(solution)/shard_map/ppermute | solution.py:362

commit v6 on v4

--- a/solution.py
+++ b/solution.py
@@ -12,7 +12,7 @@
 LOW = 2
 MEMBERS = 32
 RUN = 4
-TOGETHER = 4
+TOGETHER = 7
 BOTH = ("blk", "rep")
 AS_A_HOP = pl.CostEstimate(flops=100000000, bytes_accessed=0, transcendentals=0)
 AS_SHORT = pl.CostEstimate(flops=1, bytes_accessed=0, transcendentals=0)
@@ -324,9 +324,11 @@
     scale = (share_rows * block_total * copies) ** (-0.5)
     keep, give = half_sums(arrived)
     given = lax.ppermute(give, "blk", partner)
+    part = joined(keep, given, planes)
+    near, other, part = lax.optimization_barrier((near, other, part))
     nears, others = [near], [other]
     swaps, token = [], None
-    part = exchange(joined(keep, given, planes), "blk", over_planes)
+    part = exchange(part, "blk", over_planes)
     for step in range(steps):
         near, other = nears[-1], others[-1]
         if step == 2:

time: 82.1 us -> 81.6 us (level)
    ppermute x3, starting transfers between devices: 0.78 us -> 3.67 us  [on_device(): lax.ppermute(near, 'blk', partner)]
    ppermute x1, starting transfers between devices: 3.4 us -> 0.58 us  [on_device(): given = lax.ppermute(give, 'blk', partner)]
    ppermute x3, starting transfers between devices: 3.07 us -> 0.51 us  [on_device(): lax.ppermute(other, 'blk', partner)]
    all_to_all x2, starting transfers between devices: 9.48 us -> 12 us  [exchange(): return lax.all_to_all(x, axes, 0, 0, axis_index_groups=groups, tiled=True)]
where the time goes in v6:
time: 81.6 us; the launch traced here: 81.1 us
  blocking collectives  32 us (39%)
  starting transfers between devices  25 us (31%)
  Pallas kernels  12.4 us (15%)
  waiting for transfers between devices  8.84 us (11%)
  local copies, waits for them, and re-layouts  2.06 us (3%)
    all_to_all x2, blocking collectives, exchange(): return lax.all_to_all(x, axes, 0, 0, axis_index_groups=groups, tiled=True)  32 us
    all_to_all x2, starting transfers between devices, exchange(): return lax.all_to_all(x, axes, 0, 0, axis_index_groups=groups, tiled=True)  12 us
    ppermute x4, starting transfers between devices, on_device(): nears.append(lax.ppermute(near, 'blk', onward))  4.93 us
    pallas_call x1, Pallas kernels, spread_over(): pl.pallas_call(functools.partial(spread_kernel, sources, later), out_shap...  4.29 us
    ppermute x3, starting transfers between devices, on_device(): lax.ppermute(near, 'blk', partner)  3.67 us
    all_to_all x2, waiting for transfers between devices, exchange(): return lax.all_to_all(x, axes, 0, 0, axis_index_groups=groups, tiled=True)  3.44 us
    pallas_call x2, Pallas kernels, spread_on(): pl.pallas_call(functools.partial(spread_on_kernel, sources), out_shape=ja...  3.21 us
    ppermute x3, starting transfers between devices, on_device(): others.append(lax.ppermute(other, 'blk', onward))  2.9 us
  transfers between devices with their start and end apart: 18, of which 6 were waited for; matrix products, arithmetic and copies ran while one was open for 0% of the time, Pallas kernels for 11%

profile of v6, /device:TPU:8, one launch (start us, length us, event | category | flops | bytes accessed | tf_op | source)
XLA Modules:
  0.0 81.1 jit_solution(18396657437434740761)
XLA Ops:
  0.6 2.3 %opening.1 = bf16[16,6,32,128]{3,2,1,0:T(8,128)(2,1)} custom-call(bf16[256,256]{1,0:T(8,128)(2,1)} %features.1, bf16[256,256]{1,0:T(8,128)(2,1)} %aggregated.1, bf16[256,256]{1,0:T(8,128)(2,1)} %grad.3, bf16[256,256]{1,0:T(8,128)(2,1)} %weight.2), custom_call_target="tpu_custom_call" | custom-call | tf_op jit(solution)/shard_map/opening/pallas_call | solution.py:61
  2.9 20.0 %all_to_all.20.arrived = bf16[16,6,32,128]{3,2,1,0:T(8,128)(2,1)S(1)} all-to-all(bf16[16,6,32,128]{3,2,1,0:T(8,128)(2,1)} %opening.1), channel_id=1, replica_groups={{0,1,16,17,2,3,18,19,4,5,20,21,6,7,22,23},{8,9,24,25,10,11,26,27,12,13,..., dimensions={0} | all-to-all | bytes 1572864 | tf_op jit(solution)/shard_map/all_to_all | solution.py:27
  22.9 0.1 collective-permute-start
  23.0 0.1 half_sums.1
  23.1 0.6 collective-permute-start.1
  23.7 0.9 %collective-permute-done.1.got = f32[32,128]{1,0:T(8,128)S(1)} collective-permute-done((f32[32,128]{1,0:T(8,128)S(1)}, f32[32,128]{1,0:T(8,128)S(1)}, u32[]{:S(2)}, u32[]{:S(2)}) %collective-permute-start.1) | collective-permute-done | bytes 16416 | tf_op jit(solution)/shard_map/ppermute | solution.py:326
  24.6 0.7 joined.1
  25.2 0.0 collective-permute-done.refs_4_
  25.2 1.9 %collective-permute-start.2 = (bf16[32,32,128]{2,1,0:T(8,128)(2,1)S(1)}, bf16[32,32,128]{2,1,0:T(8,128)(2,1)S(1)}, u32[]{:S(2)}, u32[]{:S(2)}) collective-permute-start(bf16[32,32,128]{2,1,0:T(8,128)(2,1)S(1)} %bitcast.6), channel_id=1, source_target_pairs={{0,32},{8,232},{16,48},{24,248},{32,64},{40,8},{48,80},{56,24},{64... | collective-permute-start | bytes 786440 | tf_op jit(solution)/shard_map/ppermute | solution.py:341
  27.2 1.9 %collective-permute-start.5 = (bf16[32,32,128]{2,1,0:T(8,128)(2,1)S(1)}, bf16[32,32,128]{2,1,0:T(8,128)(2,1)S(1)}, u32[]{:S(2)}, u32[]{:S(2)}) collective-permute-start(bf16[32,32,128]{2,1,0:T(8,128)(2,1)S(1)} %collective-permute-done.refs_4_), channel_id=1, source_target_pairs={{0,32},{8,232},{16,48},{24,248},{32,64},{40,8},{48,80},{56,24},{64... | collective-permute-start | bytes 786440 | tf_op jit(solution)/shard_map/ppermute | solution.py:352
  29.1 6.7 %all-to-all-start.1 = ((f32[8,32,128]{2,1,0:T(8,128)}), f32[8,32,128]{2,1,0:T(8,128)S(1)}, u32[]{:S(2)}, u32[]{:S(2)}) async-start(f32[8,32,128]{2,1,0:T(8,128)} %joined.1), calls=%async_computation.1 | async-start | bytes 262144 | tf_op jit(solution)/shard_map/all_to_all | solution.py:27
  35.7 0.0 collective-permute-done.2.refs_1_
  35.8 2.0 %collective-permute-start.3 = (bf16[32,32,128]{2,1,0:T(8,128)(2,1)S(1)}, bf16[32,32,128]{2,1,0:T(8,128)(2,1)S(1)}, u32[]{:S(2)}, u32[]{:S(2)}) collective-permute-start(bf16[32,32,128]{2,1,0:T(8,128)(2,1)S(1)} %collective-permute-done.2.refs_1_), channel_id=1, source_target_pairs={{0,32},{8,232},{16,48},{24,248},{32,64},{40,8},{48,80},{56,24},{64... | collective-permute-start | bytes 786440 | tf_op jit(solution)/shard_map/ppermute | solution.py:341
  37.8 0.5 collective-permute-done.5.refs_5_
  38.3 1.0 %collective-permute-start.6 = (bf16[32,32,128]{2,1,0:T(8,128)(2,1)S(1)}, bf16[32,32,128]{2,1,0:T(8,128)(2,1)S(1)}, u32[]{:S(2)}, u32[]{:S(2)}) collective-permute-start(bf16[32,32,128]{2,1,0:T(8,128)(2,1)S(1)} %collective-permute-done.5.refs_5_), channel_id=1, source_target_pairs={{0,32},{8,232},{16,48},{24,248},{32,64},{40,8},{48,80},{56,24},{64... | collective-permute-start | bytes 786440 | tf_op jit(solution)/shard_map/ppermute | solution.py:352
  39.2 0.7 copy-done.2
  39.9 0.7 copy-done.3
  40.6 0.7 copy-done.4
  41.3 3.4 %all-to-all-done.1.parts = f32[8,32,128]{2,1,0:T(8,128)S(1)} async-done(((f32[8,32,128]{2,1,0:T(8,128)}), f32[8,32,128]{2,1,0:T(8,128)S(1)}, u32[]{:S(2)}, u32[]{:S(2)}) %all-to-all-start.1) | async-done | bytes 131104 | tf_op jit(solution)/shard_map/all_to_all | solution.py:27
  44.7 0.6 collective-permute-done.3.block.refs_2_
  45.3 0.7 collective-permute-start.4
  46.1 2.1 %collective-permute-done.6.block.refs_6_ = bf16[32,32,128]{2,1,0:T(8,128)(2,1)S(1)} collective-permute-done((bf16[32,32,128]{2,1,0:T(8,128)(2,1)S(1)}, bf16[32,32,128]{2,1,0:T(8,128)(2,1)S(1)}, u32[]{:S(2)}, u32[]{:S(2)}) %collective-permute-start.6) | collective-permute-done | bytes 262176 | tf_op jit(solution)/shard_map/ppermute | solution.py:352
  48.1 0.0 collective-permute-start.8
  48.1 0.6 collective-permute-start.9
  48.8 0.0 collective-permute-start.10
  48.8 0.5 collective-permute-start.11
  49.3 0.9 %summed.1 = f32[32,32,128]{2,1,0:T(8,128)} custom-call(f32[8,32,128]{2,1,0:T(8,128)S(1)} %all-to-all-done.1.parts), custom_call_target="tpu_custom_call" | custom-call | tf_op jit(solution)/shard_map/summed/pallas_call | solution.py:153
  50.2 5.4 %all-to-all-start.2 = ((f32[32,32,128]{2,1,0:T(8,128)}), f32[32,32,128]{2,1,0:T(8,128)S(1)}, u32[]{:S(2)}, u32[]{:S(2)}) async-start(f32[32,32,128]{2,1,0:T(8,128)} %summed.1), calls=%async_computation.2 | async-start | bytes 1048576 | tf_op jit(solution)/shard_map/all_to_all | solution.py:27
  55.5 0.0 collective-permute-done.4.refs_3_.block
  55.6 0.2 collective-permute-start.12
  55.8 0.0 collective-permute-done.8.refs_0_
  55.8 0.3 collective-permute-start.7
  56.1 0.0 collective-permute-done.9.refs_1_
  56.1 2.5 %collective-permute-start.13 = (bf16[32,32,128]{2,1,0:T(8,128)(2,1)S(1)}, bf16[32,32,128]{2,1,0:T(8,128)(2,1)S(1)}, u32[]{:S(2)}, u32[]{:S(2)}) collective-permute-start(bf16[32,32,128]{2,1,0:T(8,128)(2,1)S(1)} %collective-permute-done.4.refs_3_.block), channel_id=1, source_target_pairs={{0,8},{8,0},{16,24},{24,16},{32,40},{40,32},{48,56},{56,48},{64,72... | collective-permute-start | bytes 786440 | tf_op jit(solution)/shard_map/ppermute | solution.py:348
  58.6 0.0 collective-permute-done.10.refs_2_
  58.6 0.3 collective-permute-start.14
  58.9 4.3 %spread.1 = (f32[16,32,128]{2,1,0:T(8,128)S(1)}, bf16[32,8,128,128]{3,2,1,0:T(8,128)(2,1)S(1)}) custom-call(s32[8,32]{1,0:T(8,128)S(1)} %codes.1.before, bf16[1,32,8,128,128]{4,3,2,1,0:T(8,128)(2,1)} %tiles.1, bf16[32,32,128]{2,1,0:T(8,128)(2,1)S(1)} %bitcast.7, bf16[32,32,128]{2,1,0:T(8,128)(2,1)S(1)} %collective-permute-done.2.refs_1_, ...), custom_call_target="tpu_custom_call" | custom-call | flops 20000000000 | tf_op jit(solution)/shard_map/spread/pallas_call | solution.py:234
  63.2 0.0 collective-permute-done.11.refs_3_
  63.2 0.0 collective-permute-done.13.refs_5_
  63.2 0.0 collective-permute-done.14.refs_6_
  63.2 0.0 copy-start
  63.2 0.0 copy-start.1
  63.2 2.1 %spread_on.2.begun = f32[16,32,128]{2,1,0:T(8,128)S(1)} custom-call(s32[8,32]{1,0:T(8,128)S(1)} %codes.1.before, bf16[32,8,128,128]{3,2,1,0:T(8,128)(2,1)S(1)} %get-tuple-element.33.tiles, f32[16,32,128]{2,1,0:T(8,128)S(1)} %get-tuple-element.34.begun, bf16[32,32,128]{2,1,0:T(8,128)(2,1)S(1)} %collective-permute-done.8.refs_0_, ...), custom_call_target="tpu_custom_call" | custom-call | flops 1 | tf_op jit(solution)/shard_map/spread_on/pallas_call | solution.py:266
  65.3 0.3 collective-permute-start.15
  65.6 1.3 %collective-permute-done.15.refs_1_ = bf16[32,32,128]{2,1,0:T(8,128)(2,1)S(1)} collective-permute-done((bf16[32,32,128]{2,1,0:T(8,128)(2,1)S(1)}, bf16[32,32,128]{2,1,0:T(8,128)(2,1)S(1)}, u32[]{:S(2)}, u32[]{:S(2)}) %collective-permute-start.15) | collective-permute-done | bytes 262176 | tf_op jit(solution)/shard_map/ppermute | solution.py:363
  66.9 1.1 %spread_on.3 = f32[16,32,128]{2,1,0:T(8,128)S(1)} custom-call(s32[8,32]{1,0:T(8,128)S(1)} %codes.1.before, bf16[32,8,128,128]{3,2,1,0:T(8,128)(2,1)S(1)} %get-tuple-element.33.tiles, f32[16,32,128]{2,1,0:T(8,128)S(1)} %spread_on.2.begun, bf16[32,32,128]{2,1,0:T(8,128)(2,1)S(1)} %collective-permute-done.7.refs_0_, ...), custom_call_target="tpu_custom_call" | custom-call | flops 1 | tf_op jit(solution)/shard_map/spread_on/pallas_call | solution.py:266
  68.1 12.0 %all_to_all.21.parts = f32[8,2,32,128]{3,2,1,0:T(8,128)S(1)} all-to-all(f32[8,2,32,128]{3,2,1,0:T(8,128)S(1)} %bitcast.4), channel_id=1, replica_groups=mesh['blk'=32,'rep'=8] {'rep'}, dimensions={0} | all-to-all | bytes 524288 | tf_op jit(solution)/shard_map/all_to_all | solution.py:27
  80.1 1.0 %result.1 = (f32[256,256]{1,0:T(8,128)}, f32[256,256]{1,0:T(8,128)}, f32[256,256]{1,0:T(8,128)}) custom-call(f32[8,2,32,128]{3,2,1,0:T(8,128)S(1)} %all_to_all.21.parts, f32[32,32,128]{2,1,0:T(8,128)S(1)} %all-to-all-done.2.whole, bf16[256,256]{1,0:T(8,128)(2,1)S(1)} %copy-done, bf16[256,256]{1,0:T(8,128)(2,1)S(1)} %copy-done.1, s32[8,128]{1,0:T(8,128)S(1)} %gate.5.token), custom_call_target="tpu_custom_call" | custom-call | tf_op jit(solution)/shard_map/result/pallas_call | solution.py:180
  (13 shorter events, 0.0 us)
Async XLA Ops:
  22.9 2.3 %collective-permute-start = (bf16[32,32,128]{2,1,0:T(8,128)(2,1)S(1)}, bf16[32,32,128]{2,1,0:T(8,128)(2,1)S(1)}, u32[]{:S(2)}, u32[]{:S(2)}) collective-permute-start(bf16[32,32,128]{2,1,0:T(8,128)(2,1)S(1)} %bitcast.5), channel_id=1, source_target_pairs={{0,8},{8,0},{16,24},{24,16},{32,40},{40,32},{48,56},{56,48},{64,72... | collective-permute-start | bytes 786440 | tf_op jit(solution)/shard_map/ppermute | solution.py:310
  23.1 1.5 %collective-permute-start.1 = (f32[32,128]{1,0:T(8,128)S(1)}, f32[32,128]{1,0:T(8,128)S(1)}, u32[]{:S(2)}, u32[]{:S(2)}) collective-permute-start(f32[32,128]{1,0:T(8,128)S(1)} %get-tuple-element.24), channel_id=1, source_target_pairs={{0,8},{8,0},{16,24},{24,16},{32,40},{40,32},{48,56},{56,48},{64,72... | collective-permute-start | bytes 49160 | tf_op jit(solution)/shard_map/ppermute | solution.py:326
  25.2 10.5 %collective-permute-start.2 = (bf16[32,32,128]{2,1,0:T(8,128)(2,1)S(1)}, bf16[32,32,128]{2,1,0:T(8,128)(2,1)S(1)}, u32[]{:S(2)}, u32[]{:S(2)}) collective-permute-start(bf16[32,32,128]{2,1,0:T(8,128)(2,1)S(1)} %bitcast.6), channel_id=1, source_target_pairs={{0,32},{8,232},{16,48},{24,248},{32,64},{40,8},{48,80},{56,24},{64... | collective-permute-start | bytes 786440 | tf_op jit(solution)/shard_map/ppermute | solution.py:341
  27.2 11.1 %collective-permute-start.5 = (bf16[32,32,128]{2,1,0:T(8,128)(2,1)S(1)}, bf16[32,32,128]{2,1,0:T(8,128)(2,1)S(1)}, u32[]{:S(2)}, u32[]{:S(2)}) collective-permute-start(bf16[32,32,128]{2,1,0:T(8,128)(2,1)S(1)} %collective-permute-done.refs_4_), channel_id=1, source_target_pairs={{0,32},{8,232},{16,48},{24,248},{32,64},{40,8},{48,80},{56,24},{64... | collective-permute-start | bytes 786440 | tf_op jit(solution)/shard_map/ppermute | solution.py:352
  29.1 15.6 %all-to-all-start.1 = ((f32[8,32,128]{2,1,0:T(8,128)}), f32[8,32,128]{2,1,0:T(8,128)S(1)}, u32[]{:S(2)}, u32[]{:S(2)}) async-start(f32[8,32,128]{2,1,0:T(8,128)} %joined.1), calls=%async_computation.1 | async-start | bytes 262144 | tf_op jit(solution)/shard_map/all_to_all | solution.py:27
  35.8 9.6 %collective-permute-start.3 = (bf16[32,32,128]{2,1,0:T(8,128)(2,1)S(1)}, bf16[32,32,128]{2,1,0:T(8,128)(2,1)S(1)}, u32[]{:S(2)}, u32[]{:S(2)}) collective-permute-start(bf16[32,32,128]{2,1,0:T(8,128)(2,1)S(1)} %collective-permute-done.2.refs_1_), channel_id=1, source_target_pairs={{0,32},{8,232},{16,48},{24,248},{32,64},{40,8},{48,80},{56,24},{64... | collective-permute-start | bytes 786440 | tf_op jit(solution)/shard_map/ppermute | solution.py:341
  38.3 9.9 %collective-permute-start.6 = (bf16[32,32,128]{2,1,0:T(8,128)(2,1)S(1)}, bf16[32,32,128]{2,1,0:T(8,128)(2,1)S(1)}, u32[]{:S(2)}, u32[]{:S(2)}) collective-permute-start(bf16[32,32,128]{2,1,0:T(8,128)(2,1)S(1)} %collective-permute-done.5.refs_5_), channel_id=1, source_target_pairs={{0,32},{8,232},{16,48},{24,248},{32,64},{40,8},{48,80},{56,24},{64... | collective-permute-start | bytes 786440 | tf_op jit(solution)/shard_map/ppermute | solution.py:352
  39.2 0.7 copy-start.2
  39.9 0.7 copy-start.3
  40.6 0.7 copy-start.4
  45.3 10.2 %collective-permute-start.4 = (bf16[32,32,128]{2,1,0:T(8,128)(2,1)S(1)}, bf16[32,32,128]{2,1,0:T(8,128)(2,1)S(1)}, u32[]{:S(2)}, u32[]{:S(2)}) collective-permute-start(bf16[32,32,128]{2,1,0:T(8,128)(2,1)S(1)} %collective-permute-done.3.block.refs_2_), channel_id=1, source_target_pairs={{0,32},{8,232},{16,48},{24,248},{32,64},{40,8},{48,80},{56,24},{64... | collective-permute-start | bytes 786440 | tf_op jit(solution)/shard_map/ppermute | solution.py:341
  48.1 7.7 %collective-permute-start.8 = (bf16[32,32,128]{2,1,0:T(8,128)(2,1)S(1)}, bf16[32,32,128]{2,1,0:T(8,128)(2,1)S(1)}, u32[]{:S(2)}, u32[]{:S(2)}) collective-permute-start(bf16[32,32,128]{2,1,0:T(8,128)(2,1)S(1)} %collective-permute-done.6.block.refs_6_), channel_id=1, source_target_pairs={{0,32},{8,232},{16,48},{24,248},{32,64},{40,8},{48,80},{56,24},{64... | collective-permute-start | bytes 786440 | tf_op jit(solution)/shard_map/ppermute | solution.py:352
  48.1 7.9 %collective-permute-start.9 = (bf16[32,32,128]{2,1,0:T(8,128)(2,1)S(1)}, bf16[32,32,128]{2,1,0:T(8,128)(2,1)S(1)}, u32[]{:S(2)}, u32[]{:S(2)}) collective-permute-start(bf16[32,32,128]{2,1,0:T(8,128)(2,1)S(1)} %collective-permute-done.2.refs_1_), channel_id=1, source_target_pairs={{0,8},{8,0},{16,24},{24,16},{32,40},{40,32},{48,56},{56,48},{64,72... | collective-permute-start | bytes 786440 | tf_op jit(solution)/shard_map/ppermute | solution.py:348
  48.8 9.8 %collective-permute-start.10 = (bf16[32,32,128]{2,1,0:T(8,128)(2,1)S(1)}, bf16[32,32,128]{2,1,0:T(8,128)(2,1)S(1)}, u32[]{:S(2)}, u32[]{:S(2)}) collective-permute-start(bf16[32,32,128]{2,1,0:T(8,128)(2,1)S(1)} %collective-permute-done.5.refs_5_), channel_id=1, source_target_pairs={{0,8},{8,0},{16,24},{24,16},{32,40},{40,32},{48,56},{56,48},{64,72... | collective-permute-start | bytes 786440 | tf_op jit(solution)/shard_map/ppermute | solution.py:349
  48.8 14.4 %collective-permute-start.11 = (bf16[32,32,128]{2,1,0:T(8,128)(2,1)S(1)}, bf16[32,32,128]{2,1,0:T(8,128)(2,1)S(1)}, u32[]{:S(2)}, u32[]{:S(2)}) collective-permute-start(bf16[32,32,128]{2,1,0:T(8,128)(2,1)S(1)} %collective-permute-done.3.block.refs_2_), channel_id=1, source_target_pairs={{0,8},{8,0},{16,24},{24,16},{32,40},{40,32},{48,56},{56,48},{64,72... | collective-permute-start | bytes 786440 | tf_op jit(solution)/shard_map/ppermute | solution.py:348
  50.2 17.9 %all-to-all-start.2 = ((f32[32,32,128]{2,1,0:T(8,128)}), f32[32,32,128]{2,1,0:T(8,128)S(1)}, u32[]{:S(2)}, u32[]{:S(2)}) async-start(f32[32,32,128]{2,1,0:T(8,128)} %summed.1), calls=%async_computation.2 | async-start | bytes 1048576 | tf_op jit(solution)/shard_map/all_to_all | solution.py:27
  55.6 7.6 %collective-permute-start.12 = (bf16[32,32,128]{2,1,0:T(8,128)(2,1)S(1)}, bf16[32,32,128]{2,1,0:T(8,128)(2,1)S(1)}, u32[]{:S(2)}, u32[]{:S(2)}) collective-permute-start(bf16[32,32,128]{2,1,0:T(8,128)(2,1)S(1)} %collective-permute-done.6.block.refs_6_), channel_id=1, source_target_pairs={{0,8},{8,0},{16,24},{24,16},{32,40},{40,32},{48,56},{56,48},{64,72... | collective-permute-start | bytes 786440 | tf_op jit(solution)/shard_map/ppermute | solution.py:349
  55.8 9.5 %collective-permute-start.7 = (bf16[32,32,128]{2,1,0:T(8,128)(2,1)S(1)}, bf16[32,32,128]{2,1,0:T(8,128)(2,1)S(1)}, u32[]{:S(2)}, u32[]{:S(2)}) collective-permute-start(bf16[32,32,128]{2,1,0:T(8,128)(2,1)S(1)} %collective-permute-done.4.refs_3_.block), channel_id=1, source_target_pairs={{0,32},{8,232},{16,48},{24,248},{32,64},{40,8},{48,80},{56,24},{64... | collective-permute-start | bytes 786440 | tf_op jit(solution)/shard_map/ppermute | solution.py:341
  56.1 7.1 %collective-permute-start.13 = (bf16[32,32,128]{2,1,0:T(8,128)(2,1)S(1)}, bf16[32,32,128]{2,1,0:T(8,128)(2,1)S(1)}, u32[]{:S(2)}, u32[]{:S(2)}) collective-permute-start(bf16[32,32,128]{2,1,0:T(8,128)(2,1)S(1)} %collective-permute-done.4.refs_3_.block), channel_id=1, source_target_pairs={{0,8},{8,0},{16,24},{24,16},{32,40},{40,32},{48,56},{56,48},{64,72... | collective-permute-start | bytes 786440 | tf_op jit(solution)/shard_map/ppermute | solution.py:348
  58.6 4.6 %collective-permute-start.14 = (bf16[32,32,128]{2,1,0:T(8,128)(2,1)S(1)}, bf16[32,32,128]{2,1,0:T(8,128)(2,1)S(1)}, u32[]{:S(2)}, u32[]{:S(2)}) collective-permute-start(bf16[32,32,128]{2,1,0:T(8,128)(2,1)S(1)} %collective-permute-done.8.refs_0_), channel_id=1, source_target_pairs={{0,8},{8,0},{16,24},{24,16},{32,40},{40,32},{48,56},{56,48},{64,72... | collective-permute-start | bytes 786440 | tf_op jit(solution)/shard_map/ppermute | solution.py:349
  63.2 16.9 %copy-start = (bf16[256,256]{1,0:T(8,128)(2,1)S(1)}, bf16[256,256]{1,0:T(8,128)(2,1)}, u32[]{:S(2)}) copy-start(bf16[256,256]{1,0:T(8,128)(2,1)} %grad.3) | copy-start | bytes 393220
  63.2 16.9 %copy-start.1 = (bf16[256,256]{1,0:T(8,128)(2,1)S(1)}, bf16[256,256]{1,0:T(8,128)(2,1)}, u32[]{:S(2)}) copy-start(bf16[256,256]{1,0:T(8,128)(2,1)} %weight.3) | copy-start | bytes 393220
  65.3 1.6 %collective-permute-start.15 = (bf16[32,32,128]{2,1,0:T(8,128)(2,1)S(1)}, bf16[32,32,128]{2,1,0:T(8,128)(2,1)S(1)}, u32[]{:S(2)}, u32[]{:S(2)}) collective-permute-start(bf16[32,32,128]{2,1,0:T(8,128)(2,1)S(1)} %collective-permute-done.7.refs_0_), channel_id=1, source_target_pairs={{0,8},{8,0},{16,24},{24,16},{32,40},{40,32},{48,56},{56,48},{64,72... | collective-permute-start | bytes 786440 | tf_op jit(solution)/shard_map/ppermute | solution.py:363
